TPU v7x, 512 devices: a whole 4x4x16 slice. The times are simulated.
512 devices in a mesh: grp: 4 (over x), own: 128 (over z, y, core).
Axes of the slice: x: 4, y: 4, z: 16, core: 2. Of those that a mesh axis runs over, the one named last changes fastest.
Arguments:
- tile_row: int32 [4, 128, 24576], P('grp', 'own'), may hold values from 0 to 7
- pixel_col: int32 [4, 128, 24576], P('grp', 'own'), may hold values from 0 to 16383
- weight: bfloat16 [4, 128, 24576], P('grp', 'own'), may hold values from 0.25 to 4
- counts: int32 [4, 128, 128], P('grp', 'own'), may hold values from 1 to 192
- kernel: float32 [9, 9], replicated, may hold values from 0.01 to 0.05
Outputs:
- smoothed: float32 [1024, 16384], P('own', 'grp')
Inputs may be any that keep to these rules, and one draw needn't show every extreme that they name: `counts`: slots past a block's count hold unused values.
All inputs are finite; a program needn't handle non-finite values.
Results may differ from a plain program's by a relative error of at most 0.0012.
Values may be sent and summed in bfloat16 or wider, within the bound.
No kernel may reach another device: no remote copies, remote signals or barrier semaphores. Data moves between devices by JAX's collectives and lax.ppermute only.
A program may use at most 64 MiB of HBM per device.

v0:
```python
import jax
import jax.numpy as jnp
from jax import lax
from jax.sharding import PartitionSpec as P

W = 16384
STRIP = 8


def cut_along(value, dim, length):
    before, after = (value.shape[:dim], value.shape[dim + 1 :])
    return jnp.moveaxis(value.reshape(*before, length, -1, *after), dim, 0)


def sent_and_summed(value, axis, dim):
    blocks = cut_along(value, dim, lax.axis_size(axis))
    arrived = lax.all_to_all(blocks, axis, split_axis=0, concat_axis=0, tiled=True)
    return arrived.astype(jnp.float32).sum(axis=0)


def extended(cells, sides, width):
    for axis, dim in sides:
        count = lax.axis_size(axis)
        ends = count - 1
        head = lax.slice_in_dim(cells, 0, width, axis=dim)
        tail = lax.slice_in_dim(cells, cells.shape[dim] - width, cells.shape[dim], axis=dim)
        cells = jnp.concatenate(
            [
                lax.ppermute(tail, axis, [(i, (i + 1) % count) for i in range(ends)]),
                cells,
                lax.ppermute(head, axis, [((i + 1) % count, i) for i in range(ends)]),
            ],
            axis=dim,
        )
    return cells


def bin_points(packed, masses, col_span):
    row_ids = packed // col_span
    col_ids = packed % col_span
    groups = col_span // 128
    cell_count = STRIP * groups
    cell_index = row_ids * groups + col_ids // 128
    lane_index = col_ids % 128
    slot_count = cell_index.shape[0]
    block_len = max(1, min(slot_count, 2**21 // cell_count))
    block_count = -(-slot_count // block_len)
    cell_iota = lax.broadcasted_iota(jnp.int32, (cell_count, 1), 0)
    lane_iota = lax.broadcasted_iota(jnp.int32, (1, 128), 1)

    def add_block(i, running):
        cells_here = lax.dynamic_slice_in_dim(cell_index, i * block_len, block_len)
        lanes_here = lax.dynamic_slice_in_dim(lane_index, i * block_len, block_len)
        masses_here = lax.dynamic_slice_in_dim(masses, i * block_len, block_len)
        onehot_cells = (cell_iota == cells_here[None, :]).astype(jnp.bfloat16)
        onehot_lanes = jnp.where(
            lane_iota == lanes_here[:, None], masses_here[:, None], jnp.zeros((), jnp.bfloat16)
        )
        return running + jnp.dot(onehot_cells, onehot_lanes, preferred_element_type=jnp.float32)

    running = lax.fori_loop(0, block_count, add_block, jnp.zeros((cell_count, 128), jnp.float32))
    return running.reshape(STRIP, col_span)


def per_device(tile_row, pixel_col, weight, counts, kernel):
    owners = lax.axis_size("own")
    group_count = lax.axis_size("grp")
    cap_len = tile_row.shape[2] // owners
    tile_rows = tile_row.reshape(owners, cap_len)
    columns = pixel_col.reshape(owners, cap_len)
    masses = weight.reshape(owners, cap_len)
    live = lax.broadcasted_iota(jnp.int32, (owners, cap_len), 1) < counts.reshape(owners, 1)
    masses = jnp.where(live, masses, jnp.zeros((), jnp.bfloat16))
    quarter_cols = W // group_count
    packed_index = tile_rows * W + columns
    got_index, got_masses = (
        lax.all_to_all(packed_index, "own", split_axis=0, concat_axis=0, tiled=True),
        lax.all_to_all(masses, "own", split_axis=0, concat_axis=0, tiled=True),
    )
    heat = bin_points(got_index.reshape(-1), got_masses.reshape(-1), W)
    quarter = sent_and_summed(heat.astype(jnp.bfloat16), "grp", 1)
    framed = extended(quarter.astype(jnp.bfloat16), (("own", 0), ("grp", 1)), 4).astype(
        quarter.dtype
    )
    smoothed = jnp.zeros((STRIP, quarter_cols), jnp.float32)
    for a in range(9):
        for b in range(9):
            smoothed = smoothed + kernel[a, b] * framed[a : a + STRIP, b : b + quarter_cols]
    return smoothed


def solution(mesh):
    placed = (
        P("grp", "own", None),
        P("grp", "own", None),
        P("grp", "own", None),
        P("grp", "own", None),
        P(),
    )
    return jax.shard_map(
        per_device, mesh=mesh, in_specs=placed, out_specs=P("own", "grp"), check_vma=False
    )
```

profile of v0, /device:TPU:25, one launch (start us, length us, event | category | flops | bytes accessed | tf_op | source)
XLA Modules:
  0.0 170.2 jit_solution(7567215421963976678)
XLA Ops:
  0.0 1.2 reduce.3
  1.2 0.1 reshape.95
  1.3 0.7 fusion.93
  2.1 0.8 copy.9
  2.8 19.7 %all-to-all-start.1 = ((bf16[128,1,192]{2,1,0:T(2,128)(2,1)}), bf16[128,1,192]{2,1,0:T(2,128)(2,1)S(1)}, u32[]{:S(2)}, u32[]{:S(2)}) async-start(bf16[128,1,192]{2,1,0:T(2,128)(2,1)} %copy.9), calls=%async_computation.1 | async-start | bytes 262144 | tf_op jit(solution)/shard_map/all_to_all | solution.py:78
  22.6 0.3 add_reduce_fusion
  22.9 0.9 add.388
  23.8 15.0 %all-to-all-done.1 = bf16[128,1,192]{2,1,0:T(2,128)(2,1)S(1)} async-done(((bf16[128,1,192]{2,1,0:T(2,128)(2,1)}), bf16[128,1,192]{2,1,0:T(2,128)(2,1)S(1)}, u32[]{:S(2)}, u32[]{:S(2)}) %all-to-all-start.1) | async-done | bytes 49184 | tf_op jit(solution)/shard_map/all_to_all | solution.py:78
  38.7 7.0 %all-to-all-start = ((s32[128,1,192]{2,1,0:T(1,128)}), s32[128,1,192]{2,1,0:T(1,128)S(1)}, u32[]{:S(2)}, u32[]{:S(2)}) async-start(s32[128,1,192]{2,1,0:T(1,128)} %add.388), calls=%async_computation | async-start | bytes 262144 | tf_op jit(solution)/shard_map/all_to_all | solution.py:77
  45.8 0.7 fusion.100
  46.5 0.4 reduce.4
  46.9 0.1 reshape.96
  47.0 14.9 %all-to-all-done = s32[128,1,192]{2,1,0:T(1,128)S(1)} async-done(((s32[128,1,192]{2,1,0:T(1,128)}), s32[128,1,192]{2,1,0:T(1,128)S(1)}, u32[]{:S(2)}, u32[]{:S(2)}) %all-to-all-start) | async-done | bytes 98336 | tf_op jit(solution)/shard_map/all_to_all | solution.py:77
  61.9 0.3 reduce.2
  62.3 0.1 reshape.94
  62.4 0.2 add_select_fusion
  62.6 23.0 %while.14 = (s32[]{:T(128)}, f32[1024,128]{1,0:T(8,128)S(1)}, s32[24576]{0:T(1024)S(1)}, s32[24576]{0:T(1024)S(1)}, bf16[24576]{0:T(1024)(128)(2,1)S(1)}, /*index=5*/s32[]{:T(128)}, s32[]{:T(128)}, s32[]{:T(128)}, s32[]{:T(128)}) while((s32[]{:T(128)}, f32[1024,128]{1,0:T(8,128)S(1)}, s32[24576]{0:T(1024)S(1)}, ...), condition=%wide.region_1.2_spmd.clone, body=%wide.region_0.1_spmd.clone.sunk | while | flops 539754496 | bytes 1110177 | solution.py:61
  62.6 1.8 %fusion.108 = f32[1024,128]{1,0:T(8,128)S(1)} fusion(s32[2048]{0:T(1024)S(1)} %dynamic_slice.27, f32[1024,128]{1,0:T(8,128)S(1)} %get-tuple-element.290, s32[2048]{0:T(1024)S(1)} %dynamic_slice.28, bf16[2048]{0:T(1024)(128)(2,1)S(1)} %dynamic_slice.29, pred[]{:T(512)S(6)} %compare.9), kind=kOutput, calls=%fused_computation.5.clone.1 | convolution fusion | flops 539754496 | bytes 1069057 | tf_op jit(solution)/shard_map/while/body/eval_jaxpr/dot_general | solution.py:59
  64.5 1.8 %fusion.108 = f32[1024,128]{1,0:T(8,128)S(1)} fusion(s32[2048]{0:T(1024)S(1)} %dynamic_slice.27, f32[1024,128]{1,0:T(8,128)S(1)} %get-tuple-element.290, s32[2048]{0:T(1024)S(1)} %dynamic_slice.28, bf16[2048]{0:T(1024)(128)(2,1)S(1)} %dynamic_slice.29, pred[]{:T(512)S(6)} %compare.9), kind=kOutput, calls=%fused_computation.5.clone.1 | convolution fusion | flops 539754496 | bytes 1069057 | tf_op jit(solution)/shard_map/while/body/eval_jaxpr/dot_general | solution.py:59
  66.5 1.8 %fusion.108 = f32[1024,128]{1,0:T(8,128)S(1)} fusion(s32[2048]{0:T(1024)S(1)} %dynamic_slice.27, f32[1024,128]{1,0:T(8,128)S(1)} %get-tuple-element.290, s32[2048]{0:T(1024)S(1)} %dynamic_slice.28, bf16[2048]{0:T(1024)(128)(2,1)S(1)} %dynamic_slice.29, pred[]{:T(512)S(6)} %compare.9), kind=kOutput, calls=%fused_computation.5.clone.1 | convolution fusion | flops 539754496 | bytes 1069057 | tf_op jit(solution)/shard_map/while/body/eval_jaxpr/dot_general | solution.py:59
  68.4 1.8 %fusion.108 = f32[1024,128]{1,0:T(8,128)S(1)} fusion(s32[2048]{0:T(1024)S(1)} %dynamic_slice.27, f32[1024,128]{1,0:T(8,128)S(1)} %get-tuple-element.290, s32[2048]{0:T(1024)S(1)} %dynamic_slice.28, bf16[2048]{0:T(1024)(128)(2,1)S(1)} %dynamic_slice.29, pred[]{:T(512)S(6)} %compare.9), kind=kOutput, calls=%fused_computation.5.clone.1 | convolution fusion | flops 539754496 | bytes 1069057 | tf_op jit(solution)/shard_map/while/body/eval_jaxpr/dot_general | solution.py:59
  70.3 1.8 %fusion.108 = f32[1024,128]{1,0:T(8,128)S(1)} fusion(s32[2048]{0:T(1024)S(1)} %dynamic_slice.27, f32[1024,128]{1,0:T(8,128)S(1)} %get-tuple-element.290, s32[2048]{0:T(1024)S(1)} %dynamic_slice.28, bf16[2048]{0:T(1024)(128)(2,1)S(1)} %dynamic_slice.29, pred[]{:T(512)S(6)} %compare.9), kind=kOutput, calls=%fused_computation.5.clone.1 | convolution fusion | flops 539754496 | bytes 1069057 | tf_op jit(solution)/shard_map/while/body/eval_jaxpr/dot_general | solution.py:59
  72.2 1.8 %fusion.108 = f32[1024,128]{1,0:T(8,128)S(1)} fusion(s32[2048]{0:T(1024)S(1)} %dynamic_slice.27, f32[1024,128]{1,0:T(8,128)S(1)} %get-tuple-element.290, s32[2048]{0:T(1024)S(1)} %dynamic_slice.28, bf16[2048]{0:T(1024)(128)(2,1)S(1)} %dynamic_slice.29, pred[]{:T(512)S(6)} %compare.9), kind=kOutput, calls=%fused_computation.5.clone.1 | convolution fusion | flops 539754496 | bytes 1069057 | tf_op jit(solution)/shard_map/while/body/eval_jaxpr/dot_general | solution.py:59
  74.1 1.8 %fusion.108 = f32[1024,128]{1,0:T(8,128)S(1)} fusion(s32[2048]{0:T(1024)S(1)} %dynamic_slice.27, f32[1024,128]{1,0:T(8,128)S(1)} %get-tuple-element.290, s32[2048]{0:T(1024)S(1)} %dynamic_slice.28, bf16[2048]{0:T(1024)(128)(2,1)S(1)} %dynamic_slice.29, pred[]{:T(512)S(6)} %compare.9), kind=kOutput, calls=%fused_computation.5.clone.1 | convolution fusion | flops 539754496 | bytes 1069057 | tf_op jit(solution)/shard_map/while/body/eval_jaxpr/dot_general | solution.py:59
  76.0 1.8 %fusion.108 = f32[1024,128]{1,0:T(8,128)S(1)} fusion(s32[2048]{0:T(1024)S(1)} %dynamic_slice.27, f32[1024,128]{1,0:T(8,128)S(1)} %get-tuple-element.290, s32[2048]{0:T(1024)S(1)} %dynamic_slice.28, bf16[2048]{0:T(1024)(128)(2,1)S(1)} %dynamic_slice.29, pred[]{:T(512)S(6)} %compare.9), kind=kOutput, calls=%fused_computation.5.clone.1 | convolution fusion | flops 539754496 | bytes 1069057 | tf_op jit(solution)/shard_map/while/body/eval_jaxpr/dot_general | solution.py:59
  77.9 1.8 %fusion.108 = f32[1024,128]{1,0:T(8,128)S(1)} fusion(s32[2048]{0:T(1024)S(1)} %dynamic_slice.27, f32[1024,128]{1,0:T(8,128)S(1)} %get-tuple-element.290, s32[2048]{0:T(1024)S(1)} %dynamic_slice.28, bf16[2048]{0:T(1024)(128)(2,1)S(1)} %dynamic_slice.29, pred[]{:T(512)S(6)} %compare.9), kind=kOutput, calls=%fused_computation.5.clone.1 | convolution fusion | flops 539754496 | bytes 1069057 | tf_op jit(solution)/shard_map/while/body/eval_jaxpr/dot_general | solution.py:59
  79.9 1.8 %fusion.108 = f32[1024,128]{1,0:T(8,128)S(1)} fusion(s32[2048]{0:T(1024)S(1)} %dynamic_slice.27, f32[1024,128]{1,0:T(8,128)S(1)} %get-tuple-element.290, s32[2048]{0:T(1024)S(1)} %dynamic_slice.28, bf16[2048]{0:T(1024)(128)(2,1)S(1)} %dynamic_slice.29, pred[]{:T(512)S(6)} %compare.9), kind=kOutput, calls=%fused_computation.5.clone.1 | convolution fusion | flops 539754496 | bytes 1069057 | tf_op jit(solution)/shard_map/while/body/eval_jaxpr/dot_general | solution.py:59
  81.8 1.8 %fusion.108 = f32[1024,128]{1,0:T(8,128)S(1)} fusion(s32[2048]{0:T(1024)S(1)} %dynamic_slice.27, f32[1024,128]{1,0:T(8,128)S(1)} %get-tuple-element.290, s32[2048]{0:T(1024)S(1)} %dynamic_slice.28, bf16[2048]{0:T(1024)(128)(2,1)S(1)} %dynamic_slice.29, pred[]{:T(512)S(6)} %compare.9), kind=kOutput, calls=%fused_computation.5.clone.1 | convolution fusion | flops 539754496 | bytes 1069057 | tf_op jit(solution)/shard_map/while/body/eval_jaxpr/dot_general | solution.py:59
  83.7 1.8 %fusion.108 = f32[1024,128]{1,0:T(8,128)S(1)} fusion(s32[2048]{0:T(1024)S(1)} %dynamic_slice.27, f32[1024,128]{1,0:T(8,128)S(1)} %get-tuple-element.290, s32[2048]{0:T(1024)S(1)} %dynamic_slice.28, bf16[2048]{0:T(1024)(128)(2,1)S(1)} %dynamic_slice.29, pred[]{:T(512)S(6)} %compare.9), kind=kOutput, calls=%fused_computation.5.clone.1 | convolution fusion | flops 539754496 | bytes 1069057 | tf_op jit(solution)/shard_map/while/body/eval_jaxpr/dot_general | solution.py:59
  85.6 0.1 convert_element_type.16
  85.6 0.8 copy.10
  86.5 4.0 %all-to-all-start.2 = ((bf16[4,8,4096]{2,1,0:T(8,128)(2,1)}), bf16[4,8,4096]{2,1,0:T(8,128)(2,1)S(1)}, u32[]{:S(2)}, u32[]{:S(2)}) async-start(bf16[4,8,4096]{2,1,0:T(8,128)(2,1)} %copy.10), calls=%async_computation.2 | async-start | bytes 524288 | tf_op jit(solution)/shard_map/all_to_all | solution.py:17
  90.5 0.7 fusion.102
  91.2 0.7 fusion.101
  91.9 4.4 %all-to-all-done.2 = bf16[4,8,4096]{2,1,0:T(8,128)(2,1)S(1)} async-done(((bf16[4,8,4096]{2,1,0:T(8,128)(2,1)}), bf16[4,8,4096]{2,1,0:T(8,128)(2,1)S(1)}, u32[]{:S(2)}, u32[]{:S(2)}) %all-to-all-start.2) | async-done | bytes 262176 | tf_op jit(solution)/shard_map/all_to_all | solution.py:17
  96.5 5.6 %collective-permute-start = (bf16[4,4096]{1,0:T(4,128)(2,1)S(1)}, bf16[4,4096]{1,0:T(4,128)(2,1)S(1)}, u32[]{:S(2)}, u32[]{:S(2)}) collective-permute-start(bf16[4,4096]{1,0:T(4,128)(2,1)S(1)} %get-tuple-element.166), channel_id=1, source_target_pairs={{0,1},{1,2},{2,3},{3,4},{4,5},{5,6},{6,7},{7,8},{8,9},{9,10},{10,1... | collective-permute-start | bytes 98312 | tf_op jit(solution)/shard_map/ppermute | solution.py:29
  102.1 1.9 %collective-permute-start.1 = (bf16[4,4096]{1,0:T(4,128)(2,1)S(1)}, bf16[4,4096]{1,0:T(4,128)(2,1)S(1)}, u32[]{:S(2)}, u32[]{:S(2)}) collective-permute-start(bf16[4,4096]{1,0:T(4,128)(2,1)S(1)} %get-tuple-element.167), channel_id=1, source_target_pairs={{1,0},{2,1},{3,2},{4,3},{5,4},{6,5},{7,6},{8,7},{9,8},{10,9},{11,1... | collective-permute-start | bytes 98312 | tf_op jit(solution)/shard_map/ppermute | solution.py:31
  104.0 0.7 fusion.103
  104.8 0.0 collective-permute-done
  104.8 4.7 %collective-permute-done.1 = bf16[4,4096]{1,0:T(4,128)(2,1)S(1)} collective-permute-done((bf16[4,4096]{1,0:T(4,128)(2,1)S(1)}, bf16[4,4096]{1,0:T(4,128)(2,1)S(1)}, u32[]{:S(2)}, u32[]{:S(2)}) %collective-permute-start.1) | collective-permute-done | bytes 32800 | tf_op jit(solution)/shard_map/ppermute | solution.py:31
  109.4 0.1 pad_maximum_fusion
  109.5 0.1 fusion.98
  109.6 2.2 %collective-permute-start.2 = (bf16[16,4]{1,0:T(8,128)(2,1)S(1)}, bf16[16,4]{1,0:T(8,128)(2,1)S(1)}, u32[]{:S(2)}, u32[]{:S(2)}) collective-permute-start(bf16[16,4]{1,0:T(8,128)(2,1)S(1)} %get-tuple-element.163), channel_id=1, source_target_pairs={{0,128},{128,256},{256,384},{1,129},{129,257},{257,385},{2,130},{1... | collective-permute-start | bytes 392 | tf_op jit(solution)/shard_map/ppermute | solution.py:29
  111.8 1.5 collective-permute-start.3
  113.3 0.7 fusion.104
  113.9 2.2 %collective-permute-done.3 = bf16[16,4]{1,0:T(8,128)(2,1)S(1)} collective-permute-done((bf16[16,4]{1,0:T(8,128)(2,1)S(1)}, bf16[16,4]{1,0:T(8,128)(2,1)S(1)}, u32[]{:S(2)}, u32[]{:S(2)}) %collective-permute-start.3) | collective-permute-done | bytes 160 | tf_op jit(solution)/shard_map/ppermute | solution.py:31
  116.1 0.2 concatenate.7
  116.3 53.9 %fusion.13 = f32[8,4096]{1,0:T(8,128)} fusion(f32[16,4104]{1,0:T(8,128)S(1)} %convert_element_type.17, f32[]{:T(128)} %bitcast.82, f32[]{:T(128)} %bitcast.81, f32[]{:T(128)} %bitcast.80, f32[]{:T(128)} %bitcast.79, f32[]{:T(128)} %bitcast.78, f32[]{:T(128)} %bitcast.77, f32[]{:T(128)} %bitcast.76, f32[]{:T(128)} %bitcast.75, f32[]{:T(128)} %bitcast.74, ...), kind=kLoop, calls=%fused_computation.23 | loop fusion | flops 5275648 | bytes 10748228 | tf_op jit(solution)/shard_map/add | solution.py:88
  (48 shorter events, 0.5 us)
Async XLA Ops:
  0.0 22.6 %copy-start.2 = (s32[1,1,24576]{2,1,0:T(1,128)S(1)}, s32[1,1,24576]{2,1,0:T(1,128)}, u32[]{:S(2)}) copy-start(s32[1,1,24576]{2,1,0:T(1,128)} %param.7) | copy-start | bytes 294916
  0.0 22.6 %copy-start.1 = (s32[1,1,24576]{2,1,0:T(1,128)S(1)}, s32[1,1,24576]{2,1,0:T(1,128)}, u32[]{:S(2)}) copy-start(s32[1,1,24576]{2,1,0:T(1,128)} %param.8) | copy-start | bytes 294916
  2.8 43.0 %copy-start = (f32[9,9]{1,0:T(8,128)S(1)}, f32[9,9]{1,0:T(8,128)}, u32[]{:S(2)}) copy-start(f32[9,9]{1,0:T(8,128)} %param.11) | copy-start | bytes 976
  2.8 35.9 %all-to-all-start.1 = ((bf16[128,1,192]{2,1,0:T(2,128)(2,1)}), bf16[128,1,192]{2,1,0:T(2,128)(2,1)S(1)}, u32[]{:S(2)}, u32[]{:S(2)}) async-start(bf16[128,1,192]{2,1,0:T(2,128)(2,1)} %copy.9), calls=%async_computation.1 | async-start | bytes 262144 | tf_op jit(solution)/shard_map/all_to_all | solution.py:78
  38.7 23.2 %all-to-all-start = ((s32[128,1,192]{2,1,0:T(1,128)}), s32[128,1,192]{2,1,0:T(1,128)S(1)}, u32[]{:S(2)}, u32[]{:S(2)}) async-start(s32[128,1,192]{2,1,0:T(1,128)} %add.388), calls=%async_computation | async-start | bytes 262144 | tf_op jit(solution)/shard_map/all_to_all | solution.py:77
  86.5 9.9 %all-to-all-start.2 = ((bf16[4,8,4096]{2,1,0:T(8,128)(2,1)}), bf16[4,8,4096]{2,1,0:T(8,128)(2,1)S(1)}, u32[]{:S(2)}, u32[]{:S(2)}) async-start(bf16[4,8,4096]{2,1,0:T(8,128)(2,1)} %copy.10), calls=%async_computation.2 | async-start | bytes 524288 | tf_op jit(solution)/shard_map/all_to_all | solution.py:17
  96.5 8.3 %collective-permute-start = (bf16[4,4096]{1,0:T(4,128)(2,1)S(1)}, bf16[4,4096]{1,0:T(4,128)(2,1)S(1)}, u32[]{:S(2)}, u32[]{:S(2)}) collective-permute-start(bf16[4,4096]{1,0:T(4,128)(2,1)S(1)} %get-tuple-element.166), channel_id=1, source_target_pairs={{0,1},{1,2},{2,3},{3,4},{4,5},{5,6},{6,7},{7,8},{8,9},{9,10},{10,1... | collective-permute-start | bytes 98312 | tf_op jit(solution)/shard_map/ppermute | solution.py:29
  102.1 7.3 %collective-permute-start.1 = (bf16[4,4096]{1,0:T(4,128)(2,1)S(1)}, bf16[4,4096]{1,0:T(4,128)(2,1)S(1)}, u32[]{:S(2)}, u32[]{:S(2)}) collective-permute-start(bf16[4,4096]{1,0:T(4,128)(2,1)S(1)} %get-tuple-element.167), channel_id=1, source_target_pairs={{1,0},{2,1},{3,2},{4,3},{5,4},{6,5},{7,6},{8,7},{9,8},{10,9},{11,1... | collective-permute-start | bytes 98312 | tf_op jit(solution)/shard_map/ppermute | solution.py:31
  109.6 4.3 %collective-permute-start.2 = (bf16[16,4]{1,0:T(8,128)(2,1)S(1)}, bf16[16,4]{1,0:T(8,128)(2,1)S(1)}, u32[]{:S(2)}, u32[]{:S(2)}) collective-permute-start(bf16[16,4]{1,0:T(8,128)(2,1)S(1)} %get-tuple-element.163), channel_id=1, source_target_pairs={{0,128},{128,256},{256,384},{1,129},{129,257},{257,385},{2,130},{1... | collective-permute-start | bytes 392 | tf_op jit(solution)/shard_map/ppermute | solution.py:29
  111.8 4.4 %collective-permute-start.3 = (bf16[16,4]{1,0:T(8,128)(2,1)S(1)}, bf16[16,4]{1,0:T(8,128)(2,1)S(1)}, u32[]{:S(2)}, u32[]{:S(2)}) collective-permute-start(bf16[16,4]{1,0:T(8,128)(2,1)S(1)} %get-tuple-element.162), channel_id=1, source_target_pairs={{128,0},{256,128},{384,256},{129,1},{257,129},{385,257},{130,2},{2... | collective-permute-start | bytes 392 | tf_op jit(solution)/shard_map/ppermute | solution.py:31
where the time goes:
time: 171 us; the launch traced here: 170 us
  other arithmetic  57.1 us (33%)
  starting transfers between devices  42 us (25%)
  waiting for transfers between devices  41.2 us (24%)
  matrix products  22 us (13%)
  local copies, waits for them, and re-layouts  7.06 us (4%)
    add x1, other arithmetic, per_device(): smoothed = smoothed + kernel[a, b] * framed[a:a + STRIP, b:b + quarter_cols]  53.9 us
    dot_general x12, matrix products, add_block(): jnp.dot(onehot_cells, onehot_lanes, preferred_element_type=jnp.float32)  22 us
    all_to_all x1, starting transfers between devices, per_device(): lax.all_to_all(masses, 'own', split_axis=0, concat_axis=0, tiled=True)  19.7 us
    all_to_all x1, waiting for transfers between devices, per_device(): lax.all_to_all(masses, 'own', split_axis=0, concat_axis=0, tiled=True)  15 us
    all_to_all x1, waiting for transfers between devices, per_device(): lax.all_to_all(packed_index, 'own', split_axis=0, concat_axis=0, tiled=True)  14.9 us
    ppermute x2, starting transfers between devices, extended(): lax.ppermute(tail, axis, [(i, (i + 1) % count) for i in range(ends)])  7.81 us
    all_to_all x1, starting transfers between devices, per_device(): lax.all_to_all(packed_index, 'own', split_axis=0, concat_axis=0, tiled=True)  7.02 us
    ppermute x2, waiting for transfers between devices, extended(): lax.ppermute(head, axis, [((i + 1) % count, i) for i in range(ends)])  6.88 us
  transfers between devices with their start and end apart: 7, of which 5 were waited for; matrix products, arithmetic and copies ran while one was open for 3% of the time, Pallas kernels for 0%

commit v1 on v0

v1 whole, which is shorter than its diff:
```python
import jax
import jax.numpy as jnp
from jax import lax
from jax.experimental import pallas as pl
from jax.experimental.pallas import tpu as pltpu
from jax.sharding import PartitionSpec as P

W = 16384
STRIP = 8
CAP = 192
LANES = 128
HALO = 4
SPAN = 256
CELLS = STRIP * W // SPAN
ROWS = 8


def vmem_spec():
    return pl.BlockSpec(memory_space=pltpu.VMEM)


def smem_spec():
    return pl.BlockSpec(memory_space=pltpu.SMEM)


def pack_kernel(row_ref, col_ref, weight_ref, count_ref, out_ref, wide_ref):
    points = row_ref.shape[0]
    pairs = points // 3
    for i in range(points):
        wide_ref[pl.ds(i, 1), :] = weight_ref[i].astype(jnp.float32)
    lane = lax.broadcasted_iota(jnp.int32, (pairs, LANES), 1)
    block = lax.broadcasted_iota(jnp.int32, (pairs, LANES), 0)
    counts = jnp.broadcast_to(count_ref[...], (pairs, LANES))
    even = jnp.sum(jnp.where(lane == 2 * block, counts, 0), axis=1, keepdims=True)
    odd = jnp.sum(jnp.where(lane == 2 * block + 1, counts, 0), axis=1, keepdims=True)
    low = lane < 64
    lives = (
        lane < even,
        jnp.where(low, lane + 128, lane - 64) < jnp.where(low, even, odd),
        lane + 64 < odd,
    )
    ids, masses = [], []
    for k in range(3):
        tile_row = row_ref[pl.ds(k, pairs, stride=3), :]
        column = col_ref[pl.ds(k, pairs, stride=3), :]
        index = ((column // SPAN) * STRIP + tile_row) * SPAN + column % SPAN
        ids.append(index.astype(jnp.float32))
        masses.append(jnp.where(lives[k], wide_ref[pl.ds(k, pairs, stride=3), :], 0.0))
    half = LANES // 2
    out_ref[pl.ds(0, pairs, stride=6), :] = ids[0]
    out_ref[pl.ds(1, pairs, stride=6), :] = jnp.where(low, ids[1], pltpu.roll(masses[1], half, 1))
    out_ref[pl.ds(2, pairs, stride=6), :] = masses[0]
    out_ref[pl.ds(3, pairs, stride=6), :] = ids[2]
    out_ref[pl.ds(4, pairs, stride=6), :] = jnp.where(low, pltpu.roll(ids[1], half, 1), masses[1])
    out_ref[pl.ds(5, pairs, stride=6), :] = masses[2]


def bin_kernel(points_ref, out_ref, first_ref, second_ref, mass_ref, acc_ref):
    sources = points_ref.shape[0] // 3
    half = sources // 2
    low = lax.broadcasted_iota(jnp.int32, (half, LANES), 1) < 64
    upper = points_ref[pl.ds(1, half, stride=3), :]
    lower = points_ref[pl.ds(1 + 3 * half, half, stride=3), :]
    mixed_ids = jnp.where(low, upper, pltpu.roll(lower, 64, 1))
    mixed_masses = jnp.where(low, pltpu.roll(upper, 64, 1), lower)
    for ids, masses, at in (
        (points_ref[pl.ds(0, sources, stride=3), :], points_ref[pl.ds(2, sources, stride=3), :], 0),
        (mixed_ids, mixed_masses, sources),
    ):
        ids = ids.astype(jnp.int32)
        here = pl.ds(at, ids.shape[0])
        first_ref[here, :] = (ids // SPAN).astype(jnp.float32) - 256.0
        second_ref[here, :] = (ids % SPAN).astype(jnp.float32)
        mass_ref[here, :] = masses
    first_iota = (
        lax.broadcasted_iota(jnp.int32, (CELLS, LANES), 0).astype(jnp.float32) - 256.0
    ).astype(jnp.bfloat16)
    second_iota = lax.broadcasted_iota(jnp.int32, (SPAN, LANES), 0).astype(jnp.float32).astype(jnp.bfloat16)
    one = jnp.ones((), jnp.bfloat16)
    zero = jnp.zeros((), jnp.bfloat16)
    acc_ref[...] = jnp.zeros_like(acc_ref)

    def step(i, carry):
        here = pl.ds(pl.multiple_of(i * ROWS, ROWS), ROWS)
        first = first_ref[here, :].astype(jnp.bfloat16)
        second = second_ref[here, :].astype(jnp.bfloat16)
        mass = mass_ref[here, :].astype(jnp.bfloat16)
        left, right = [], []
        for r in range(ROWS):
            left.append(jnp.where(first_iota == first[r : r + 1], one, zero))
            right.append(jnp.where(second_iota == second[r : r + 1], mass[r : r + 1], zero))
        acc_ref[...] += lax.dot_general(
            jnp.concatenate(left, axis=1),
            jnp.concatenate(right, axis=1),
            (((1,), (1,)), ((), ())),
            preferred_element_type=jnp.float32,
        )
        return carry

    lax.fori_loop(0, first_ref.shape[0] // ROWS, step, 0)
    quarters, _, width = out_ref.shape
    span = width - LANES
    groups = span // SPAN
    low8 = lax.broadcasted_iota(jnp.int32, (STRIP, LANES), 1) < 64
    blank = jnp.zeros((STRIP, LANES), jnp.float32)
    for q in range(quarters):
        for c in range(groups):
            at = (q * groups + c) * STRIP
            out_ref[q, :, c * SPAN : (c + 1) * SPAN] = acc_ref[at : at + STRIP, :].astype(jnp.bfloat16)
        at = q * groups * STRIP
        before = acc_ref[at - STRIP : at, LANES:] if q else blank
        at += groups * STRIP
        after = acc_ref[at : at + STRIP, :LANES] if q < quarters - 1 else blank
        out_ref[q, :, span:] = jnp.where(low8, after, before).astype(jnp.bfloat16)


def sum_kernel(parity_ref, parts_ref, sum_ref, near_ref, far_ref):
    total = parts_ref[0].astype(jnp.float32)
    for g in range(1, parts_ref.shape[0]):
        total = total + parts_ref[g].astype(jnp.float32)
    sum_ref[...] = total
    top = total[:HALO]
    bottom = total[HALO:]
    is_odd = parity_ref[0] == 1
    near_ref[...] = jnp.where(is_odd, top, bottom).astype(jnp.bfloat16)
    far_ref[...] = jnp.where(is_odd, bottom, top).astype(jnp.bfloat16)


def smooth_kernel(parity_ref, kernel_ref, own_ref, near_ref, far_ref, out_ref):
    own = own_ref[...]
    near = near_ref[...].astype(jnp.float32)
    far = far_ref[...].astype(jnp.float32)
    is_odd = parity_ref[0] == 1
    above = jnp.where(is_odd, near, far)
    below = jnp.where(is_odd, far, near)
    frame = jnp.concatenate([above, own, below], axis=0)
    width = frame.shape[1]
    wins = [frame[a : a + STRIP] for a in range(9)]
    total = None
    for b in range(9):
        part = kernel_ref[0, b] * wins[0]
        for a in range(1, 9):
            part = part + kernel_ref[a, b] * wins[a]
        shift = (HALO - b) % width
        part = pltpu.roll(part, shift, 1) if shift else part
        total = part if total is None else total + part
    out_ref[...] = total[:, : out_ref.shape[1]]


def per_device(tile_row, pixel_col, weight, counts, kernel):
    owners = lax.axis_size("own")
    groups = lax.axis_size("grp")
    points = tile_row.shape[2] // LANES
    quarter = W // groups
    width = quarter + LANES
    packed = pl.pallas_call(
        pack_kernel,
        out_shape=jax.ShapeDtypeStruct((3 * owners, LANES), jnp.float32),
        in_specs=[vmem_spec()] * 4,
        out_specs=vmem_spec(),
        scratch_shapes=[pltpu.VMEM((points, LANES), jnp.float32)],
        name="pack",
    )(
        tile_row.reshape(points, LANES),
        pixel_col.reshape(points, LANES),
        weight.reshape(points, 1, LANES),
        counts.reshape(1, owners),
    )
    arrived = lax.all_to_all(
        packed.reshape(3 * owners, 1, LANES), "own", split_axis=0, concat_axis=0, tiled=True
    ).reshape(3 * owners, LANES)
    parts = pl.pallas_call(
        bin_kernel,
        out_shape=jax.ShapeDtypeStruct((groups, STRIP, width), jnp.bfloat16),
        in_specs=[vmem_spec()],
        out_specs=vmem_spec(),
        scratch_shapes=[pltpu.VMEM((points, LANES), jnp.float32)] * 3
        + [pltpu.VMEM((CELLS, SPAN), jnp.float32)],
        compiler_params=pltpu.CompilerParams(vmem_limit_bytes=48 * 2**20),
        name="bin",
    )(arrived)
    parts = lax.all_to_all(parts, "grp", split_axis=0, concat_axis=0, tiled=True)
    me = lax.axis_index("own")
    parity = (me % 2).reshape(1).astype(jnp.int32)
    own, near, far = pl.pallas_call(
        sum_kernel,
        out_shape=(
            jax.ShapeDtypeStruct((STRIP, width), jnp.float32),
            jax.ShapeDtypeStruct((HALO, width), jnp.bfloat16),
            jax.ShapeDtypeStruct((HALO, width), jnp.bfloat16),
        ),
        in_specs=[smem_spec(), vmem_spec()],
        out_specs=(vmem_spec(),) * 3,
        name="total",
    )(parity, parts)
    on_chip = [(i, i ^ 1) for i in range(owners)]
    across = [(i, i + 1) for i in range(1, owners - 1, 2)]
    across = across + [(j, i) for i, j in across]
    near = lax.ppermute(near, "own", on_chip)
    far = lax.ppermute(far, "own", across)
    return pl.pallas_call(
        smooth_kernel,
        out_shape=jax.ShapeDtypeStruct((STRIP, quarter), jnp.float32),
        in_specs=[smem_spec(), smem_spec()] + [vmem_spec()] * 3,
        out_specs=vmem_spec(),
        name="smooth",
    )(parity, kernel, own, near, far)


def solution(mesh):
    placed = (
        P("grp", "own", None),
        P("grp", "own", None),
        P("grp", "own", None),
        P("grp", "own", None),
        P(),
    )
    return jax.shard_map(
        per_device, mesh=mesh, in_specs=placed, out_specs=P("own", "grp"), check_vma=False
    )
```

time: 171 us -> 81 us (0.47)
  other arithmetic: 57.1 us -> 0 us
  blocking collectives: 0 us -> 38.6 us
  waiting for transfers between devices: 41.2 us -> 9.84 us
  starting transfers between devices: 42 us -> 11.3 us
  matrix products: 22 us -> 0 us
  Pallas kernels: 0 us -> 19.5 us
  local copies, waits for them, and re-layouts: 7.06 us -> 1.32 us
    add x2 -> x0, other arithmetic: 54.2 us -> none  [the longest x1 53.9 us: per_device(): smoothed = smoothed + kernel[a, b] * framed[a:a + STRIP, b:b + quarter_cols]]
    all_to_all x0 -> x1, blocking collectives: none -> 38.6 us  [per_device(): lax.all_to_all(packed.reshape(3 * owners, 1, LANES), 'own', split_axis=0,...]
    all_to_all x3 -> x1, waiting for transfers between devices: 34.3 us -> 6.07 us  [per_device(): lax.all_to_all(parts, 'grp', split_axis=0, concat_axis=0, tiled=True)]
    all_to_all x3 -> x1, starting transfers between devices: 30.8 us -> 4.03 us  [per_device(): lax.all_to_all(parts, 'grp', split_axis=0, concat_axis=0, tiled=True)]
    dot_general x12 -> x0, matrix products: 22 us -> none  [add_block(): jnp.dot(onehot_cells, onehot_lanes, preferred_element_type=jnp.float32)]
    pallas_call x0 -> x4, Pallas kernels: none -> 19.5 us  [the longest x1 12.5 us: per_device(): pl.pallas_call(bin_kernel, out_shape=jax.ShapeDtypeStruct((groups, STRIP,...]
    ppermute x4 -> x2, starting transfers between devices: 11.2 us -> 7.31 us  [the longest x1 3.77 us: per_device(): far = lax.ppermute(far, 'own', across)]
    slice x7 -> x0, local copies, waits for them, and re-layouts: 3.65 us -> none  [the longest x5 3.54 us: per_device(): smoothed = smoothed + kernel[a, b] * framed[a:a + STRIP, b:b + quarter_cols]]
  transfers between devices with their start and end apart: 7 -> 3, of which waited for: 5 -> 2; matrix products, arithmetic and copies ran while one was open for 3% -> 0% of each run, Pallas kernels for 0% -> 0%
where the time goes in v1:
time: 81 us; the launch traced here: 80.6 us
  blocking collectives  38.6 us (48%)
  Pallas kernels  19.5 us (24%)
  starting transfers between devices  11.3 us (14%)
  waiting for transfers between devices  9.84 us (12%)
  local copies, waits for them, and re-layouts  1.32 us (2%)
    all_to_all x1, blocking collectives, per_device(): lax.all_to_all(packed.reshape(3 * owners, 1, LANES), 'own', split_axis=0,...  38.6 us
    pallas_call x1, Pallas kernels, per_device(): pl.pallas_call(bin_kernel, out_shape=jax.ShapeDtypeStruct((groups, STRIP,...  12.5 us
    all_to_all x1, waiting for transfers between devices, per_device(): lax.all_to_all(parts, 'grp', split_axis=0, concat_axis=0, tiled=True)  6.07 us
    all_to_all x1, starting transfers between devices, per_device(): lax.all_to_all(parts, 'grp', split_axis=0, concat_axis=0, tiled=True)  4.03 us
    ppermute x1, starting transfers between devices, per_device(): far = lax.ppermute(far, 'own', across)  3.77 us
    ppermute x1, waiting for transfers between devices, per_device(): far = lax.ppermute(far, 'own', across)  3.76 us
    ppermute x1, starting transfers between devices, per_device(): near = lax.ppermute(near, 'own', on_chip)  3.54 us
    pallas_call x1, Pallas kernels, per_device(): pl.pallas_call(smooth_kernel, out_shape=jax.ShapeDtypeStruct((STRIP, quar...  3.47 us
  transfers between devices with their start and end apart: 3, of which 2 were waited for; matrix products, arithmetic and copies ran while one was open for 0% of the time, Pallas kernels for 0%

profile of v1, /device:TPU:25, one launch (start us, length us, event | category | flops | bytes accessed | tf_op | source)
XLA Modules:
  0.0 80.6 jit_solution(14699957340235237861)
XLA Ops:
  0.0 1.9 %pack.1 = f32[384,128]{1,0:T(8,128)} custom-call(s32[192,128]{1,0:T(8,128)} %bitcast.11, s32[192,128]{1,0:T(8,128)} %bitcast.12, bf16[192,1,128]{2,1,0:T(2,128)(2,1)} %bitcast.13, s32[1,128]{1,0:T(1,128)} %bitcast.14), custom_call_target="tpu_custom_call" | custom-call | tf_op jit(solution)/shard_map/pack/pallas_call | solution.py:156
  1.9 38.6 %all_to_all.10 = f32[384,1,128]{2,1,0:T(1,128)S(1)} all-to-all(f32[384,1,128]{2,1,0:T(1,128)} %bitcast.10), channel_id=1, replica_groups=mesh['grp'=4,'own'=128] {'own'}, dimensions={0} | all-to-all | bytes 393216 | tf_op jit(solution)/shard_map/all_to_all | solution.py:169
  40.5 12.5 %bin.1 = bf16[4,8,4224]{2,1,0:T(8,128)(2,1)} custom-call(f32[384,128]{1,0:T(8,128)S(1)} %bitcast.9), custom_call_target="tpu_custom_call" | custom-call | tf_op jit(solution)/shard_map/bin/pallas_call | solution.py:172
  53.0 4.0 %all-to-all-start.1 = ((bf16[4,8,4224]{2,1,0:T(8,128)(2,1)}), bf16[4,8,4224]{2,1,0:T(8,128)(2,1)S(1)}, u32[]{:S(2)}, u32[]{:S(2)}) async-start(bf16[4,8,4224]{2,1,0:T(8,128)(2,1)} %bin.1), calls=%async_computation.1 | async-start | bytes 540672 | tf_op jit(solution)/shard_map/all_to_all | solution.py:182
  57.0 6.1 %all-to-all-done.1.parts_ref = bf16[4,8,4224]{2,1,0:T(8,128)(2,1)S(1)} async-done(((bf16[4,8,4224]{2,1,0:T(8,128)(2,1)}), bf16[4,8,4224]{2,1,0:T(8,128)(2,1)S(1)}, u32[]{:S(2)}, u32[]{:S(2)}) %all-to-all-start.1) | async-done | bytes 270368 | tf_op jit(solution)/shard_map/all_to_all | solution.py:182
  63.1 0.0 copy-start
  63.1 0.7 copy-done
  63.8 1.7 %total.1 = (f32[8,4224]{1,0:T(8,128)}, bf16[4,4224]{1,0:T(4,128)(2,1)}, bf16[4,4224]{1,0:T(4,128)(2,1)}) custom-call(s32[1]{0:T(128)} %bitcast.parity_ref, bf16[4,8,4224]{2,1,0:T(8,128)(2,1)} %copy-done), custom_call_target="tpu_custom_call" | custom-call | tf_op jit(solution)/shard_map/total/pallas_call | solution.py:185
  65.4 3.5 %collective-permute-start = (bf16[4,4224]{1,0:T(4,128)(2,1)}, bf16[4,4224]{1,0:T(4,128)(2,1)S(1)}, u32[]{:S(2)}, u32[]{:S(2)}) collective-permute-start(bf16[4,4224]{1,0:T(4,128)(2,1)} %get-tuple-element.9), channel_id=1, source_target_pairs={{0,1},{1,0},{2,3},{3,2},{4,5},{5,4},{6,7},{7,6},{8,9},{9,8},{10,11... | collective-permute-start | bytes 101384 | tf_op jit(solution)/shard_map/ppermute | solution.py:199
  69.0 3.8 %collective-permute-start.1 = (bf16[4,4224]{1,0:T(4,128)(2,1)}, bf16[4,4224]{1,0:T(4,128)(2,1)S(1)}, u32[]{:S(2)}, u32[]{:S(2)}) collective-permute-start(bf16[4,4224]{1,0:T(4,128)(2,1)} %get-tuple-element.10), channel_id=1, source_target_pairs={{1,2},{3,4},{5,6},{7,8},{9,10},{11,12},{13,14},{15,16},{17,18},{19... | collective-permute-start | bytes 101384 | tf_op jit(solution)/shard_map/ppermute | solution.py:200
  72.7 0.0 collective-permute-done.near_ref
  72.8 0.0 copy-start.1
  72.8 3.8 %collective-permute-done.1.far_ref = bf16[4,4224]{1,0:T(4,128)(2,1)S(1)} collective-permute-done((bf16[4,4224]{1,0:T(4,128)(2,1)}, bf16[4,4224]{1,0:T(4,128)(2,1)S(1)}, u32[]{:S(2)}, u32[]{:S(2)}) %collective-permute-start.1) | collective-permute-done | bytes 33824 | tf_op jit(solution)/shard_map/ppermute | solution.py:200
  76.5 0.0 copy-start.2
  76.5 0.0 copy-done.1
  76.5 0.6 copy-done.2
  77.1 3.5 %smooth.1 = f32[8,4096]{1,0:T(8,128)} custom-call(s32[1]{0:T(128)} %bitcast.parity_ref, f32[9,9]{1,0:T(8,128)} %kernel_ref.1, f32[8,4224]{1,0:T(8,128)} %get-tuple-element.8.own_ref, bf16[4,4224]{1,0:T(4,128)(2,1)} %copy-done.1, bf16[4,4224]{1,0:T(4,128)(2,1)} %copy-done.2), custom_call_target="tpu_custom_call" | custom-call | tf_op jit(solution)/shard_map/smooth/pallas_call | solution.py:201
Async XLA Ops:
  53.0 10.1 %all-to-all-start.1 = ((bf16[4,8,4224]{2,1,0:T(8,128)(2,1)}), bf16[4,8,4224]{2,1,0:T(8,128)(2,1)S(1)}, u32[]{:S(2)}, u32[]{:S(2)}) async-start(bf16[4,8,4224]{2,1,0:T(8,128)(2,1)} %bin.1), calls=%async_computation.1 | async-start | bytes 540672 | tf_op jit(solution)/shard_map/all_to_all | solution.py:182
  63.1 0.7 copy-start
  65.4 7.3 %collective-permute-start = (bf16[4,4224]{1,0:T(4,128)(2,1)}, bf16[4,4224]{1,0:T(4,128)(2,1)S(1)}, u32[]{:S(2)}, u32[]{:S(2)}) collective-permute-start(bf16[4,4224]{1,0:T(4,128)(2,1)} %get-tuple-element.9), channel_id=1, source_target_pairs={{0,1},{1,0},{2,3},{3,2},{4,5},{5,4},{6,7},{7,6},{8,9},{9,8},{10,11... | collective-permute-start | bytes 101384 | tf_op jit(solution)/shard_map/ppermute | solution.py:199
  69.0 7.6 %collective-permute-start.1 = (bf16[4,4224]{1,0:T(4,128)(2,1)}, bf16[4,4224]{1,0:T(4,128)(2,1)S(1)}, u32[]{:S(2)}, u32[]{:S(2)}) collective-permute-start(bf16[4,4224]{1,0:T(4,128)(2,1)} %get-tuple-element.10), channel_id=1, source_target_pairs={{1,2},{3,4},{5,6},{7,8},{9,10},{11,12},{13,14},{15,16},{17,18},{19... | collective-permute-start | bytes 101384 | tf_op jit(solution)/shard_map/ppermute | solution.py:200
  72.8 3.8 %copy-start.1 = (bf16[4,4224]{1,0:T(4,128)(2,1)}, bf16[4,4224]{1,0:T(4,128)(2,1)S(1)}, u32[]{:S(2)}) copy-start(bf16[4,4224]{1,0:T(4,128)(2,1)S(1)} %collective-permute-done.near_ref) | copy-start | bytes 101380
  76.5 0.6 copy-start.2

commit v2 on v1

--- a/solution.py
+++ b/solution.py
@@ -10,9 +10,12 @@
 CAP = 192
 LANES = 128
 HALO = 4
+TAPS = 2 * HALO + 1
+PARTS = 32
+TERM = 48
 SPAN = 256
 CELLS = STRIP * W // SPAN
-ROWS = 8
+ROWS = 64
 
 
 def vmem_spec():
@@ -21,6 +24,10 @@
 
 def smem_spec():
     return pl.BlockSpec(memory_space=pltpu.SMEM)
+
+
+def limit(mebibytes):
+    return pltpu.CompilerParams(vmem_limit_bytes=mebibytes * 2**20)
 
 
 def pack_kernel(row_ref, col_ref, weight_ref, count_ref, out_ref, wide_ref):
@@ -43,7 +50,7 @@
     for k in range(3):
         tile_row = row_ref[pl.ds(k, pairs, stride=3), :]
         column = col_ref[pl.ds(k, pairs, stride=3), :]
-        index = ((column // SPAN) * STRIP + tile_row) * SPAN + column % SPAN
+        index = (((column >> 8) * STRIP + tile_row) << 8) + (column & 255)
         ids.append(index.astype(jnp.float32))
         masses.append(jnp.where(lives[k], wide_ref[pl.ds(k, pairs, stride=3), :], 0.0))
     half = LANES // 2
@@ -69,8 +76,8 @@
     ):
         ids = ids.astype(jnp.int32)
         here = pl.ds(at, ids.shape[0])
-        first_ref[here, :] = (ids // SPAN).astype(jnp.float32) - 256.0
-        second_ref[here, :] = (ids % SPAN).astype(jnp.float32)
+        first_ref[here, :] = ((ids >> 8) - 256).astype(jnp.float32)
+        second_ref[here, :] = (ids & 255).astype(jnp.float32)
         mass_ref[here, :] = masses
     first_iota = (
         lax.broadcasted_iota(jnp.int32, (CELLS, LANES), 0).astype(jnp.float32) - 256.0
@@ -98,52 +105,78 @@
         return carry
 
     lax.fori_loop(0, first_ref.shape[0] // ROWS, step, 0)
-    quarters, _, width = out_ref.shape
+    width = out_ref.shape[1]
+    quarters = out_ref.shape[0] // STRIP
     span = width - LANES
     groups = span // SPAN
     low8 = lax.broadcasted_iota(jnp.int32, (STRIP, LANES), 1) < 64
     blank = jnp.zeros((STRIP, LANES), jnp.float32)
     for q in range(quarters):
+        rows = pl.ds(q * STRIP, STRIP)
         for c in range(groups):
             at = (q * groups + c) * STRIP
-            out_ref[q, :, c * SPAN : (c + 1) * SPAN] = acc_ref[at : at + STRIP, :].astype(jnp.bfloat16)
+            out_ref[rows, c * SPAN : (c + 1) * SPAN] = acc_ref[at : at + STRIP, :].astype(jnp.bfloat16)
         at = q * groups * STRIP
         before = acc_ref[at - STRIP : at, LANES:] if q else blank
         at += groups * STRIP
         after = acc_ref[at : at + STRIP, :LANES] if q < quarters - 1 else blank
-        out_ref[q, :, span:] = jnp.where(low8, after, before).astype(jnp.bfloat16)
-
-
-def sum_kernel(parity_ref, parts_ref, sum_ref, near_ref, far_ref):
-    total = parts_ref[0].astype(jnp.float32)
-    for g in range(1, parts_ref.shape[0]):
-        total = total + parts_ref[g].astype(jnp.float32)
-    sum_ref[...] = total
-    top = total[:HALO]
-    bottom = total[HALO:]
-    is_odd = parity_ref[0] == 1
-    near_ref[...] = jnp.where(is_odd, top, bottom).astype(jnp.bfloat16)
-    far_ref[...] = jnp.where(is_odd, bottom, top).astype(jnp.bfloat16)
-
-
-def smooth_kernel(parity_ref, kernel_ref, own_ref, near_ref, far_ref, out_ref):
-    own = own_ref[...]
+        out_ref[rows, span:] = jnp.where(low8, after, before).astype(jnp.bfloat16)
+
+
+def band_kernel(parity_ref, kernel_ref, band_ref, odd_ref):
+    parity = parity_ref[0]
+    row = lax.broadcasted_iota(jnp.int32, (STRIP, 3 * TERM), 0)
+    lane = lax.broadcasted_iota(jnp.int32, (STRIP, 3 * TERM), 1)
+    source = lane % TERM
+    near = source - PARTS
+    far = near - HALO
+    near = near + (1 - parity) * (STRIP + HALO)
+    far = far + parity * (STRIP + HALO)
+    framed = jnp.where(
+        source < PARTS,
+        HALO + source % STRIP,
+        jnp.where(source < PARTS + HALO, near, jnp.where(source < PARTS + 2 * HALO, far, -STRIP)),
+    )
+    tap = framed - row
+    for b in range(TAPS):
+        whole = jnp.zeros(tap.shape, jnp.float32)
+        for a in range(TAPS):
+            whole = jnp.where(tap == a, kernel_ref[a, b], whole)
+        high = whole.astype(jnp.bfloat16).astype(jnp.float32)
+        rest = whole - high
+        middle = rest.astype(jnp.bfloat16).astype(jnp.float32)
+        term = jnp.where(lane < TERM, high, jnp.where(lane < 2 * TERM, middle, rest - middle))
+        band_ref[pl.ds(b * STRIP, STRIP), :] = term
+    odd_ref[...] = jnp.broadcast_to(parity.astype(jnp.float32), odd_ref.shape)
+
+
+def sum_kernel(odd_ref, parts_ref, near_ref, far_ref):
+    is_odd = odd_ref[:HALO, :] > 0.5
+    for t in range(parts_ref.shape[1] // LANES):
+        here = slice(t * LANES, (t + 1) * LANES)
+        total = parts_ref[:STRIP, here].astype(jnp.float32)
+        for g in range(1, parts_ref.shape[0] // STRIP):
+            total = total + parts_ref[g * STRIP : (g + 1) * STRIP, here].astype(jnp.float32)
+        top = total[:HALO]
+        bottom = total[HALO:]
+        near_ref[:, here] = jnp.where(is_odd, top, bottom).astype(jnp.bfloat16)
+        far_ref[:, here] = jnp.where(is_odd, bottom, top).astype(jnp.bfloat16)
+
+
+def smooth_kernel(band_ref, parts_ref, near_ref, far_ref, out_ref):
+    width = parts_ref.shape[1]
     near = near_ref[...].astype(jnp.float32)
     far = far_ref[...].astype(jnp.float32)
-    is_odd = parity_ref[0] == 1
-    above = jnp.where(is_odd, near, far)
-    below = jnp.where(is_odd, far, near)
-    frame = jnp.concatenate([above, own, below], axis=0)
-    width = frame.shape[1]
-    wins = [frame[a : a + STRIP] for a in range(9)]
-    total = None
-    for b in range(9):
-        part = kernel_ref[0, b] * wins[0]
-        for a in range(1, 9):
-            part = part + kernel_ref[a, b] * wins[a]
-        shift = (HALO - b) % width
-        part = pltpu.roll(part, shift, 1) if shift else part
-        total = part if total is None else total + part
+    blank = jnp.zeros((STRIP, width), jnp.float32)
+    halo = jnp.concatenate([near, far, blank], axis=0).astype(jnp.bfloat16)
+    frame = jnp.concatenate([parts_ref[...], halo], axis=0)
+    frame = jnp.concatenate([frame, frame, frame], axis=0)
+    shifted = jnp.dot(band_ref[...].astype(jnp.bfloat16), frame, preferred_element_type=jnp.float32)
+    total = shifted[HALO * STRIP : (HALO + 1) * STRIP]
+    for b in range(TAPS):
+        if b != HALO:
+            part = shifted[b * STRIP : (b + 1) * STRIP]
+            total = total + pltpu.roll(part, (HALO - b) % width, 1)
     out_ref[...] = total[:, : out_ref.shape[1]]
 
 
@@ -159,6 +192,7 @@
         in_specs=[vmem_spec()] * 4,
         out_specs=vmem_spec(),
         scratch_shapes=[pltpu.VMEM((points, LANES), jnp.float32)],
+        compiler_params=limit(4),
         name="pack",
     )(
         tile_row.reshape(points, LANES),
@@ -171,40 +205,49 @@
     ).reshape(3 * owners, LANES)
     parts = pl.pallas_call(
         bin_kernel,
-        out_shape=jax.ShapeDtypeStruct((groups, STRIP, width), jnp.bfloat16),
+        out_shape=jax.ShapeDtypeStruct((groups * STRIP, width), jnp.bfloat16),
         in_specs=[vmem_spec()],
         out_specs=vmem_spec(),
         scratch_shapes=[pltpu.VMEM((points, LANES), jnp.float32)] * 3
         + [pltpu.VMEM((CELLS, SPAN), jnp.float32)],
-        compiler_params=pltpu.CompilerParams(vmem_limit_bytes=48 * 2**20),
+        compiler_params=limit(32),
         name="bin",
     )(arrived)
-    parts = lax.all_to_all(parts, "grp", split_axis=0, concat_axis=0, tiled=True)
-    me = lax.axis_index("own")
-    parity = (me % 2).reshape(1).astype(jnp.int32)
-    own, near, far = pl.pallas_call(
+    sent, kernel = lax.optimization_barrier((parts, kernel))
+    parts = lax.all_to_all(sent, "grp", split_axis=0, concat_axis=0, tiled=True)
+    parity = (lax.axis_index("own") & 1).reshape(1).astype(jnp.int32)
+    band, odd = pl.pallas_call(
+        band_kernel,
+        out_shape=(
+            jax.ShapeDtypeStruct((TAPS * STRIP, 3 * TERM), jnp.float32),
+            jax.ShapeDtypeStruct((STRIP, LANES), jnp.float32),
+        ),
+        in_specs=[smem_spec(), smem_spec()],
+        out_specs=(vmem_spec(),) * 2,
+        compiler_params=limit(4),
+        name="band",
+    )(parity, kernel)
+    near, far = pl.pallas_call(
         sum_kernel,
-        out_shape=(
-            jax.ShapeDtypeStruct((STRIP, width), jnp.float32),
-            jax.ShapeDtypeStruct((HALO, width), jnp.bfloat16),
-            jax.ShapeDtypeStruct((HALO, width), jnp.bfloat16),
-        ),
-        in_specs=[smem_spec(), vmem_spec()],
-        out_specs=(vmem_spec(),) * 3,
+        out_shape=(jax.ShapeDtypeStruct((HALO, width), jnp.bfloat16),) * 2,
+        in_specs=[vmem_spec()] * 2,
+        out_specs=(vmem_spec(),) * 2,
+        compiler_params=limit(4),
         name="total",
-    )(parity, parts)
+    )(odd, parts)
     on_chip = [(i, i ^ 1) for i in range(owners)]
     across = [(i, i + 1) for i in range(1, owners - 1, 2)]
     across = across + [(j, i) for i, j in across]
+    far = lax.ppermute(far, "own", across)
     near = lax.ppermute(near, "own", on_chip)
-    far = lax.ppermute(far, "own", across)
     return pl.pallas_call(
         smooth_kernel,
         out_shape=jax.ShapeDtypeStruct((STRIP, quarter), jnp.float32),
-        in_specs=[smem_spec(), smem_spec()] + [vmem_spec()] * 3,
+        in_specs=[vmem_spec()] * 4,
         out_specs=vmem_spec(),
+        compiler_params=limit(16),
         name="smooth",
-    )(parity, kernel, own, near, far)
+    )(band, parts, near, far)
 
 
 def solution(mesh):

time: 81 us -> 72.5 us (0.90)
  Pallas kernels: 19.5 us -> 10.1 us
  local copies, waits for them, and re-layouts: 1.32 us -> 4.03 us
  waiting for transfers between devices: 9.84 us -> 8.13 us
    pallas_call x2 -> x3, Pallas kernels: 14.2 us -> 8.76 us  [the longest x1 7.95 us: per_device(): pl.pallas_call(bin_kernel, out_shape=jax.ShapeDtypeStruct((groups * STRIP...]
    unnamed x6 -> x10, local copies, waits for them, and re-layouts: 1.32 us -> 4.03 us
    pallas_call x1, Pallas kernels: 3.47 us -> 1.18 us  [per_device(): pl.pallas_call(smooth_kernel, out_shape=jax.ShapeDtypeStruct((STRIP, quar...]
    pallas_call x1, Pallas kernels: 1.86 us -> 0.2 us  [per_device(): pl.pallas_call(pack_kernel, out_shape=jax.ShapeDtypeStruct((3 * owners, L...]
    all_to_all x1, waiting for transfers between devices: 6.07 us -> 4.6 us  [per_device(): parts = lax.all_to_all(sent, 'grp', split_axis=0, concat_axis=0, tiled=True)]
  transfers between devices with their start and end apart: 3 -> 3, of which waited for: 2 -> 2; matrix products, arithmetic and copies ran while one was open for 0% -> 0% of each run, Pallas kernels for 0% -> 1%
where the time goes in v2:
time: 72.5 us; the launch traced here: 72.1 us
  blocking collectives  38.4 us (53%)
  starting transfers between devices  11.4 us (16%)
  Pallas kernels  10.1 us (14%)
  waiting for transfers between devices  8.13 us (11%)
  local copies, waits for them, and re-layouts  4.03 us (6%)
    all_to_all x1, blocking collectives, per_device(): lax.all_to_all(packed.reshape(3 * owners, 1, LANES), 'own', split_axis=0,...  38.4 us
    pallas_call x1, Pallas kernels, per_device(): pl.pallas_call(bin_kernel, out_shape=jax.ShapeDtypeStruct((groups * STRIP...  7.95 us
    all_to_all x1, waiting for transfers between devices, per_device(): parts = lax.all_to_all(sent, 'grp', split_axis=0, concat_axis=0, tiled=True)  4.6 us
    unnamed x10, local copies, waits for them, and re-layouts  4.03 us
    all_to_all x1, starting transfers between devices, per_device(): parts = lax.all_to_all(sent, 'grp', split_axis=0, concat_axis=0, tiled=True)  4.01 us
    ppermute x1, starting transfers between devices, per_device(): far = lax.ppermute(far, 'own', across)  3.81 us
    ppermute x1, starting transfers between devices, per_device(): near = lax.ppermute(near, 'own', on_chip)  3.57 us
    ppermute x1, waiting for transfers between devices, per_device(): far = lax.ppermute(far, 'own', across)  3.52 us
  transfers between devices with their start and end apart: 3, of which 2 were waited for; matrix products, arithmetic and copies ran while one was open for 0% of the time, Pallas kernels for 1%

profile of v2, /device:TPU:25, one launch (start us, length us, event | category | flops | bytes accessed | tf_op | source)
XLA Modules:
  0.0 72.1 jit_solution(10086408443821484727)
XLA Ops:
  0.0 0.0 copy-start.4
  0.0 0.7 copy-done.4
  0.7 0.0 copy-start
  0.7 0.9 %copy-done = s32[1,1,24576]{2,1,0:T(1,128)S(1)} copy-done((s32[1,1,24576]{2,1,0:T(1,128)S(1)}, s32[1,1,24576]{2,1,0:T(1,128)}, u32[]{:S(2)}) %copy-start) | copy-done | bytes 98328
  1.5 0.0 copy-start.1
  1.6 0.9 %copy-done.1 = s32[1,1,24576]{2,1,0:T(1,128)S(1)} copy-done((s32[1,1,24576]{2,1,0:T(1,128)S(1)}, s32[1,1,24576]{2,1,0:T(1,128)}, u32[]{:S(2)}) %copy-start.1) | copy-done | bytes 98328
  2.4 0.0 copy-start.2
  2.4 0.9 %copy-done.2 = bf16[1,1,24576]{2,1,0:T(2,128)(2,1)S(1)} copy-done((bf16[1,1,24576]{2,1,0:T(2,128)(2,1)S(1)}, bf16[1,1,24576]{2,1,0:T(2,128)(2,1)}, u32[]{:S(2)}) %copy-start.2) | copy-done | bytes 49176
  3.3 0.2 pack.1
  3.5 38.4 %all_to_all.16 = f32[384,1,128]{2,1,0:T(1,128)S(1)} all-to-all(f32[384,1,128]{2,1,0:T(1,128)S(1)} %bitcast.14), channel_id=1, replica_groups=mesh['grp'=4,'own'=128] {'own'}, dimensions={0} | all-to-all | bytes 393216 | tf_op jit(solution)/shard_map/all_to_all | solution.py:203
  41.9 8.0 %bin.1 = bf16[32,4224]{1,0:T(8,128)(2,1)} custom-call(f32[384,128]{1,0:T(8,128)S(1)} %bitcast.13), custom_call_target="tpu_custom_call" | custom-call | tf_op jit(solution)/shard_map/bin/pallas_call | solution.py:206
  49.9 4.0 %all-to-all-start.1 = ((bf16[4,8,4224]{2,1,0:T(8,128)(2,1)}), bf16[4,8,4224]{2,1,0:T(8,128)(2,1)S(1)}, u32[]{:S(2)}, u32[]{:S(2)}) async-start(bf16[4,8,4224]{2,1,0:T(8,128)(2,1)} %bitcast.8), calls=%async_computation.1 | async-start | bytes 540672 | tf_op jit(solution)/shard_map/all_to_all | solution.py:217
  53.9 0.0 copy-start.3
  53.9 0.7 copy-done.3
  54.6 0.7 %band.1 = (f32[72,144]{1,0:T(8,128)S(1)}, f32[8,128]{1,0:T(8,128)S(1)}) custom-call(s32[1]{0:T(128)} %bitcast.parity_ref, f32[9,9]{1,0:T(8,128)S(1)} %copy-done.3), custom_call_target="tpu_custom_call" | custom-call | tf_op jit(solution)/shard_map/band/pallas_call | solution.py:219
  55.3 4.6 %all-to-all-done.1 = bf16[4,8,4224]{2,1,0:T(8,128)(2,1)S(1)} async-done(((bf16[4,8,4224]{2,1,0:T(8,128)(2,1)}), bf16[4,8,4224]{2,1,0:T(8,128)(2,1)S(1)}, u32[]{:S(2)}, u32[]{:S(2)}) %all-to-all-start.1) | async-done | bytes 270368 | tf_op jit(solution)/shard_map/all_to_all | solution.py:217
  59.9 0.1 total.1
  60.0 3.6 %collective-permute-start = (bf16[4,4224]{1,0:T(4,128)(2,1)S(1)}, bf16[4,4224]{1,0:T(4,128)(2,1)S(1)}, u32[]{:S(2)}, u32[]{:S(2)}) collective-permute-start(bf16[4,4224]{1,0:T(4,128)(2,1)S(1)} %get-tuple-element.15), channel_id=1, source_target_pairs={{0,1},{1,0},{2,3},{3,2},{4,5},{5,4},{6,7},{7,6},{8,9},{9,8},{10,11... | collective-permute-start | bytes 101384 | tf_op jit(solution)/shard_map/ppermute | solution.py:242
  63.6 3.8 %collective-permute-start.1 = (bf16[4,4224]{1,0:T(4,128)(2,1)S(1)}, bf16[4,4224]{1,0:T(4,128)(2,1)S(1)}, u32[]{:S(2)}, u32[]{:S(2)}) collective-permute-start(bf16[4,4224]{1,0:T(4,128)(2,1)S(1)} %get-tuple-element.16), channel_id=1, source_target_pairs={{1,2},{3,4},{5,6},{7,8},{9,10},{11,12},{13,14},{15,16},{17,18},{19... | collective-permute-start | bytes 101384 | tf_op jit(solution)/shard_map/ppermute | solution.py:241
  67.4 0.0 collective-permute-done.near_ref
  67.4 3.5 %collective-permute-done.1.far_ref = bf16[4,4224]{1,0:T(4,128)(2,1)S(1)} collective-permute-done((bf16[4,4224]{1,0:T(4,128)(2,1)S(1)}, bf16[4,4224]{1,0:T(4,128)(2,1)S(1)}, u32[]{:S(2)}, u32[]{:S(2)}) %collective-permute-start.1) | collective-permute-done | bytes 33824 | tf_op jit(solution)/shard_map/ppermute | solution.py:241
  70.9 1.2 %smooth.1 = f32[8,4096]{1,0:T(8,128)} custom-call(f32[72,144]{1,0:T(8,128)S(1)} %get-tuple-element.12.band_ref, bf16[32,4224]{1,0:T(8,128)(2,1)S(1)} %bitcast.12, bf16[4,4224]{1,0:T(4,128)(2,1)S(1)} %collective-permute-done.near_ref, bf16[4,4224]{1,0:T(4,128)(2,1)S(1)} %collective-permute-done.1.far_ref), custom_call_target="tpu_custom_call" | custom-call | tf_op jit(solution)/shard_map/smooth/pallas_call | solution.py:243
Async XLA Ops:
  0.0 0.7 copy-start.4
  0.7 0.9 %copy-start = (s32[1,1,24576]{2,1,0:T(1,128)S(1)}, s32[1,1,24576]{2,1,0:T(1,128)}, u32[]{:S(2)}) copy-start(s32[1,1,24576]{2,1,0:T(1,128)} %param.5) | copy-start | bytes 294916
  1.5 0.9 %copy-start.1 = (s32[1,1,24576]{2,1,0:T(1,128)S(1)}, s32[1,1,24576]{2,1,0:T(1,128)}, u32[]{:S(2)}) copy-start(s32[1,1,24576]{2,1,0:T(1,128)} %param.6) | copy-start | bytes 294916
  2.4 0.9 %copy-start.2 = (bf16[1,1,24576]{2,1,0:T(2,128)(2,1)S(1)}, bf16[1,1,24576]{2,1,0:T(2,128)(2,1)}, u32[]{:S(2)}) copy-start(bf16[1,1,24576]{2,1,0:T(2,128)(2,1)} %param.7) | copy-start | bytes 147460
  49.9 10.1 %all-to-all-start.1 = ((bf16[4,8,4224]{2,1,0:T(8,128)(2,1)}), bf16[4,8,4224]{2,1,0:T(8,128)(2,1)S(1)}, u32[]{:S(2)}, u32[]{:S(2)}) async-start(bf16[4,8,4224]{2,1,0:T(8,128)(2,1)} %bitcast.8), calls=%async_computation.1 | async-start | bytes 540672 | tf_op jit(solution)/shard_map/all_to_all | solution.py:217
  53.9 0.7 copy-start.3
  60.0 7.4 %collective-permute-start = (bf16[4,4224]{1,0:T(4,128)(2,1)S(1)}, bf16[4,4224]{1,0:T(4,128)(2,1)S(1)}, u32[]{:S(2)}, u32[]{:S(2)}) collective-permute-start(bf16[4,4224]{1,0:T(4,128)(2,1)S(1)} %get-tuple-element.15), channel_id=1, source_target_pairs={{0,1},{1,0},{2,3},{3,2},{4,5},{5,4},{6,7},{7,6},{8,9},{9,8},{10,11... | collective-permute-start | bytes 101384 | tf_op jit(solution)/shard_map/ppermute | solution.py:242
  63.6 7.4 %collective-permute-start.1 = (bf16[4,4224]{1,0:T(4,128)(2,1)S(1)}, bf16[4,4224]{1,0:T(4,128)(2,1)S(1)}, u32[]{:S(2)}, u32[]{:S(2)}) collective-permute-start(bf16[4,4224]{1,0:T(4,128)(2,1)S(1)} %get-tuple-element.16), channel_id=1, source_target_pairs={{1,2},{3,4},{5,6},{7,8},{9,10},{11,12},{13,14},{15,16},{17,18},{19... | collective-permute-start | bytes 101384 | tf_op jit(solution)/shard_map/ppermute | solution.py:241

commit v3 on v2

--- a/solution.py
+++ b/solution.py
@@ -1,3 +1,5 @@
+import functools
+
 import jax
 import jax.numpy as jnp
 from jax import lax
@@ -15,7 +17,7 @@
 TERM = 48
 SPAN = 256
 CELLS = STRIP * W // SPAN
-ROWS = 64
+ROWS = 96
 
 
 def vmem_spec():
@@ -30,7 +32,17 @@
     return pltpu.CompilerParams(vmem_limit_bytes=mebibytes * 2**20)
 
 
-def pack_kernel(row_ref, col_ref, weight_ref, count_ref, out_ref, wide_ref):
+def pack_kernel(row_in, col_in, weight_in, count_in, out_ref, row_ref, col_ref, weight_ref, count_ref, wide_ref, sems):
+    copies = [
+        pltpu.make_async_copy(source, target, sems.at[i])
+        for i, (source, target) in enumerate(
+            ((weight_in, weight_ref), (count_in, count_ref), (row_in, row_ref), (col_in, col_ref))
+        )
+    ]
+    for copy in copies:
+        copy.start()
+    for copy in copies:
+        copy.wait()
     points = row_ref.shape[0]
     pairs = points // 3
     for i in range(points):
@@ -150,17 +162,14 @@
     odd_ref[...] = jnp.broadcast_to(parity.astype(jnp.float32), odd_ref.shape)
 
 
-def sum_kernel(odd_ref, parts_ref, near_ref, far_ref):
-    is_odd = odd_ref[:HALO, :] > 0.5
+def edge_kernel(odd_ref, parts_ref, edge_ref, *, top_if_odd):
+    is_top = (odd_ref[:HALO, :] > 0.5) == top_if_odd
     for t in range(parts_ref.shape[1] // LANES):
         here = slice(t * LANES, (t + 1) * LANES)
         total = parts_ref[:STRIP, here].astype(jnp.float32)
         for g in range(1, parts_ref.shape[0] // STRIP):
             total = total + parts_ref[g * STRIP : (g + 1) * STRIP, here].astype(jnp.float32)
-        top = total[:HALO]
-        bottom = total[HALO:]
-        near_ref[:, here] = jnp.where(is_odd, top, bottom).astype(jnp.bfloat16)
-        far_ref[:, here] = jnp.where(is_odd, bottom, top).astype(jnp.bfloat16)
+        edge_ref[:, here] = jnp.where(is_top, total[:HALO], total[HALO:]).astype(jnp.bfloat16)
 
 
 def smooth_kernel(band_ref, parts_ref, near_ref, far_ref, out_ref):
@@ -189,16 +198,28 @@
     packed = pl.pallas_call(
         pack_kernel,
         out_shape=jax.ShapeDtypeStruct((3 * owners, LANES), jnp.float32),
-        in_specs=[vmem_spec()] * 4,
+        in_specs=[pl.BlockSpec(memory_space=pltpu.HBM)] * 4,
         out_specs=vmem_spec(),
-        scratch_shapes=[pltpu.VMEM((points, LANES), jnp.float32)],
+        scratch_shapes=[
+            pltpu.VMEM((points, LANES), jnp.int32),
+            pltpu.VMEM((points, LANES), jnp.int32),
+            pltpu.VMEM((points, 1, LANES), jnp.bfloat16),
+            pltpu.VMEM((1, owners), jnp.int32),
+            pltpu.VMEM((points, LANES), jnp.float32),
+            pltpu.SemaphoreType.DMA((4,)),
+        ],
         compiler_params=limit(4),
         name="pack",
     )(
-        tile_row.reshape(points, LANES),
-        pixel_col.reshape(points, LANES),
-        weight.reshape(points, 1, LANES),
-        counts.reshape(1, owners),
+        *(
+            pltpu.with_memory_space_constraint(value.reshape(shape), pltpu.HBM)
+            for value, shape in (
+                (tile_row, (points, LANES)),
+                (pixel_col, (points, LANES)),
+                (weight, (points, 1, LANES)),
+                (counts, (1, owners)),
+            )
+        )
     )
     arrived = lax.all_to_all(
         packed.reshape(3 * owners, 1, LANES), "own", split_axis=0, concat_axis=0, tiled=True
@@ -227,14 +248,19 @@
         compiler_params=limit(4),
         name="band",
     )(parity, kernel)
-    near, far = pl.pallas_call(
-        sum_kernel,
-        out_shape=(jax.ShapeDtypeStruct((HALO, width), jnp.bfloat16),) * 2,
-        in_specs=[vmem_spec()] * 2,
-        out_specs=(vmem_spec(),) * 2,
-        compiler_params=limit(4),
-        name="total",
-    )(odd, parts)
+    def edge(parts, top_if_odd, name):
+        return pl.pallas_call(
+            functools.partial(edge_kernel, top_if_odd=top_if_odd),
+            out_shape=jax.ShapeDtypeStruct((HALO, width), jnp.bfloat16),
+            in_specs=[vmem_spec()] * 2,
+            out_specs=vmem_spec(),
+            compiler_params=limit(4),
+            name=name,
+        )(odd, parts)
+
+    near = edge(parts, True, "near")
+    near, later = lax.optimization_barrier((near, parts))
+    far = edge(later, False, "far")
     on_chip = [(i, i ^ 1) for i in range(owners)]
     across = [(i, i + 1) for i in range(1, owners - 1, 2)]
     across = across + [(j, i) for i, j in across]

time: 72.5 us -> 68.1 us (0.939)
  local copies, waits for them, and re-layouts: 4.03 us -> 0.7 us
  waiting for transfers between devices: 8.13 us -> 5.77 us
  Pallas kernels: 10.1 us -> 11 us
    ppermute x1, waiting for transfers between devices: 3.52 us -> 0.01 us  [per_device(): far = lax.ppermute(far, 'own', across)]
    unnamed x10 -> x2, local copies, waits for them, and re-layouts: 4.03 us -> 0.7 us
    ppermute x1, starting transfers between devices: 3.57 us -> 1.92 us  [per_device(): near = lax.ppermute(near, 'own', on_chip)]
    ppermute x1, starting transfers between devices: 3.81 us -> 5.45 us  [per_device(): far = lax.ppermute(far, 'own', across)]
    ppermute x1, waiting for transfers between devices: 0.01 us -> 1.16 us  [per_device(): near = lax.ppermute(near, 'own', on_chip)]
    pallas_call x1, Pallas kernels: 0.2 us -> 1.24 us  [per_device(): pl.pallas_call(pack_kernel, out_shape=jax.ShapeDtypeStruct((3 * owners, L...]
where the time goes in v3:
time: 68.1 us; the launch traced here: 67.3 us
  blocking collectives  38.4 us (56%)
  starting transfers between devices  11.4 us (17%)
  Pallas kernels  11 us (16%)
  waiting for transfers between devices  5.77 us (8%)
  local copies, waits for them, and re-layouts  0.7 us (1%)
    all_to_all x1, blocking collectives, per_device(): lax.all_to_all(packed.reshape(3 * owners, 1, LANES), 'own', split_axis=0,...  38.4 us
    pallas_call x1, Pallas kernels, per_device(): pl.pallas_call(bin_kernel, out_shape=jax.ShapeDtypeStruct((groups * STRIP...  7.73 us
    ppermute x1, starting transfers between devices, per_device(): far = lax.ppermute(far, 'own', across)  5.45 us
    all_to_all x1, waiting for transfers between devices, per_device(): parts = lax.all_to_all(sent, 'grp', split_axis=0, concat_axis=0, tiled=True)  4.61 us
    all_to_all x1, starting transfers between devices, per_device(): parts = lax.all_to_all(sent, 'grp', split_axis=0, concat_axis=0, tiled=True)  4.02 us
    ppermute x1, starting transfers between devices, per_device(): near = lax.ppermute(near, 'own', on_chip)  1.92 us
  transfers between devices with their start and end apart: 3, of which 2 were waited for; matrix products, arithmetic and copies ran while one was open for 0% of the time, Pallas kernels for 1%

profile of v3, /device:TPU:25, one launch (start us, length us, event | category | flops | bytes accessed | tf_op | source)
XLA Modules:
  0.0 67.3 jit_solution(9249241768451438068)
XLA Ops:
  0.0 1.2 %pack.1 = f32[384,128]{1,0:T(8,128)S(1)} custom-call(s32[192,128]{1,0:T(8,128)} %bitcast.16, s32[192,128]{1,0:T(8,128)} %bitcast.17, bf16[192,1,128]{2,1,0:T(2,128)(2,1)} %bitcast.18, s32[1,128]{1,0:T(1,128)} %bitcast.19), custom_call_target="tpu_custom_call" | custom-call | tf_op jit(solution)/shard_map/pack/pallas_call | solution.py:198
  1.2 38.4 %all_to_all.16 = f32[384,1,128]{2,1,0:T(1,128)S(1)} all-to-all(f32[384,1,128]{2,1,0:T(1,128)S(1)} %bitcast.15), channel_id=1, replica_groups=mesh['grp'=4,'own'=128] {'own'}, dimensions={0} | all-to-all | bytes 393216 | tf_op jit(solution)/shard_map/all_to_all | solution.py:224
  39.6 7.7 %bin.1 = bf16[32,4224]{1,0:T(8,128)(2,1)} custom-call(f32[384,128]{1,0:T(8,128)S(1)} %bitcast.14), custom_call_target="tpu_custom_call" | custom-call | tf_op jit(solution)/shard_map/bin/pallas_call | solution.py:227
  47.4 4.0 %all-to-all-start.1 = ((bf16[4,8,4224]{2,1,0:T(8,128)(2,1)}), bf16[4,8,4224]{2,1,0:T(8,128)(2,1)S(1)}, u32[]{:S(2)}, u32[]{:S(2)}) async-start(bf16[4,8,4224]{2,1,0:T(8,128)(2,1)} %bitcast.8), calls=%async_computation.1 | async-start | bytes 540672 | tf_op jit(solution)/shard_map/all_to_all | solution.py:238
  51.4 0.0 copy-start
  51.4 0.7 %copy-done = f32[9,9]{1,0:T(8,128)S(1)} copy-done((f32[9,9]{1,0:T(8,128)S(1)}, f32[9,9]{1,0:T(8,128)}, u32[]{:S(2)}) %copy-start) | copy-done | bytes 348
  52.1 0.7 %band.1 = (f32[72,144]{1,0:T(8,128)S(1)}, f32[8,128]{1,0:T(8,128)S(1)}) custom-call(s32[1]{0:T(128)} %bitcast.parity_ref, f32[9,9]{1,0:T(8,128)S(1)} %copy-done), custom_call_target="tpu_custom_call" | custom-call | tf_op jit(solution)/shard_map/band/pallas_call | solution.py:240
  52.8 4.6 %all-to-all-done.1 = bf16[4,8,4224]{2,1,0:T(8,128)(2,1)S(1)} async-done(((bf16[4,8,4224]{2,1,0:T(8,128)(2,1)}), bf16[4,8,4224]{2,1,0:T(8,128)(2,1)S(1)}, u32[]{:S(2)}, u32[]{:S(2)}) %all-to-all-start.1) | async-done | bytes 270368 | tf_op jit(solution)/shard_map/all_to_all | solution.py:238
  57.5 0.1 far.1
  57.6 5.4 %collective-permute-start.1 = (bf16[4,4224]{1,0:T(4,128)(2,1)S(1)}, bf16[4,4224]{1,0:T(4,128)(2,1)S(1)}, u32[]{:S(2)}, u32[]{:S(2)}) collective-permute-start(bf16[4,4224]{1,0:T(4,128)(2,1)S(1)} %far.1), channel_id=1, source_target_pairs={{1,2},{3,4},{5,6},{7,8},{9,10},{11,12},{13,14},{15,16},{17,18},{19... | collective-permute-start | bytes 101384 | tf_op jit(solution)/shard_map/ppermute | solution.py:267
  63.0 1.9 %collective-permute-start = (bf16[4,4224]{1,0:T(4,128)(2,1)S(1)}, bf16[4,4224]{1,0:T(4,128)(2,1)S(1)}, u32[]{:S(2)}, u32[]{:S(2)}) collective-permute-start(bf16[4,4224]{1,0:T(4,128)(2,1)S(1)} %near.1), channel_id=1, source_target_pairs={{0,1},{1,0},{2,3},{3,2},{4,5},{5,4},{6,7},{7,6},{8,9},{9,8},{10,11... | collective-permute-start | bytes 101384 | tf_op jit(solution)/shard_map/ppermute | solution.py:268
  64.9 0.0 collective-permute-done.1.far_ref
  65.0 1.2 %collective-permute-done.near_ref = bf16[4,4224]{1,0:T(4,128)(2,1)S(1)} collective-permute-done((bf16[4,4224]{1,0:T(4,128)(2,1)S(1)}, bf16[4,4224]{1,0:T(4,128)(2,1)S(1)}, u32[]{:S(2)}, u32[]{:S(2)}) %collective-permute-start) | collective-permute-done | bytes 33824 | tf_op jit(solution)/shard_map/ppermute | solution.py:268
  66.1 1.2 %smooth.1 = f32[8,4096]{1,0:T(8,128)} custom-call(f32[72,144]{1,0:T(8,128)S(1)} %get-tuple-element.12.band_ref, bf16[32,4224]{1,0:T(8,128)(2,1)S(1)} %bitcast.13, bf16[4,4224]{1,0:T(4,128)(2,1)S(1)} %collective-permute-done.near_ref, bf16[4,4224]{1,0:T(4,128)(2,1)S(1)} %collective-permute-done.1.far_ref), custom_call_target="tpu_custom_call" | custom-call | tf_op jit(solution)/shard_map/smooth/pallas_call | solution.py:269
  (1 shorter events, 0.0 us)
Async XLA Ops:
  47.4 10.1 %all-to-all-start.1 = ((bf16[4,8,4224]{2,1,0:T(8,128)(2,1)}), bf16[4,8,4224]{2,1,0:T(8,128)(2,1)S(1)}, u32[]{:S(2)}, u32[]{:S(2)}) async-start(bf16[4,8,4224]{2,1,0:T(8,128)(2,1)} %bitcast.8), calls=%async_computation.1 | async-start | bytes 540672 | tf_op jit(solution)/shard_map/all_to_all | solution.py:238
  51.4 0.7 %copy-start = (f32[9,9]{1,0:T(8,128)S(1)}, f32[9,9]{1,0:T(8,128)}, u32[]{:S(2)}) copy-start(f32[9,9]{1,0:T(8,128)} %kernel_ref) | copy-start | bytes 976
  57.6 7.4 %collective-permute-start.1 = (bf16[4,4224]{1,0:T(4,128)(2,1)S(1)}, bf16[4,4224]{1,0:T(4,128)(2,1)S(1)}, u32[]{:S(2)}, u32[]{:S(2)}) collective-permute-start(bf16[4,4224]{1,0:T(4,128)(2,1)S(1)} %far.1), channel_id=1, source_target_pairs={{1,2},{3,4},{5,6},{7,8},{9,10},{11,12},{13,14},{15,16},{17,18},{19... | collective-permute-start | bytes 101384 | tf_op jit(solution)/shard_map/ppermute | solution.py:267
  63.0 3.1 %collective-permute-start = (bf16[4,4224]{1,0:T(4,128)(2,1)S(1)}, bf16[4,4224]{1,0:T(4,128)(2,1)S(1)}, u32[]{:S(2)}, u32[]{:S(2)}) collective-permute-start(bf16[4,4224]{1,0:T(4,128)(2,1)S(1)} %near.1), channel_id=1, source_target_pairs={{0,1},{1,0},{2,3},{3,2},{4,5},{5,4},{6,7},{7,6},{8,9},{9,8},{10,11... | collective-permute-start | bytes 101384 | tf_op jit(solution)/shard_map/ppermute | solution.py:268

commit v4 on v3

--- a/solution.py
+++ b/solution.py
@@ -13,11 +13,12 @@
 LANES = 128
 HALO = 4
 TAPS = 2 * HALO + 1
-PARTS = 32
+PARTS = 40
 TERM = 48
 SPAN = 256
 CELLS = STRIP * W // SPAN
 ROWS = 96
+OWN_ROWS = 96
 
 
 def vmem_spec():
@@ -74,25 +75,10 @@
     out_ref[pl.ds(5, pairs, stride=6), :] = masses[2]
 
 
-def bin_kernel(points_ref, out_ref, first_ref, second_ref, mass_ref, acc_ref):
-    sources = points_ref.shape[0] // 3
-    half = sources // 2
-    low = lax.broadcasted_iota(jnp.int32, (half, LANES), 1) < 64
-    upper = points_ref[pl.ds(1, half, stride=3), :]
-    lower = points_ref[pl.ds(1 + 3 * half, half, stride=3), :]
-    mixed_ids = jnp.where(low, upper, pltpu.roll(lower, 64, 1))
-    mixed_masses = jnp.where(low, pltpu.roll(upper, 64, 1), lower)
-    for ids, masses, at in (
-        (points_ref[pl.ds(0, sources, stride=3), :], points_ref[pl.ds(2, sources, stride=3), :], 0),
-        (mixed_ids, mixed_masses, sources),
-    ):
-        ids = ids.astype(jnp.int32)
-        here = pl.ds(at, ids.shape[0])
-        first_ref[here, :] = ((ids >> 8) - 256).astype(jnp.float32)
-        second_ref[here, :] = (ids & 255).astype(jnp.float32)
-        mass_ref[here, :] = masses
+def one_hot_sum(acc_ref, first_ref, second_ref, mass_ref, rows):
+    cells = acc_ref.shape[0]
     first_iota = (
-        lax.broadcasted_iota(jnp.int32, (CELLS, LANES), 0).astype(jnp.float32) - 256.0
+        lax.broadcasted_iota(jnp.int32, (cells, LANES), 0).astype(jnp.float32) - 256.0
     ).astype(jnp.bfloat16)
     second_iota = lax.broadcasted_iota(jnp.int32, (SPAN, LANES), 0).astype(jnp.float32).astype(jnp.bfloat16)
     one = jnp.ones((), jnp.bfloat16)
@@ -100,12 +86,12 @@
     acc_ref[...] = jnp.zeros_like(acc_ref)
 
     def step(i, carry):
-        here = pl.ds(pl.multiple_of(i * ROWS, ROWS), ROWS)
+        here = pl.ds(pl.multiple_of(i * rows, rows), rows)
         first = first_ref[here, :].astype(jnp.bfloat16)
         second = second_ref[here, :].astype(jnp.bfloat16)
         mass = mass_ref[here, :].astype(jnp.bfloat16)
         left, right = [], []
-        for r in range(ROWS):
+        for r in range(rows):
             left.append(jnp.where(first_iota == first[r : r + 1], one, zero))
             right.append(jnp.where(second_iota == second[r : r + 1], mass[r : r + 1], zero))
         acc_ref[...] += lax.dot_general(
@@ -116,23 +102,64 @@
         )
         return carry
 
-    lax.fori_loop(0, first_ref.shape[0] // ROWS, step, 0)
-    width = out_ref.shape[1]
+    lax.fori_loop(0, first_ref.shape[0] // rows, step, 0)
+
+
+def store_strip(out_ref, rows, acc_ref, at, before, after):
+    span = out_ref.shape[1] - LANES
+    for c in range(span // SPAN):
+        block = acc_ref[at + c * STRIP : at + (c + 1) * STRIP, :]
+        out_ref[rows, c * SPAN : (c + 1) * SPAN] = block.astype(jnp.bfloat16)
+    low = lax.broadcasted_iota(jnp.int32, (STRIP, LANES), 1) < 64
+    out_ref[rows, span:] = jnp.where(low, after, before).astype(jnp.bfloat16)
+
+
+def others_kernel(points_ref, out_ref, side_ref, first_ref, second_ref, mass_ref, acc_ref):
     quarters = out_ref.shape[0] // STRIP
-    span = width - LANES
-    groups = span // SPAN
-    low8 = lax.broadcasted_iota(jnp.int32, (STRIP, LANES), 1) < 64
+    here = lax.axis_index("grp")
+    share = CELLS // quarters
+    sources = points_ref.shape[0] // 3
+    half = sources // 2
+    low = lax.broadcasted_iota(jnp.int32, (half, LANES), 1) < 64
+    upper = points_ref[pl.ds(1, half, stride=3), :]
+    lower = points_ref[pl.ds(1 + 3 * half, half, stride=3), :]
+    mixed_ids = jnp.where(low, upper, pltpu.roll(lower, 64, 1))
+    mixed_masses = jnp.where(low, pltpu.roll(upper, 64, 1), lower)
+    origin = (here + 1) * share - STRIP
+    for ids, masses, at in (
+        (points_ref[pl.ds(0, sources, stride=3), :], points_ref[pl.ds(2, sources, stride=3), :], 0),
+        (mixed_ids, mixed_masses, sources),
+    ):
+        ids = ids.astype(jnp.int32)
+        rows = pl.ds(at, ids.shape[0])
+        first = ((ids >> 8) - origin) & (CELLS - 1)
+        first_ref[rows, :] = (first - 256).astype(jnp.float32)
+        second_ref[rows, :] = (ids & 255).astype(jnp.float32)
+        mass_ref[rows, :] = masses
+    one_hot_sum(acc_ref, first_ref, second_ref, mass_ref, ROWS)
     blank = jnp.zeros((STRIP, LANES), jnp.float32)
-    for q in range(quarters):
-        rows = pl.ds(q * STRIP, STRIP)
-        for c in range(groups):
-            at = (q * groups + c) * STRIP
-            out_ref[rows, c * SPAN : (c + 1) * SPAN] = acc_ref[at : at + STRIP, :].astype(jnp.bfloat16)
-        at = q * groups * STRIP
-        before = acc_ref[at - STRIP : at, LANES:] if q else blank
-        at += groups * STRIP
-        after = acc_ref[at : at + STRIP, :LANES] if q < quarters - 1 else blank
-        out_ref[rows, span:] = jnp.where(low8, after, before).astype(jnp.bfloat16)
+    for r in range(1, quarters):
+        quarter = (here + r) & (quarters - 1)
+        at = STRIP + (r - 1) * share
+        before = jnp.where(quarter == 0, blank, acc_ref[at - STRIP : at, LANES:])
+        after = jnp.where(quarter == quarters - 1, blank, acc_ref[at + share : at + share + STRIP, :LANES])
+        rows = pl.ds(pl.multiple_of(quarter * STRIP, STRIP), STRIP)
+        store_strip(out_ref, rows, acc_ref, at, before, after)
+    out_ref[pl.ds(pl.multiple_of(here * STRIP, STRIP), STRIP), :] = jnp.zeros(
+        (STRIP, out_ref.shape[1]), jnp.bfloat16
+    )
+    last = STRIP + (quarters - 1) * share
+    side_ref[:STRIP, :] = jnp.where(here == 0, blank, acc_ref[last - STRIP : last, LANES:])
+    side_ref[STRIP:, :] = jnp.where(here == quarters - 1, blank, acc_ref[STRIP : 2 * STRIP, :LANES])
+
+
+def own_kernel(first_ref, second_ref, mass_ref, side_ref, out_ref, moved_ref, acc_ref):
+    moved = first_ref[...] + float(acc_ref.shape[0] - STRIP)
+    moved_ref[...] = jnp.where(moved < CELLS // 2, moved, moved - CELLS)
+    one_hot_sum(acc_ref, moved_ref, second_ref, mass_ref, OWN_ROWS)
+    before = side_ref[:STRIP, :]
+    after = side_ref[STRIP:, :]
+    store_strip(out_ref, pl.ds(0, STRIP), acc_ref, 0, before, after)
 
 
 def band_kernel(parity_ref, kernel_ref, band_ref, odd_ref):
@@ -147,7 +174,7 @@
     framed = jnp.where(
         source < PARTS,
         HALO + source % STRIP,
-        jnp.where(source < PARTS + HALO, near, jnp.where(source < PARTS + 2 * HALO, far, -STRIP)),
+        jnp.where(source < PARTS + HALO, near, far),
     )
     tap = framed - row
     for b in range(TAPS):
@@ -162,23 +189,22 @@
     odd_ref[...] = jnp.broadcast_to(parity.astype(jnp.float32), odd_ref.shape)
 
 
-def edge_kernel(odd_ref, parts_ref, edge_ref, *, top_if_odd):
+def edge_kernel(odd_ref, parts_ref, own_ref, edge_ref, *, top_if_odd):
     is_top = (odd_ref[:HALO, :] > 0.5) == top_if_odd
     for t in range(parts_ref.shape[1] // LANES):
         here = slice(t * LANES, (t + 1) * LANES)
-        total = parts_ref[:STRIP, here].astype(jnp.float32)
-        for g in range(1, parts_ref.shape[0] // STRIP):
+        total = own_ref[:, here].astype(jnp.float32)
+        for g in range(parts_ref.shape[0] // STRIP):
             total = total + parts_ref[g * STRIP : (g + 1) * STRIP, here].astype(jnp.float32)
         edge_ref[:, here] = jnp.where(is_top, total[:HALO], total[HALO:]).astype(jnp.bfloat16)
 
 
-def smooth_kernel(band_ref, parts_ref, near_ref, far_ref, out_ref):
+def smooth_kernel(band_ref, parts_ref, own_ref, near_ref, far_ref, out_ref):
     width = parts_ref.shape[1]
     near = near_ref[...].astype(jnp.float32)
     far = far_ref[...].astype(jnp.float32)
-    blank = jnp.zeros((STRIP, width), jnp.float32)
-    halo = jnp.concatenate([near, far, blank], axis=0).astype(jnp.bfloat16)
-    frame = jnp.concatenate([parts_ref[...], halo], axis=0)
+    rest = jnp.concatenate([own_ref[...].astype(jnp.float32), near, far], axis=0)
+    frame = jnp.concatenate([parts_ref[...], rest.astype(jnp.bfloat16)], axis=0)
     frame = jnp.concatenate([frame, frame, frame], axis=0)
     shifted = jnp.dot(band_ref[...].astype(jnp.bfloat16), frame, preferred_element_type=jnp.float32)
     total = shifted[HALO * STRIP : (HALO + 1) * STRIP]
@@ -224,18 +250,37 @@
     arrived = lax.all_to_all(
         packed.reshape(3 * owners, 1, LANES), "own", split_axis=0, concat_axis=0, tiled=True
     ).reshape(3 * owners, LANES)
-    parts = pl.pallas_call(
-        bin_kernel,
-        out_shape=jax.ShapeDtypeStruct((groups * STRIP, width), jnp.bfloat16),
+    plane = jax.ShapeDtypeStruct((points, LANES), jnp.float32)
+    sent, side, first, second, mass = pl.pallas_call(
+        others_kernel,
+        out_shape=(
+            jax.ShapeDtypeStruct((groups * STRIP, width), jnp.bfloat16),
+            jax.ShapeDtypeStruct((2 * STRIP, LANES), jnp.float32),
+            plane,
+            plane,
+            plane,
+        ),
         in_specs=[vmem_spec()],
+        out_specs=(vmem_spec(),) * 5,
+        scratch_shapes=[pltpu.VMEM((CELLS - CELLS // groups + 2 * STRIP, SPAN), jnp.float32)],
+        compiler_params=limit(32),
+        name="others",
+    )(arrived)
+    sent, kernel = lax.optimization_barrier((sent, kernel))
+    parts = lax.all_to_all(sent, "grp", split_axis=0, concat_axis=0, tiled=True)
+    own = pl.pallas_call(
+        own_kernel,
+        out_shape=jax.ShapeDtypeStruct((STRIP, width), jnp.bfloat16),
+        in_specs=[vmem_spec()] * 4,
         out_specs=vmem_spec(),
-        scratch_shapes=[pltpu.VMEM((points, LANES), jnp.float32)] * 3
-        + [pltpu.VMEM((CELLS, SPAN), jnp.float32)],
+        scratch_shapes=[
+            pltpu.VMEM((points, LANES), jnp.float32),
+            pltpu.VMEM((CELLS // groups, SPAN), jnp.float32),
+        ],
         compiler_params=limit(32),
-        name="bin",
-    )(arrived)
-    sent, kernel = lax.optimization_barrier((parts, kernel))
-    parts = lax.all_to_all(sent, "grp", split_axis=0, concat_axis=0, tiled=True)
+        cost_estimate=pl.CostEstimate(flops=2 * points * LANES * W * STRIP // groups, bytes_accessed=2**19, transcendentals=0),
+        name="own",
+    )(first, second, mass, side)
     parity = (lax.axis_index("own") & 1).reshape(1).astype(jnp.int32)
     band, odd = pl.pallas_call(
         band_kernel,
@@ -252,11 +297,11 @@
         return pl.pallas_call(
             functools.partial(edge_kernel, top_if_odd=top_if_odd),
             out_shape=jax.ShapeDtypeStruct((HALO, width), jnp.bfloat16),
-            in_specs=[vmem_spec()] * 2,
+            in_specs=[vmem_spec()] * 3,
             out_specs=vmem_spec(),
             compiler_params=limit(4),
             name=name,
-        )(odd, parts)
+        )(odd, parts, own)
 
     near = edge(parts, True, "near")
     near, later = lax.optimization_barrier((near, parts))
@@ -269,11 +314,11 @@
     return pl.pallas_call(
         smooth_kernel,
         out_shape=jax.ShapeDtypeStruct((STRIP, quarter), jnp.float32),
-        in_specs=[vmem_spec()] * 4,
+        in_specs=[vmem_spec()] * 5,
         out_specs=vmem_spec(),
         compiler_params=limit(16),
         name="smooth",
-    )(band, parts, near, far)
+    )(band, parts, own, near, far)
 
 
 def solution(mesh):

time: 68.1 us -> 66.7 us (0.979)
  waiting for transfers between devices: 5.77 us -> 1.43 us
  Pallas kernels: 11 us -> 13.9 us
    all_to_all x1, waiting for transfers between devices: 4.61 us -> 0.26 us  [per_device(): parts = lax.all_to_all(sent, 'grp', split_axis=0, concat_axis=0, tiled=True)]
    pallas_call x1 -> x2, Pallas kernels: 7.73 us -> 10.6 us  [the longest x1 6.31 us: per_device(): pl.pallas_call(others_kernel, out_shape=(jax.ShapeDtypeStruct((groups * S...]
  transfers between devices with their start and end apart: 3 -> 3, of which waited for: 2 -> 2; matrix products, arithmetic and copies ran while one was open for 0% -> 0% of each run, Pallas kernels for 1% -> 8%
where the time goes in v4:
time: 66.7 us; the launch traced here: 65.9 us
  blocking collectives  38.4 us (58%)
  Pallas kernels  13.9 us (21%)
  starting transfers between devices  11.4 us (17%)
  waiting for transfers between devices  1.43 us (2%)
  local copies, waits for them, and re-layouts  0.7 us (1%)
    all_to_all x1, blocking collectives, per_device(): lax.all_to_all(packed.reshape(3 * owners, 1, LANES), 'own', split_axis=0,...  38.4 us
    pallas_call x1, Pallas kernels, per_device(): pl.pallas_call(others_kernel, out_shape=(jax.ShapeDtypeStruct((groups * S...  6.31 us
    ppermute x1, starting transfers between devices, per_device(): far = lax.ppermute(far, 'own', across)  5.46 us
    pallas_call x1, Pallas kernels, per_device(): pl.pallas_call(own_kernel, out_shape=jax.ShapeDtypeStruct((STRIP, width),...  4.34 us
    all_to_all x1, starting transfers between devices, per_device(): parts = lax.all_to_all(sent, 'grp', split_axis=0, concat_axis=0, tiled=True)  4.01 us
    ppermute x1, starting transfers between devices, per_device(): near = lax.ppermute(near, 'own', on_chip)  1.92 us
  transfers between devices with their start and end apart: 3, of which 2 were waited for; matrix products, arithmetic and copies ran while one was open for 0% of the time, Pallas kernels for 8%

profile of v4, /device:TPU:25, one launch (start us, length us, event | category | flops | bytes accessed | tf_op | source)
XLA Modules:
  0.0 65.9 jit_solution(16720186717099483395)
XLA Ops:
  0.0 1.2 %pack.1 = f32[384,128]{1,0:T(8,128)S(1)} custom-call(s32[192,128]{1,0:T(8,128)} %bitcast.16, s32[192,128]{1,0:T(8,128)} %bitcast.17, bf16[192,1,128]{2,1,0:T(2,128)(2,1)} %bitcast.18, s32[1,128]{1,0:T(1,128)} %bitcast.19), custom_call_target="tpu_custom_call" | custom-call | tf_op jit(solution)/shard_map/pack/pallas_call | solution.py:224
  1.2 38.4 %all_to_all.16 = f32[384,1,128]{2,1,0:T(1,128)S(1)} all-to-all(f32[384,1,128]{2,1,0:T(1,128)S(1)} %bitcast.15), channel_id=1, replica_groups=mesh['grp'=4,'own'=128] {'own'}, dimensions={0} | all-to-all | bytes 393216 | tf_op jit(solution)/shard_map/all_to_all | solution.py:250
  39.6 6.3 %others.1 = (bf16[32,4224]{1,0:T(8,128)(2,1)}, f32[16,128]{1,0:T(8,128)S(1)}, f32[192,128]{1,0:T(8,128)S(1)}, f32[192,128]{1,0:T(8,128)S(1)}, f32[192,128]{1,0:T(8,128)S(1)}) custom-call(f32[384,128]{1,0:T(8,128)S(1)} %bitcast.14), custom_call_target="tpu_custom_call" | custom-call | tf_op jit(solution)/shard_map/others/pallas_call | solution.py:254
  46.0 4.0 %all-to-all-start.1 = ((bf16[4,8,4224]{2,1,0:T(8,128)(2,1)}), bf16[4,8,4224]{2,1,0:T(8,128)(2,1)S(1)}, u32[]{:S(2)}, u32[]{:S(2)}) async-start(bf16[4,8,4224]{2,1,0:T(8,128)(2,1)} %bitcast.8), calls=%async_computation.1 | async-start | bytes 540672 | tf_op jit(solution)/shard_map/all_to_all | solution.py:270
  50.0 0.0 copy-start
  50.0 0.7 %copy-done = f32[9,9]{1,0:T(8,128)S(1)} copy-done((f32[9,9]{1,0:T(8,128)S(1)}, f32[9,9]{1,0:T(8,128)}, u32[]{:S(2)}) %copy-start) | copy-done | bytes 348
  50.7 0.7 %band.1 = (f32[72,144]{1,0:T(8,128)S(1)}, f32[8,128]{1,0:T(8,128)S(1)}) custom-call(s32[1]{0:T(128)} %bitcast.parity_ref, f32[9,9]{1,0:T(8,128)S(1)} %copy-done), custom_call_target="tpu_custom_call" | custom-call | tf_op jit(solution)/shard_map/band/pallas_call | solution.py:285
  51.4 4.3 %own.1.own_ref = bf16[8,4224]{1,0:T(8,128)(2,1)S(1)} custom-call(f32[192,128]{1,0:T(8,128)S(1)} %get-tuple-element.20.first_ref, f32[192,128]{1,0:T(8,128)S(1)} %get-tuple-element.21.second_ref, f32[192,128]{1,0:T(8,128)S(1)} %get-tuple-element.22.mass_ref, f32[16,128]{1,0:T(8,128)S(1)} %get-tuple-element.23.side_ref), custom_call_target="tpu_custom_call" | custom-call | flops 1610612736 | bytes 524288 | tf_op jit(solution)/shard_map/own/pallas_call | solution.py:271
  55.8 0.3 all-to-all-done.1
  56.0 0.1 near.1
  56.1 0.1 far.1
  56.1 5.5 %collective-permute-start.1 = (bf16[4,4224]{1,0:T(4,128)(2,1)S(1)}, bf16[4,4224]{1,0:T(4,128)(2,1)S(1)}, u32[]{:S(2)}, u32[]{:S(2)}) collective-permute-start(bf16[4,4224]{1,0:T(4,128)(2,1)S(1)} %far.1), channel_id=1, source_target_pairs={{1,2},{3,4},{5,6},{7,8},{9,10},{11,12},{13,14},{15,16},{17,18},{19... | collective-permute-start | bytes 101384 | tf_op jit(solution)/shard_map/ppermute | solution.py:312
  61.6 1.9 %collective-permute-start = (bf16[4,4224]{1,0:T(4,128)(2,1)S(1)}, bf16[4,4224]{1,0:T(4,128)(2,1)S(1)}, u32[]{:S(2)}, u32[]{:S(2)}) collective-permute-start(bf16[4,4224]{1,0:T(4,128)(2,1)S(1)} %near.1), channel_id=1, source_target_pairs={{0,1},{1,0},{2,3},{3,2},{4,5},{5,4},{6,7},{7,6},{8,9},{9,8},{10,11... | collective-permute-start | bytes 101384 | tf_op jit(solution)/shard_map/ppermute | solution.py:313
  63.5 0.0 collective-permute-done.1.far_ref
  63.6 1.2 %collective-permute-done.near_ref = bf16[4,4224]{1,0:T(4,128)(2,1)S(1)} collective-permute-done((bf16[4,4224]{1,0:T(4,128)(2,1)S(1)}, bf16[4,4224]{1,0:T(4,128)(2,1)S(1)}, u32[]{:S(2)}, u32[]{:S(2)}) %collective-permute-start) | collective-permute-done | bytes 33824 | tf_op jit(solution)/shard_map/ppermute | solution.py:313
  64.7 1.2 %smooth.1 = f32[8,4096]{1,0:T(8,128)} custom-call(f32[72,144]{1,0:T(8,128)S(1)} %get-tuple-element.18.band_ref, bf16[32,4224]{1,0:T(8,128)(2,1)S(1)} %bitcast.13, bf16[8,4224]{1,0:T(8,128)(2,1)S(1)} %own.1.own_ref, bf16[4,4224]{1,0:T(4,128)(2,1)S(1)} %collective-permute-done.near_ref, bf16[4,4224]{1,0:T(4,128)(2,1)S(1)} %collective-permute-done.1.far_ref), custom_call_target="tpu_custom_call" | custom-call | tf_op jit(solution)/shard_map/smooth/pallas_call | solution.py:314
Async XLA Ops:
  46.0 10.1 %all-to-all-start.1 = ((bf16[4,8,4224]{2,1,0:T(8,128)(2,1)}), bf16[4,8,4224]{2,1,0:T(8,128)(2,1)S(1)}, u32[]{:S(2)}, u32[]{:S(2)}) async-start(bf16[4,8,4224]{2,1,0:T(8,128)(2,1)} %bitcast.8), calls=%async_computation.1 | async-start | bytes 540672 | tf_op jit(solution)/shard_map/all_to_all | solution.py:270
  50.0 0.7 %copy-start = (f32[9,9]{1,0:T(8,128)S(1)}, f32[9,9]{1,0:T(8,128)}, u32[]{:S(2)}) copy-start(f32[9,9]{1,0:T(8,128)} %kernel_ref) | copy-start | bytes 976
  56.1 7.4 %collective-permute-start.1 = (bf16[4,4224]{1,0:T(4,128)(2,1)S(1)}, bf16[4,4224]{1,0:T(4,128)(2,1)S(1)}, u32[]{:S(2)}, u32[]{:S(2)}) collective-permute-start(bf16[4,4224]{1,0:T(4,128)(2,1)S(1)} %far.1), channel_id=1, source_target_pairs={{1,2},{3,4},{5,6},{7,8},{9,10},{11,12},{13,14},{15,16},{17,18},{19... | collective-permute-start | bytes 101384 | tf_op jit(solution)/shard_map/ppermute | solution.py:312
  61.6 3.1 %collective-permute-start = (bf16[4,4224]{1,0:T(4,128)(2,1)S(1)}, bf16[4,4224]{1,0:T(4,128)(2,1)S(1)}, u32[]{:S(2)}, u32[]{:S(2)}) collective-permute-start(bf16[4,4224]{1,0:T(4,128)(2,1)S(1)} %near.1), channel_id=1, source_target_pairs={{0,1},{1,0},{2,3},{3,2},{4,5},{5,4},{6,7},{7,6},{8,9},{9,8},{10,11... | collective-permute-start | bytes 101384 | tf_op jit(solution)/shard_map/ppermute | solution.py:313

commit v5 on v4

--- a/solution.py
+++ b/solution.py
@@ -247,9 +247,23 @@
             )
         )
     )
+    packed, kernel = lax.optimization_barrier((packed, kernel))
     arrived = lax.all_to_all(
         packed.reshape(3 * owners, 1, LANES), "own", split_axis=0, concat_axis=0, tiled=True
     ).reshape(3 * owners, LANES)
+    parity = (lax.axis_index("own") & 1).reshape(1).astype(jnp.int32)
+    band, odd = pl.pallas_call(
+        band_kernel,
+        out_shape=(
+            jax.ShapeDtypeStruct((TAPS * STRIP, 3 * TERM), jnp.float32),
+            jax.ShapeDtypeStruct((STRIP, LANES), jnp.float32),
+        ),
+        in_specs=[smem_spec(), smem_spec()],
+        out_specs=(vmem_spec(),) * 2,
+        compiler_params=limit(4),
+        name="band",
+    )(parity, kernel)
+    arrived, band, odd = lax.optimization_barrier((arrived, band, odd))
     plane = jax.ShapeDtypeStruct((points, LANES), jnp.float32)
     sent, side, first, second, mass = pl.pallas_call(
         others_kernel,
@@ -266,7 +280,6 @@
         compiler_params=limit(32),
         name="others",
     )(arrived)
-    sent, kernel = lax.optimization_barrier((sent, kernel))
     parts = lax.all_to_all(sent, "grp", split_axis=0, concat_axis=0, tiled=True)
     own = pl.pallas_call(
         own_kernel,
@@ -281,18 +294,6 @@
         cost_estimate=pl.CostEstimate(flops=2 * points * LANES * W * STRIP // groups, bytes_accessed=2**19, transcendentals=0),
         name="own",
     )(first, second, mass, side)
-    parity = (lax.axis_index("own") & 1).reshape(1).astype(jnp.int32)
-    band, odd = pl.pallas_call(
-        band_kernel,
-        out_shape=(
-            jax.ShapeDtypeStruct((TAPS * STRIP, 3 * TERM), jnp.float32),
-            jax.ShapeDtypeStruct((STRIP, LANES), jnp.float32),
-        ),
-        in_specs=[smem_spec(), smem_spec()],
-        out_specs=(vmem_spec(),) * 2,
-        compiler_params=limit(4),
-        name="band",
-    )(parity, kernel)
     def edge(parts, top_if_odd, name):
         return pl.pallas_call(
             functools.partial(edge_kernel, top_if_odd=top_if_odd),

time: 66.7 us -> 67.6 us (1.013)
  blocking collectives: 38.4 us -> 0 us
  starting transfers between devices: 11.4 us -> 31 us
  waiting for transfers between devices: 1.43 us -> 20.4 us
  Pallas kernels: 13.9 us -> 14.6 us
    all_to_all x1 -> x0, blocking collectives: 38.4 us -> none  [per_device(): lax.all_to_all(packed.reshape(3 * owners, 1, LANES), 'own', split_axis=0,...]
    all_to_all x0 -> x1, starting transfers between devices: none -> 19.6 us  [per_device(): lax.all_to_all(packed.reshape(3 * owners, 1, LANES), 'own', split_axis=0,...]
    all_to_all x0 -> x1, waiting for transfers between devices: none -> 17.5 us  [per_device(): lax.all_to_all(packed.reshape(3 * owners, 1, LANES), 'own', split_axis=0,...]
    all_to_all x1, waiting for transfers between devices: 0.26 us -> 1.72 us  [per_device(): parts = lax.all_to_all(sent, 'grp', split_axis=0, concat_axis=0, tiled=True)]
  transfers between devices with their start and end apart: 3 -> 4, of which waited for: 2 -> 3; matrix products, arithmetic and copies ran while one was open for 0% -> 0% of each run, Pallas kernels for 8% -> 8%
where the time goes in v5:
time: 67.6 us; the launch traced here: 66.7 us
  starting transfers between devices  31 us (46%)
  waiting for transfers between devices  20.4 us (30%)
  Pallas kernels  14.6 us (22%)
  local copies, waits for them, and re-layouts  0.69 us (1%)
    all_to_all x1, starting transfers between devices, per_device(): lax.all_to_all(packed.reshape(3 * owners, 1, LANES), 'own', split_axis=0,...  19.6 us
    all_to_all x1, waiting for transfers between devices, per_device(): lax.all_to_all(packed.reshape(3 * owners, 1, LANES), 'own', split_axis=0,...  17.5 us
    pallas_call x1, Pallas kernels, per_device(): pl.pallas_call(others_kernel, out_shape=(jax.ShapeDtypeStruct((groups * S...  6.29 us
    ppermute x1, starting transfers between devices, per_device(): far = lax.ppermute(far, 'own', across)  5.42 us
    pallas_call x1, Pallas kernels, per_device(): pl.pallas_call(own_kernel, out_shape=jax.ShapeDtypeStruct((STRIP, width),...  4.33 us
    all_to_all x1, starting transfers between devices, per_device(): parts = lax.all_to_all(sent, 'grp', split_axis=0, concat_axis=0, tiled=True)  4.02 us
    ppermute x1, starting transfers between devices, per_device(): near = lax.ppermute(near, 'own', on_chip)  1.92 us
    pallas_call x1, Pallas kernels, per_device(): pl.pallas_call(pack_kernel, out_shape=jax.ShapeDtypeStruct((3 * owners, L...  1.89 us
  transfers between devices with their start and end apart: 4, of which 3 were waited for; matrix products, arithmetic and copies ran while one was open for 0% of the time, Pallas kernels for 8%

profile of v5, /device:TPU:25, one launch (start us, length us, event | category | flops | bytes accessed | tf_op | source)
XLA Modules:
  0.0 66.7 jit_solution(6727820709708365325)
XLA Ops:
  0.0 1.9 %pack.1 = f32[384,128]{1,0:T(8,128)} custom-call(s32[192,128]{1,0:T(8,128)} %bitcast.15, s32[192,128]{1,0:T(8,128)} %bitcast.16, bf16[192,1,128]{2,1,0:T(2,128)(2,1)} %bitcast.17, s32[1,128]{1,0:T(1,128)} %bitcast.18), custom_call_target="tpu_custom_call" | custom-call | tf_op jit(solution)/shard_map/pack/pallas_call | solution.py:224
  1.9 19.6 %all-to-all-start = ((f32[384,1,128]{2,1,0:T(1,128)}), f32[384,1,128]{2,1,0:T(1,128)S(1)}, u32[]{:S(2)}, u32[]{:S(2)}) async-start(f32[384,1,128]{2,1,0:T(1,128)} %bitcast.5), calls=%async_computation | async-start | bytes 393216 | tf_op jit(solution)/shard_map/all_to_all | solution.py:251
  21.5 0.0 copy-start
  21.5 0.7 %copy-done = f32[9,9]{1,0:T(8,128)S(1)} copy-done((f32[9,9]{1,0:T(8,128)S(1)}, f32[9,9]{1,0:T(8,128)}, u32[]{:S(2)}) %copy-start) | copy-done | bytes 348
  22.2 0.7 %band.1 = (f32[72,144]{1,0:T(8,128)S(1)}, f32[8,128]{1,0:T(8,128)S(1)}) custom-call(s32[1]{0:T(128)} %bitcast.7.parity_ref, f32[9,9]{1,0:T(8,128)S(1)} %copy-done), custom_call_target="tpu_custom_call" | custom-call | tf_op jit(solution)/shard_map/band/pallas_call | solution.py:255
  23.0 17.5 %all-to-all-done = f32[384,1,128]{2,1,0:T(1,128)S(1)} async-done(((f32[384,1,128]{2,1,0:T(1,128)}), f32[384,1,128]{2,1,0:T(1,128)S(1)}, u32[]{:S(2)}, u32[]{:S(2)}) %all-to-all-start) | async-done | bytes 196640 | tf_op jit(solution)/shard_map/all_to_all | solution.py:251
  40.5 6.3 %others.1 = (bf16[32,4224]{1,0:T(8,128)(2,1)}, f32[16,128]{1,0:T(8,128)S(1)}, f32[192,128]{1,0:T(8,128)S(1)}, f32[192,128]{1,0:T(8,128)S(1)}, f32[192,128]{1,0:T(8,128)S(1)}) custom-call(f32[384,128]{1,0:T(8,128)S(1)} %bitcast.14), custom_call_target="tpu_custom_call" | custom-call | tf_op jit(solution)/shard_map/others/pallas_call | solution.py:268
  46.8 4.0 %all-to-all-start.1 = ((bf16[4,8,4224]{2,1,0:T(8,128)(2,1)}), bf16[4,8,4224]{2,1,0:T(8,128)(2,1)S(1)}, u32[]{:S(2)}, u32[]{:S(2)}) async-start(bf16[4,8,4224]{2,1,0:T(8,128)(2,1)} %bitcast.8), calls=%async_computation.1 | async-start | bytes 540672 | tf_op jit(solution)/shard_map/all_to_all | solution.py:283
  50.8 4.3 %own.1.own_ref = bf16[8,4224]{1,0:T(8,128)(2,1)S(1)} custom-call(f32[192,128]{1,0:T(8,128)S(1)} %get-tuple-element.26.first_ref, f32[192,128]{1,0:T(8,128)S(1)} %get-tuple-element.27.second_ref, f32[192,128]{1,0:T(8,128)S(1)} %get-tuple-element.28.mass_ref, f32[16,128]{1,0:T(8,128)S(1)} %get-tuple-element.29.side_ref), custom_call_target="tpu_custom_call" | custom-call | flops 1610612736 | bytes 524288 | tf_op jit(solution)/shard_map/own/pallas_call | solution.py:284
  55.2 1.7 %all-to-all-done.1 = bf16[4,8,4224]{2,1,0:T(8,128)(2,1)S(1)} async-done(((bf16[4,8,4224]{2,1,0:T(8,128)(2,1)}), bf16[4,8,4224]{2,1,0:T(8,128)(2,1)S(1)}, u32[]{:S(2)}, u32[]{:S(2)}) %all-to-all-start.1) | async-done | bytes 270368 | tf_op jit(solution)/shard_map/all_to_all | solution.py:283
  56.9 0.1 near.1
  57.0 0.1 far.1
  57.0 5.4 %collective-permute-start.1 = (bf16[4,4224]{1,0:T(4,128)(2,1)S(1)}, bf16[4,4224]{1,0:T(4,128)(2,1)S(1)}, u32[]{:S(2)}, u32[]{:S(2)}) collective-permute-start(bf16[4,4224]{1,0:T(4,128)(2,1)S(1)} %far.1), channel_id=1, source_target_pairs={{1,2},{3,4},{5,6},{7,8},{9,10},{11,12},{13,14},{15,16},{17,18},{19... | collective-permute-start | bytes 101384 | tf_op jit(solution)/shard_map/ppermute | solution.py:313
  62.4 1.9 %collective-permute-start = (bf16[4,4224]{1,0:T(4,128)(2,1)S(1)}, bf16[4,4224]{1,0:T(4,128)(2,1)S(1)}, u32[]{:S(2)}, u32[]{:S(2)}) collective-permute-start(bf16[4,4224]{1,0:T(4,128)(2,1)S(1)} %near.1), channel_id=1, source_target_pairs={{0,1},{1,0},{2,3},{3,2},{4,5},{5,4},{6,7},{7,6},{8,9},{9,8},{10,11... | collective-permute-start | bytes 101384 | tf_op jit(solution)/shard_map/ppermute | solution.py:314
  64.4 0.0 collective-permute-done.1.far_ref
  64.4 1.2 %collective-permute-done.near_ref = bf16[4,4224]{1,0:T(4,128)(2,1)S(1)} collective-permute-done((bf16[4,4224]{1,0:T(4,128)(2,1)S(1)}, bf16[4,4224]{1,0:T(4,128)(2,1)S(1)}, u32[]{:S(2)}, u32[]{:S(2)}) %collective-permute-start) | collective-permute-done | bytes 33824 | tf_op jit(solution)/shard_map/ppermute | solution.py:314
  65.6 1.2 %smooth.1 = f32[8,4096]{1,0:T(8,128)} custom-call(f32[72,144]{1,0:T(8,128)S(1)} %get-tuple-element.23.band_ref, bf16[32,4224]{1,0:T(8,128)(2,1)S(1)} %bitcast.13, bf16[8,4224]{1,0:T(8,128)(2,1)S(1)} %own.1.own_ref, bf16[4,4224]{1,0:T(4,128)(2,1)S(1)} %collective-permute-done.near_ref, bf16[4,4224]{1,0:T(4,128)(2,1)S(1)} %collective-permute-done.1.far_ref), custom_call_target="tpu_custom_call" | custom-call | tf_op jit(solution)/shard_map/smooth/pallas_call | solution.py:315
Async XLA Ops:
  1.9 38.6 %all-to-all-start = ((f32[384,1,128]{2,1,0:T(1,128)}), f32[384,1,128]{2,1,0:T(1,128)S(1)}, u32[]{:S(2)}, u32[]{:S(2)}) async-start(f32[384,1,128]{2,1,0:T(1,128)} %bitcast.5), calls=%async_computation | async-start | bytes 393216 | tf_op jit(solution)/shard_map/all_to_all | solution.py:251
  21.5 0.7 %copy-start = (f32[9,9]{1,0:T(8,128)S(1)}, f32[9,9]{1,0:T(8,128)}, u32[]{:S(2)}) copy-start(f32[9,9]{1,0:T(8,128)} %kernel_ref) | copy-start | bytes 976
  46.8 10.1 %all-to-all-start.1 = ((bf16[4,8,4224]{2,1,0:T(8,128)(2,1)}), bf16[4,8,4224]{2,1,0:T(8,128)(2,1)S(1)}, u32[]{:S(2)}, u32[]{:S(2)}) async-start(bf16[4,8,4224]{2,1,0:T(8,128)(2,1)} %bitcast.8), calls=%async_computation.1 | async-start | bytes 540672 | tf_op jit(solution)/shard_map/all_to_all | solution.py:283
  57.0 7.4 %collective-permute-start.1 = (bf16[4,4224]{1,0:T(4,128)(2,1)S(1)}, bf16[4,4224]{1,0:T(4,128)(2,1)S(1)}, u32[]{:S(2)}, u32[]{:S(2)}) collective-permute-start(bf16[4,4224]{1,0:T(4,128)(2,1)S(1)} %far.1), channel_id=1, source_target_pairs={{1,2},{3,4},{5,6},{7,8},{9,10},{11,12},{13,14},{15,16},{17,18},{19... | collective-permute-start | bytes 101384 | tf_op jit(solution)/shard_map/ppermute | solution.py:313
  62.4 3.1 %collective-permute-start = (bf16[4,4224]{1,0:T(4,128)(2,1)S(1)}, bf16[4,4224]{1,0:T(4,128)(2,1)S(1)}, u32[]{:S(2)}, u32[]{:S(2)}) collective-permute-start(bf16[4,4224]{1,0:T(4,128)(2,1)S(1)} %near.1), channel_id=1, source_target_pairs={{0,1},{1,0},{2,3},{3,2},{4,5},{5,4},{6,7},{7,6},{8,9},{9,8},{10,11... | collective-permute-start | bytes 101384 | tf_op jit(solution)/shard_map/ppermute | solution.py:314

commit v6 on v4

--- a/solution.py
+++ b/solution.py
@@ -83,10 +83,9 @@
     second_iota = lax.broadcasted_iota(jnp.int32, (SPAN, LANES), 0).astype(jnp.float32).astype(jnp.bfloat16)
     one = jnp.ones((), jnp.bfloat16)
     zero = jnp.zeros((), jnp.bfloat16)
-    acc_ref[...] = jnp.zeros_like(acc_ref)
-
-    def step(i, carry):
-        here = pl.ds(pl.multiple_of(i * rows, rows), rows)
+
+    def part(i):
+        here = pl.ds(i * rows, rows)
         first = first_ref[here, :].astype(jnp.bfloat16)
         second = second_ref[here, :].astype(jnp.bfloat16)
         mass = mass_ref[here, :].astype(jnp.bfloat16)
@@ -94,15 +93,16 @@
         for r in range(rows):
             left.append(jnp.where(first_iota == first[r : r + 1], one, zero))
             right.append(jnp.where(second_iota == second[r : r + 1], mass[r : r + 1], zero))
-        acc_ref[...] += lax.dot_general(
+        return lax.dot_general(
             jnp.concatenate(left, axis=1),
             jnp.concatenate(right, axis=1),
             (((1,), (1,)), ((), ())),
             preferred_element_type=jnp.float32,
         )
-        return carry
-
-    lax.fori_loop(0, first_ref.shape[0] // rows, step, 0)
+
+    acc_ref[...] = part(0)
+    for i in range(1, first_ref.shape[0] // rows):
+        acc_ref[...] += part(i)
 
 
 def store_strip(out_ref, rows, acc_ref, at, before, after):
@@ -154,7 +154,7 @@
 
 
 def own_kernel(first_ref, second_ref, mass_ref, side_ref, out_ref, moved_ref, acc_ref):
-    moved = first_ref[...] + float(acc_ref.shape[0] - STRIP)
+    moved = first_ref[...] + float(out_ref.shape[1] // SPAN * STRIP - STRIP)
     moved_ref[...] = jnp.where(moved < CELLS // 2, moved, moved - CELLS)
     one_hot_sum(acc_ref, moved_ref, second_ref, mass_ref, OWN_ROWS)
     before = side_ref[:STRIP, :]
@@ -275,7 +275,7 @@
         out_specs=vmem_spec(),
         scratch_shapes=[
             pltpu.VMEM((points, LANES), jnp.float32),
-            pltpu.VMEM((CELLS // groups, SPAN), jnp.float32),
+            pltpu.VMEM((max(CELLS // groups, 256), SPAN), jnp.float32),
         ],
         compiler_params=limit(32),
         cost_estimate=pl.CostEstimate(flops=2 * points * LANES * W * STRIP // groups, bytes_accessed=2**19, transcendentals=0),

time: 66.7 us -> 66.4 us (level)
  Pallas kernels: 13.9 us -> 12.7 us
  waiting for transfers between devices: 1.43 us -> 2.29 us
    pallas_call x1, Pallas kernels: 4.34 us -> 3.47 us  [per_device(): pl.pallas_call(own_kernel, out_shape=jax.ShapeDtypeStruct((STRIP, width),...]
    all_to_all x1, waiting for transfers between devices: 0.26 us -> 1.12 us  [per_device(): parts = lax.all_to_all(sent, 'grp', split_axis=0, concat_axis=0, tiled=True)]
  transfers between devices with their start and end apart: 3 -> 3, of which waited for: 2 -> 2; matrix products, arithmetic and copies ran while one was open for 0% -> 0% of each run, Pallas kernels for 8% -> 6%
where the time goes in v6:
time: 66.4 us; the launch traced here: 65.6 us
  blocking collectives  38.4 us (58%)
  Pallas kernels  12.7 us (19%)
  starting transfers between devices  11.4 us (17%)
  waiting for transfers between devices  2.29 us (3%)
  local copies, waits for them, and re-layouts  0.7 us (1%)
    all_to_all x1, blocking collectives, per_device(): lax.all_to_all(packed.reshape(3 * owners, 1, LANES), 'own', split_axis=0,...  38.4 us
    pallas_call x1, Pallas kernels, per_device(): pl.pallas_call(others_kernel, out_shape=(jax.ShapeDtypeStruct((groups * S...  5.97 us
    ppermute x1, starting transfers between devices, per_device(): far = lax.ppermute(far, 'own', across)  5.46 us
    all_to_all x1, starting transfers between devices, per_device(): parts = lax.all_to_all(sent, 'grp', split_axis=0, concat_axis=0, tiled=True)  4.01 us
    pallas_call x1, Pallas kernels, per_device(): pl.pallas_call(own_kernel, out_shape=jax.ShapeDtypeStruct((STRIP, width),...  3.47 us
    ppermute x1, starting transfers between devices, per_device(): near = lax.ppermute(near, 'own', on_chip)  1.92 us
  transfers between devices with their start and end apart: 3, of which 2 were waited for; matrix products, arithmetic and copies ran while one was open for 0% of the time, Pallas kernels for 6%

profile of v6, /device:TPU:25, one launch (start us, length us, event | category | flops | bytes accessed | tf_op | source)
XLA Modules:
  0.0 65.6 jit_solution(11953102505407665499)
XLA Ops:
  0.0 1.2 %pack.1 = f32[384,128]{1,0:T(8,128)S(1)} custom-call(s32[192,128]{1,0:T(8,128)} %bitcast.16, s32[192,128]{1,0:T(8,128)} %bitcast.17, bf16[192,1,128]{2,1,0:T(2,128)(2,1)} %bitcast.18, s32[1,128]{1,0:T(1,128)} %bitcast.19), custom_call_target="tpu_custom_call" | custom-call | tf_op jit(solution)/shard_map/pack/pallas_call | solution.py:224
  1.2 38.4 %all_to_all.16 = f32[384,1,128]{2,1,0:T(1,128)S(1)} all-to-all(f32[384,1,128]{2,1,0:T(1,128)S(1)} %bitcast.15), channel_id=1, replica_groups=mesh['grp'=4,'own'=128] {'own'}, dimensions={0} | all-to-all | bytes 393216 | tf_op jit(solution)/shard_map/all_to_all | solution.py:250
  39.6 6.0 %others.1 = (bf16[32,4224]{1,0:T(8,128)(2,1)}, f32[16,128]{1,0:T(8,128)S(1)}, f32[192,128]{1,0:T(8,128)S(1)}, f32[192,128]{1,0:T(8,128)S(1)}, f32[192,128]{1,0:T(8,128)S(1)}) custom-call(f32[384,128]{1,0:T(8,128)S(1)} %bitcast.14), custom_call_target="tpu_custom_call" | custom-call | tf_op jit(solution)/shard_map/others/pallas_call | solution.py:254
  45.6 4.0 %all-to-all-start.1 = ((bf16[4,8,4224]{2,1,0:T(8,128)(2,1)}), bf16[4,8,4224]{2,1,0:T(8,128)(2,1)S(1)}, u32[]{:S(2)}, u32[]{:S(2)}) async-start(bf16[4,8,4224]{2,1,0:T(8,128)(2,1)} %bitcast.8), calls=%async_computation.1 | async-start | bytes 540672 | tf_op jit(solution)/shard_map/all_to_all | solution.py:270
  49.6 0.0 copy-start
  49.6 0.7 %copy-done = f32[9,9]{1,0:T(8,128)S(1)} copy-done((f32[9,9]{1,0:T(8,128)S(1)}, f32[9,9]{1,0:T(8,128)}, u32[]{:S(2)}) %copy-start) | copy-done | bytes 348
  50.3 0.7 %band.1 = (f32[72,144]{1,0:T(8,128)S(1)}, f32[8,128]{1,0:T(8,128)S(1)}) custom-call(s32[1]{0:T(128)} %bitcast.parity_ref, f32[9,9]{1,0:T(8,128)S(1)} %copy-done), custom_call_target="tpu_custom_call" | custom-call | tf_op jit(solution)/shard_map/band/pallas_call | solution.py:285
  51.1 3.5 %own.1.own_ref = bf16[8,4224]{1,0:T(8,128)(2,1)S(1)} custom-call(f32[192,128]{1,0:T(8,128)S(1)} %get-tuple-element.20.first_ref, f32[192,128]{1,0:T(8,128)S(1)} %get-tuple-element.21.second_ref, f32[192,128]{1,0:T(8,128)S(1)} %get-tuple-element.22.mass_ref, f32[16,128]{1,0:T(8,128)S(1)} %get-tuple-element.23.side_ref), custom_call_target="tpu_custom_call" | custom-call | flops 1610612736 | bytes 524288 | tf_op jit(solution)/shard_map/own/pallas_call | solution.py:271
  54.6 1.1 %all-to-all-done.1 = bf16[4,8,4224]{2,1,0:T(8,128)(2,1)S(1)} async-done(((bf16[4,8,4224]{2,1,0:T(8,128)(2,1)}), bf16[4,8,4224]{2,1,0:T(8,128)(2,1)S(1)}, u32[]{:S(2)}, u32[]{:S(2)}) %all-to-all-start.1) | async-done | bytes 270368 | tf_op jit(solution)/shard_map/all_to_all | solution.py:270
  55.7 0.1 near.1
  55.7 0.1 far.1
  55.8 5.5 %collective-permute-start.1 = (bf16[4,4224]{1,0:T(4,128)(2,1)S(1)}, bf16[4,4224]{1,0:T(4,128)(2,1)S(1)}, u32[]{:S(2)}, u32[]{:S(2)}) collective-permute-start(bf16[4,4224]{1,0:T(4,128)(2,1)S(1)} %far.1), channel_id=1, source_target_pairs={{1,2},{3,4},{5,6},{7,8},{9,10},{11,12},{13,14},{15,16},{17,18},{19... | collective-permute-start | bytes 101384 | tf_op jit(solution)/shard_map/ppermute | solution.py:312
  61.3 1.9 %collective-permute-start = (bf16[4,4224]{1,0:T(4,128)(2,1)S(1)}, bf16[4,4224]{1,0:T(4,128)(2,1)S(1)}, u32[]{:S(2)}, u32[]{:S(2)}) collective-permute-start(bf16[4,4224]{1,0:T(4,128)(2,1)S(1)} %near.1), channel_id=1, source_target_pairs={{0,1},{1,0},{2,3},{3,2},{4,5},{5,4},{6,7},{7,6},{8,9},{9,8},{10,11... | collective-permute-start | bytes 101384 | tf_op jit(solution)/shard_map/ppermute | solution.py:313
  63.2 0.0 collective-permute-done.1.far_ref
  63.2 1.2 %collective-permute-done.near_ref = bf16[4,4224]{1,0:T(4,128)(2,1)S(1)} collective-permute-done((bf16[4,4224]{1,0:T(4,128)(2,1)S(1)}, bf16[4,4224]{1,0:T(4,128)(2,1)S(1)}, u32[]{:S(2)}, u32[]{:S(2)}) %collective-permute-start) | collective-permute-done | bytes 33824 | tf_op jit(solution)/shard_map/ppermute | solution.py:313
  64.4 1.2 %smooth.1 = f32[8,4096]{1,0:T(8,128)} custom-call(f32[72,144]{1,0:T(8,128)S(1)} %get-tuple-element.18.band_ref, bf16[32,4224]{1,0:T(8,128)(2,1)S(1)} %bitcast.13, bf16[8,4224]{1,0:T(8,128)(2,1)S(1)} %own.1.own_ref, bf16[4,4224]{1,0:T(4,128)(2,1)S(1)} %collective-permute-done.near_ref, bf16[4,4224]{1,0:T(4,128)(2,1)S(1)} %collective-permute-done.1.far_ref), custom_call_target="tpu_custom_call" | custom-call | tf_op jit(solution)/shard_map/smooth/pallas_call | solution.py:314
Async XLA Ops:
  45.6 10.1 %all-to-all-start.1 = ((bf16[4,8,4224]{2,1,0:T(8,128)(2,1)}), bf16[4,8,4224]{2,1,0:T(8,128)(2,1)S(1)}, u32[]{:S(2)}, u32[]{:S(2)}) async-start(bf16[4,8,4224]{2,1,0:T(8,128)(2,1)} %bitcast.8), calls=%async_computation.1 | async-start | bytes 540672 | tf_op jit(solution)/shard_map/all_to_all | solution.py:270
  49.6 0.7 %copy-start = (f32[9,9]{1,0:T(8,128)S(1)}, f32[9,9]{1,0:T(8,128)}, u32[]{:S(2)}) copy-start(f32[9,9]{1,0:T(8,128)} %kernel_ref) | copy-start | bytes 976
  55.8 7.4 %collective-permute-start.1 = (bf16[4,4224]{1,0:T(4,128)(2,1)S(1)}, bf16[4,4224]{1,0:T(4,128)(2,1)S(1)}, u32[]{:S(2)}, u32[]{:S(2)}) collective-permute-start(bf16[4,4224]{1,0:T(4,128)(2,1)S(1)} %far.1), channel_id=1, source_target_pairs={{1,2},{3,4},{5,6},{7,8},{9,10},{11,12},{13,14},{15,16},{17,18},{19... | collective-permute-start | bytes 101384 | tf_op jit(solution)/shard_map/ppermute | solution.py:312
  61.3 3.1 %collective-permute-start = (bf16[4,4224]{1,0:T(4,128)(2,1)S(1)}, bf16[4,4224]{1,0:T(4,128)(2,1)S(1)}, u32[]{:S(2)}, u32[]{:S(2)}) collective-permute-start(bf16[4,4224]{1,0:T(4,128)(2,1)S(1)} %near.1), channel_id=1, source_target_pairs={{0,1},{1,0},{2,3},{3,2},{4,5},{5,4},{6,7},{7,6},{8,9},{9,8},{10,11... | collective-permute-start | bytes 101384 | tf_op jit(solution)/shard_map/ppermute | solution.py:313

commit v7 on v6

--- a/solution.py
+++ b/solution.py
@@ -17,8 +17,8 @@
 TERM = 48
 SPAN = 256
 CELLS = STRIP * W // SPAN
-ROWS = 96
-OWN_ROWS = 96
+ROWS = 136
+STEP = 8
 
 
 def vmem_spec():
@@ -75,34 +75,57 @@
     out_ref[pl.ds(5, pairs, stride=6), :] = masses[2]
 
 
-def one_hot_sum(acc_ref, first_ref, second_ref, mass_ref, rows):
-    cells = acc_ref.shape[0]
+def one_hot_sum(cells, first_ref, second_ref, mass_ref, start, rows):
     first_iota = (
         lax.broadcasted_iota(jnp.int32, (cells, LANES), 0).astype(jnp.float32) - 256.0
     ).astype(jnp.bfloat16)
     second_iota = lax.broadcasted_iota(jnp.int32, (SPAN, LANES), 0).astype(jnp.float32).astype(jnp.bfloat16)
     one = jnp.ones((), jnp.bfloat16)
     zero = jnp.zeros((), jnp.bfloat16)
-
-    def part(i):
-        here = pl.ds(i * rows, rows)
-        first = first_ref[here, :].astype(jnp.bfloat16)
-        second = second_ref[here, :].astype(jnp.bfloat16)
-        mass = mass_ref[here, :].astype(jnp.bfloat16)
-        left, right = [], []
-        for r in range(rows):
-            left.append(jnp.where(first_iota == first[r : r + 1], one, zero))
-            right.append(jnp.where(second_iota == second[r : r + 1], mass[r : r + 1], zero))
-        return lax.dot_general(
-            jnp.concatenate(left, axis=1),
-            jnp.concatenate(right, axis=1),
-            (((1,), (1,)), ((), ())),
-            preferred_element_type=jnp.float32,
-        )
-
-    acc_ref[...] = part(0)
-    for i in range(1, first_ref.shape[0] // rows):
-        acc_ref[...] += part(i)
+    here = pl.ds(start, rows)
+    first = first_ref[here, :].astype(jnp.bfloat16)
+    second = second_ref[here, :].astype(jnp.bfloat16)
+    mass = mass_ref[here, :].astype(jnp.bfloat16)
+    left, right = [], []
+    for r in range(rows):
+        left.append(jnp.where(first_iota == first[r : r + 1], one, zero))
+        right.append(jnp.where(second_iota == second[r : r + 1], mass[r : r + 1], zero))
+    return lax.dot_general(
+        jnp.concatenate(left, axis=1),
+        jnp.concatenate(right, axis=1),
+        (((1,), (1,)), ((), ())),
+        preferred_element_type=jnp.float32,
+    )
+
+
+def packed_units(planes, live):
+    units = live.shape[0]
+    count = units // 2
+    low = lax.broadcasted_iota(jnp.int32, (count, LANES), 1) < 64
+
+    def placed(value, is_high, to_high):
+        moved = value if is_high == to_high else pltpu.roll(value, 64, 1)
+        return jnp.where(low, 0.0, moved) if to_high else jnp.where(low, moved, 0.0)
+
+    sources = jnp.concatenate(
+        [
+            jnp.concatenate([placed(value, is_high, to_high) for value, is_high in kind], axis=1)
+            for to_high in (False, True)
+            for kind in planes
+        ],
+        axis=0,
+    ).astype(jnp.bfloat16)
+    row = lax.broadcasted_iota(jnp.int32, (units, units), 0)
+    column = lax.broadcasted_iota(jnp.int32, (units, units), 1)
+    counted = jnp.where(row < column, 1.0, jnp.where(row == column, 512.0, 0.0))
+    counted = (jnp.broadcast_to(live, (units, units)) * counted).astype(jnp.bfloat16)
+    place = jnp.dot(jnp.ones((8, units), jnp.bfloat16), counted, preferred_element_type=jnp.float32)
+    place = jnp.broadcast_to(place[:1] - 512.0, (count, units))
+    target = lax.broadcasted_iota(jnp.int32, (count, units), 0).astype(jnp.float32) * 2.0
+    chosen = jnp.concatenate(
+        [jnp.where(place == target, 1.0, 0.0), jnp.where(place == target + 1.0, 1.0, 0.0)], axis=1
+    ).astype(jnp.bfloat16)
+    return jnp.dot(chosen, sources, preferred_element_type=jnp.float32)
 
 
 def store_strip(out_ref, rows, acc_ref, at, before, after):
@@ -120,23 +143,48 @@
     share = CELLS // quarters
     sources = points_ref.shape[0] // 3
     half = sources // 2
+    origin = (here + 1) * share - STRIP
+
+    def split(ids):
+        ids = ids.astype(jnp.int32)
+        first = ((ids >> 8) - origin) & (CELLS - 1)
+        return (first - 256).astype(jnp.float32), (ids & 255).astype(jnp.float32)
+
+    ids = points_ref[pl.ds(0, sources, stride=3), :]
+    mixed = points_ref[pl.ds(1, sources, stride=3), :]
+    masses = points_ref[pl.ds(2, sources, stride=3), :]
     low = lax.broadcasted_iota(jnp.int32, (half, LANES), 1) < 64
-    upper = points_ref[pl.ds(1, half, stride=3), :]
-    lower = points_ref[pl.ds(1 + 3 * half, half, stride=3), :]
-    mixed_ids = jnp.where(low, upper, pltpu.roll(lower, 64, 1))
-    mixed_masses = jnp.where(low, pltpu.roll(upper, 64, 1), lower)
-    origin = (here + 1) * share - STRIP
-    for ids, masses, at in (
-        (points_ref[pl.ds(0, sources, stride=3), :], points_ref[pl.ds(2, sources, stride=3), :], 0),
-        (mixed_ids, mixed_masses, sources),
-    ):
-        ids = ids.astype(jnp.int32)
-        rows = pl.ds(at, ids.shape[0])
-        first = ((ids >> 8) - origin) & (CELLS - 1)
-        first_ref[rows, :] = (first - 256).astype(jnp.float32)
-        second_ref[rows, :] = (ids & 255).astype(jnp.float32)
-        mass_ref[rows, :] = masses
-    one_hot_sum(acc_ref, first_ref, second_ref, mass_ref, ROWS)
+    refs = (first_ref, second_ref, mass_ref)
+    heads = [jnp.where(low, value[:half], pltpu.roll(value[half:], 64, 1)) for value in (ids, masses)]
+    for ref, value in zip(refs, (*split(heads[0]), heads[1])):
+        ref[:half, :] = value
+    low = lax.broadcasted_iota(jnp.int32, (sources, LANES), 1) < 64
+    live = jnp.concatenate(
+        [
+            jnp.max(jnp.where(low | (value == 0.0), 0.0, 1.0), axis=1, keepdims=True)
+            for value in (masses, mixed)
+        ],
+        axis=0,
+    )
+    tails = packed_units(
+        (
+            [(value, True) for value in (*split(ids), masses)],
+            [(value, False) for value in split(mixed)] + [(mixed, True)],
+        ),
+        live,
+    )
+    for i, ref in enumerate(refs):
+        ref[half:, :] = tails[:, i * LANES : (i + 1) * LANES]
+    rows = half + ((jnp.sum(live).astype(jnp.int32) + 1) >> 1)
+    cells = acc_ref.shape[0]
+    acc_ref[...] = one_hot_sum(cells, *refs, 0, ROWS)
+
+    def more(i, carry):
+        start = pl.multiple_of(ROWS + i * STEP, STEP)
+        acc_ref[...] += one_hot_sum(cells, *refs, start, STEP)
+        return carry
+
+    lax.fori_loop(0, (jnp.maximum(rows - ROWS, 0) + STEP - 1) // STEP, more, 0)
     blank = jnp.zeros((STRIP, LANES), jnp.float32)
     for r in range(1, quarters):
         quarter = (here + r) & (quarters - 1)
@@ -156,7 +204,14 @@
 def own_kernel(first_ref, second_ref, mass_ref, side_ref, out_ref, moved_ref, acc_ref):
     moved = first_ref[...] + float(out_ref.shape[1] // SPAN * STRIP - STRIP)
     moved_ref[...] = jnp.where(moved < CELLS // 2, moved, moved - CELLS)
-    one_hot_sum(acc_ref, moved_ref, second_ref, mass_ref, OWN_ROWS)
+    cells = acc_ref.shape[0]
+    acc_ref[...] = one_hot_sum(cells, moved_ref, second_ref, mass_ref, 0, ROWS)
+    rest = first_ref.shape[0] - ROWS
+
+    @pl.when(jnp.max(jnp.abs(mass_ref[ROWS:, :])) > 0.0)
+    def _():
+        acc_ref[...] += one_hot_sum(cells, moved_ref, second_ref, mass_ref, ROWS, rest)
+
     before = side_ref[:STRIP, :]
     after = side_ref[STRIP:, :]
     store_strip(out_ref, pl.ds(0, STRIP), acc_ref, 0, before, after)

time: 66.4 us -> 66.5 us (level)
    ppermute x1, starting transfers between devices: 5.46 us -> 4.51 us  [per_device(): far = lax.ppermute(far, 'own', across)]
    ppermute x1, waiting for transfers between devices: 0.01 us -> 0.91 us  [per_device(): far = lax.ppermute(far, 'own', across)]
    ppermute x1, waiting for transfers between devices: 1.16 us -> 0.27 us  [per_device(): near = lax.ppermute(near, 'own', on_chip)]
  transfers between devices with their start and end apart: 3 -> 3, of which waited for: 2 -> 3; matrix products, arithmetic and copies ran while one was open for 0% -> 0% of each run, Pallas kernels for 6% -> 7%
where the time goes in v7:
time: 66.5 us; the launch traced here: 65.7 us
  blocking collectives  38.4 us (58%)
  Pallas kernels  12.9 us (19%)
  starting transfers between devices  10.9 us (16%)
  waiting for transfers between devices  2.79 us (4%)
  local copies, waits for them, and re-layouts  0.7 us (1%)
    all_to_all x1, blocking collectives, per_device(): lax.all_to_all(packed.reshape(3 * owners, 1, LANES), 'own', split_axis=0,...  38.4 us
    pallas_call x1, Pallas kernels, per_device(): pl.pallas_call(others_kernel, out_shape=(jax.ShapeDtypeStruct((groups * S...  5.91 us
    ppermute x1, starting transfers between devices, per_device(): far = lax.ppermute(far, 'own', across)  4.51 us
    all_to_all x1, starting transfers between devices, per_device(): parts = lax.all_to_all(sent, 'grp', split_axis=0, concat_axis=0, tiled=True)  4.43 us
    pallas_call x1, Pallas kernels, per_device(): pl.pallas_call(own_kernel, out_shape=jax.ShapeDtypeStruct((STRIP, width),...  3.66 us
    ppermute x1, starting transfers between devices, per_device(): near = lax.ppermute(near, 'own', on_chip)  1.92 us
    all_to_all x1, waiting for transfers between devices, per_device(): parts = lax.all_to_all(sent, 'grp', split_axis=0, concat_axis=0, tiled=True)  1.62 us
  transfers between devices with their start and end apart: 3, of which 3 were waited for; matrix products, arithmetic and copies ran while one was open for 0% of the time, Pallas kernels for 7%

profile of v7, /device:TPU:25, one launch (start us, length us, event | category | flops | bytes accessed | tf_op | source)
XLA Modules:
  0.0 65.7 jit_solution(10392690578019222281)
XLA Ops:
  0.0 1.2 %pack.1 = f32[384,128]{1,0:T(8,128)S(1)} custom-call(s32[192,128]{1,0:T(8,128)} %bitcast.16, s32[192,128]{1,0:T(8,128)} %bitcast.17, bf16[192,1,128]{2,1,0:T(2,128)(2,1)} %bitcast.18, s32[1,128]{1,0:T(1,128)} %bitcast.19), custom_call_target="tpu_custom_call" | custom-call | tf_op jit(solution)/shard_map/pack/pallas_call | solution.py:279
  1.2 38.4 %all_to_all.16 = f32[384,1,128]{2,1,0:T(1,128)S(1)} all-to-all(f32[384,1,128]{2,1,0:T(1,128)S(1)} %bitcast.15), channel_id=1, replica_groups=mesh['grp'=4,'own'=128] {'own'}, dimensions={0} | all-to-all | bytes 393216 | tf_op jit(solution)/shard_map/all_to_all | solution.py:305
  39.6 5.9 %others.1 = (bf16[32,4224]{1,0:T(8,128)(2,1)}, f32[16,128]{1,0:T(8,128)S(1)}, f32[192,128]{1,0:T(8,128)S(1)}, f32[192,128]{1,0:T(8,128)S(1)}, f32[192,128]{1,0:T(8,128)S(1)}) custom-call(f32[384,128]{1,0:T(8,128)S(1)} %bitcast.14), custom_call_target="tpu_custom_call" | custom-call | tf_op jit(solution)/shard_map/others/pallas_call | solution.py:309
  45.6 4.4 %all-to-all-start.1 = ((bf16[4,8,4224]{2,1,0:T(8,128)(2,1)}), bf16[4,8,4224]{2,1,0:T(8,128)(2,1)S(1)}, u32[]{:S(2)}, u32[]{:S(2)}) async-start(bf16[4,8,4224]{2,1,0:T(8,128)(2,1)} %bitcast.8), calls=%async_computation.1 | async-start | bytes 540672 | tf_op jit(solution)/shard_map/all_to_all | solution.py:325
  50.0 0.0 copy-start
  50.0 0.7 %copy-done = f32[9,9]{1,0:T(8,128)S(1)} copy-done((f32[9,9]{1,0:T(8,128)S(1)}, f32[9,9]{1,0:T(8,128)}, u32[]{:S(2)}) %copy-start) | copy-done | bytes 348
  50.7 0.7 %band.1 = (f32[72,144]{1,0:T(8,128)S(1)}, f32[8,128]{1,0:T(8,128)S(1)}) custom-call(s32[1]{0:T(128)} %bitcast.parity_ref, f32[9,9]{1,0:T(8,128)S(1)} %copy-done), custom_call_target="tpu_custom_call" | custom-call | tf_op jit(solution)/shard_map/band/pallas_call | solution.py:340
  51.4 3.7 %own.1.own_ref = bf16[8,4224]{1,0:T(8,128)(2,1)S(1)} custom-call(f32[192,128]{1,0:T(8,128)S(1)} %get-tuple-element.20.first_ref, f32[192,128]{1,0:T(8,128)S(1)} %get-tuple-element.21.second_ref, f32[192,128]{1,0:T(8,128)S(1)} %get-tuple-element.22.mass_ref, f32[16,128]{1,0:T(8,128)S(1)} %get-tuple-element.23.side_ref), custom_call_target="tpu_custom_call" | custom-call | flops 1610612736 | bytes 524288 | tf_op jit(solution)/shard_map/own/pallas_call | solution.py:326
  55.1 1.6 %all-to-all-done.1 = bf16[4,8,4224]{2,1,0:T(8,128)(2,1)S(1)} async-done(((bf16[4,8,4224]{2,1,0:T(8,128)(2,1)}), bf16[4,8,4224]{2,1,0:T(8,128)(2,1)S(1)}, u32[]{:S(2)}, u32[]{:S(2)}) %all-to-all-start.1) | async-done | bytes 270368 | tf_op jit(solution)/shard_map/all_to_all | solution.py:325
  56.7 0.1 near.1
  56.8 0.1 far.1
  56.9 4.5 %collective-permute-start.1 = (bf16[4,4224]{1,0:T(4,128)(2,1)S(1)}, bf16[4,4224]{1,0:T(4,128)(2,1)S(1)}, u32[]{:S(2)}, u32[]{:S(2)}) collective-permute-start(bf16[4,4224]{1,0:T(4,128)(2,1)S(1)} %far.1), channel_id=1, source_target_pairs={{1,2},{3,4},{5,6},{7,8},{9,10},{11,12},{13,14},{15,16},{17,18},{19... | collective-permute-start | bytes 101384 | tf_op jit(solution)/shard_map/ppermute | solution.py:367
  61.4 1.9 %collective-permute-start = (bf16[4,4224]{1,0:T(4,128)(2,1)S(1)}, bf16[4,4224]{1,0:T(4,128)(2,1)S(1)}, u32[]{:S(2)}, u32[]{:S(2)}) collective-permute-start(bf16[4,4224]{1,0:T(4,128)(2,1)S(1)} %near.1), channel_id=1, source_target_pairs={{0,1},{1,0},{2,3},{3,2},{4,5},{5,4},{6,7},{7,6},{8,9},{9,8},{10,11... | collective-permute-start | bytes 101384 | tf_op jit(solution)/shard_map/ppermute | solution.py:368
  63.3 0.9 %collective-permute-done.1.far_ref = bf16[4,4224]{1,0:T(4,128)(2,1)S(1)} collective-permute-done((bf16[4,4224]{1,0:T(4,128)(2,1)S(1)}, bf16[4,4224]{1,0:T(4,128)(2,1)S(1)}, u32[]{:S(2)}, u32[]{:S(2)}) %collective-permute-start.1) | collective-permute-done | bytes 33824 | tf_op jit(solution)/shard_map/ppermute | solution.py:367
  64.2 0.3 collective-permute-done.near_ref
  64.5 1.2 %smooth.1 = f32[8,4096]{1,0:T(8,128)} custom-call(f32[72,144]{1,0:T(8,128)S(1)} %get-tuple-element.18.band_ref, bf16[32,4224]{1,0:T(8,128)(2,1)S(1)} %bitcast.13, bf16[8,4224]{1,0:T(8,128)(2,1)S(1)} %own.1.own_ref, bf16[4,4224]{1,0:T(4,128)(2,1)S(1)} %collective-permute-done.near_ref, bf16[4,4224]{1,0:T(4,128)(2,1)S(1)} %collective-permute-done.1.far_ref), custom_call_target="tpu_custom_call" | custom-call | tf_op jit(solution)/shard_map/smooth/pallas_call | solution.py:369
Async XLA Ops:
  45.6 11.2 %all-to-all-start.1 = ((bf16[4,8,4224]{2,1,0:T(8,128)(2,1)}), bf16[4,8,4224]{2,1,0:T(8,128)(2,1)S(1)}, u32[]{:S(2)}, u32[]{:S(2)}) async-start(bf16[4,8,4224]{2,1,0:T(8,128)(2,1)} %bitcast.8), calls=%async_computation.1 | async-start | bytes 540672 | tf_op jit(solution)/shard_map/all_to_all | solution.py:325
  50.0 0.7 %copy-start = (f32[9,9]{1,0:T(8,128)S(1)}, f32[9,9]{1,0:T(8,128)}, u32[]{:S(2)}) copy-start(f32[9,9]{1,0:T(8,128)} %kernel_ref) | copy-start | bytes 976
  56.9 7.4 %collective-permute-start.1 = (bf16[4,4224]{1,0:T(4,128)(2,1)S(1)}, bf16[4,4224]{1,0:T(4,128)(2,1)S(1)}, u32[]{:S(2)}, u32[]{:S(2)}) collective-permute-start(bf16[4,4224]{1,0:T(4,128)(2,1)S(1)} %far.1), channel_id=1, source_target_pairs={{1,2},{3,4},{5,6},{7,8},{9,10},{11,12},{13,14},{15,16},{17,18},{19... | collective-permute-start | bytes 101384 | tf_op jit(solution)/shard_map/ppermute | solution.py:367
  61.4 3.1 %collective-permute-start = (bf16[4,4224]{1,0:T(4,128)(2,1)S(1)}, bf16[4,4224]{1,0:T(4,128)(2,1)S(1)}, u32[]{:S(2)}, u32[]{:S(2)}) collective-permute-start(bf16[4,4224]{1,0:T(4,128)(2,1)S(1)} %near.1), channel_id=1, source_target_pairs={{0,1},{1,0},{2,3},{3,2},{4,5},{5,4},{6,7},{7,6},{8,9},{9,8},{10,11... | collective-permute-start | bytes 101384 | tf_op jit(solution)/shard_map/ppermute | solution.py:368

commit v8 on v7

--- a/solution.py
+++ b/solution.py
@@ -70,9 +70,9 @@
     out_ref[pl.ds(0, pairs, stride=6), :] = ids[0]
     out_ref[pl.ds(1, pairs, stride=6), :] = jnp.where(low, ids[1], pltpu.roll(masses[1], half, 1))
     out_ref[pl.ds(2, pairs, stride=6), :] = masses[0]
-    out_ref[pl.ds(3, pairs, stride=6), :] = ids[2]
-    out_ref[pl.ds(4, pairs, stride=6), :] = jnp.where(low, pltpu.roll(ids[1], half, 1), masses[1])
-    out_ref[pl.ds(5, pairs, stride=6), :] = masses[2]
+    out_ref[pl.ds(3, pairs, stride=6), :] = pltpu.roll(jnp.where(low, ids[2], ids[1]), half, 1)
+    out_ref[pl.ds(4, pairs, stride=6), :] = jnp.where(low, pltpu.roll(ids[2], half, 1), masses[2])
+    out_ref[pl.ds(5, pairs, stride=6), :] = pltpu.roll(jnp.where(low, masses[2], masses[1]), half, 1)
 
 
 def one_hot_sum(cells, first_ref, second_ref, mass_ref, start, rows):

time: 66.5 us -> 65.5 us (0.985)
  Pallas kernels: 12.9 us -> 10.9 us
    pallas_call x1, Pallas kernels: 3.66 us -> 2.51 us  [per_device(): pl.pallas_call(own_kernel, out_shape=jax.ShapeDtypeStruct((STRIP, width),...]
    ppermute x1, starting transfers between devices: 4.51 us -> 5.45 us  [per_device(): far = lax.ppermute(far, 'own', across)]
    ppermute x1, waiting for transfers between devices: 0.91 us -> 0.01 us  [per_device(): far = lax.ppermute(far, 'own', across)]
    ppermute x1, waiting for transfers between devices: 0.27 us -> 1.16 us  [per_device(): near = lax.ppermute(near, 'own', on_chip)]
    pallas_call x1, Pallas kernels: 5.91 us -> 5.06 us  [per_device(): pl.pallas_call(others_kernel, out_shape=(jax.ShapeDtypeStruct((groups * S...]
  transfers between devices with their start and end apart: 3 -> 3, of which waited for: 3 -> 2; matrix products, arithmetic and copies ran while one was open for 0% -> 0% of each run, Pallas kernels for 7% -> 5%
where the time goes in v8:
time: 65.5 us; the launch traced here: 64.7 us
  blocking collectives  38.4 us (59%)
  starting transfers between devices  11.4 us (17%)
  Pallas kernels  10.9 us (17%)
  waiting for transfers between devices  3.26 us (5%)
  local copies, waits for them, and re-layouts  0.7 us (1%)
    all_to_all x1, blocking collectives, per_device(): lax.all_to_all(packed.reshape(3 * owners, 1, LANES), 'own', split_axis=0,...  38.4 us
    ppermute x1, starting transfers between devices, per_device(): far = lax.ppermute(far, 'own', across)  5.45 us
    pallas_call x1, Pallas kernels, per_device(): pl.pallas_call(others_kernel, out_shape=(jax.ShapeDtypeStruct((groups * S...  5.06 us
    all_to_all x1, starting transfers between devices, per_device(): parts = lax.all_to_all(sent, 'grp', split_axis=0, concat_axis=0, tiled=True)  4.01 us
    pallas_call x1, Pallas kernels, per_device(): pl.pallas_call(own_kernel, out_shape=jax.ShapeDtypeStruct((STRIP, width),...  2.51 us
    all_to_all x1, waiting for transfers between devices, per_device(): parts = lax.all_to_all(sent, 'grp', split_axis=0, concat_axis=0, tiled=True)  2.1 us
    ppermute x1, starting transfers between devices, per_device(): near = lax.ppermute(near, 'own', on_chip)  1.92 us
  transfers between devices with their start and end apart: 3, of which 2 were waited for; matrix products, arithmetic and copies ran while one was open for 0% of the time, Pallas kernels for 5%

profile of v8, /device:TPU:25, one launch (start us, length us, event | category | flops | bytes accessed | tf_op | source)
XLA Modules:
  0.0 64.7 jit_solution(7170955512295457843)
XLA Ops:
  0.0 1.2 %pack.1 = f32[384,128]{1,0:T(8,128)S(1)} custom-call(s32[192,128]{1,0:T(8,128)} %bitcast.16, s32[192,128]{1,0:T(8,128)} %bitcast.17, bf16[192,1,128]{2,1,0:T(2,128)(2,1)} %bitcast.18, s32[1,128]{1,0:T(1,128)} %bitcast.19), custom_call_target="tpu_custom_call" | custom-call | tf_op jit(solution)/shard_map/pack/pallas_call | solution.py:279
  1.3 38.4 %all_to_all.16 = f32[384,1,128]{2,1,0:T(1,128)S(1)} all-to-all(f32[384,1,128]{2,1,0:T(1,128)S(1)} %bitcast.15), channel_id=1, replica_groups=mesh['grp'=4,'own'=128] {'own'}, dimensions={0} | all-to-all | bytes 393216 | tf_op jit(solution)/shard_map/all_to_all | solution.py:305
  39.7 5.1 %others.1 = (bf16[32,4224]{1,0:T(8,128)(2,1)}, f32[16,128]{1,0:T(8,128)S(1)}, f32[192,128]{1,0:T(8,128)S(1)}, f32[192,128]{1,0:T(8,128)S(1)}, f32[192,128]{1,0:T(8,128)S(1)}) custom-call(f32[384,128]{1,0:T(8,128)S(1)} %bitcast.14), custom_call_target="tpu_custom_call" | custom-call | tf_op jit(solution)/shard_map/others/pallas_call | solution.py:309
  44.7 4.0 %all-to-all-start.1 = ((bf16[4,8,4224]{2,1,0:T(8,128)(2,1)}), bf16[4,8,4224]{2,1,0:T(8,128)(2,1)S(1)}, u32[]{:S(2)}, u32[]{:S(2)}) async-start(bf16[4,8,4224]{2,1,0:T(8,128)(2,1)} %bitcast.8), calls=%async_computation.1 | async-start | bytes 540672 | tf_op jit(solution)/shard_map/all_to_all | solution.py:325
  48.7 0.0 copy-start
  48.7 0.7 %copy-done = f32[9,9]{1,0:T(8,128)S(1)} copy-done((f32[9,9]{1,0:T(8,128)S(1)}, f32[9,9]{1,0:T(8,128)}, u32[]{:S(2)}) %copy-start) | copy-done | bytes 348
  49.4 0.7 %band.1 = (f32[72,144]{1,0:T(8,128)S(1)}, f32[8,128]{1,0:T(8,128)S(1)}) custom-call(s32[1]{0:T(128)} %bitcast.parity_ref, f32[9,9]{1,0:T(8,128)S(1)} %copy-done), custom_call_target="tpu_custom_call" | custom-call | tf_op jit(solution)/shard_map/band/pallas_call | solution.py:340
  50.2 2.5 %own.1.own_ref = bf16[8,4224]{1,0:T(8,128)(2,1)S(1)} custom-call(f32[192,128]{1,0:T(8,128)S(1)} %get-tuple-element.20.first_ref, f32[192,128]{1,0:T(8,128)S(1)} %get-tuple-element.21.second_ref, f32[192,128]{1,0:T(8,128)S(1)} %get-tuple-element.22.mass_ref, f32[16,128]{1,0:T(8,128)S(1)} %get-tuple-element.23.side_ref), custom_call_target="tpu_custom_call" | custom-call | flops 1610612736 | bytes 524288 | tf_op jit(solution)/shard_map/own/pallas_call | solution.py:326
  52.7 2.1 %all-to-all-done.1 = bf16[4,8,4224]{2,1,0:T(8,128)(2,1)S(1)} async-done(((bf16[4,8,4224]{2,1,0:T(8,128)(2,1)}), bf16[4,8,4224]{2,1,0:T(8,128)(2,1)S(1)}, u32[]{:S(2)}, u32[]{:S(2)}) %all-to-all-start.1) | async-done | bytes 270368 | tf_op jit(solution)/shard_map/all_to_all | solution.py:325
  54.8 0.1 near.1
  54.8 0.1 far.1
  54.9 5.5 %collective-permute-start.1 = (bf16[4,4224]{1,0:T(4,128)(2,1)S(1)}, bf16[4,4224]{1,0:T(4,128)(2,1)S(1)}, u32[]{:S(2)}, u32[]{:S(2)}) collective-permute-start(bf16[4,4224]{1,0:T(4,128)(2,1)S(1)} %far.1), channel_id=1, source_target_pairs={{1,2},{3,4},{5,6},{7,8},{9,10},{11,12},{13,14},{15,16},{17,18},{19... | collective-permute-start | bytes 101384 | tf_op jit(solution)/shard_map/ppermute | solution.py:367
  60.4 1.9 %collective-permute-start = (bf16[4,4224]{1,0:T(4,128)(2,1)S(1)}, bf16[4,4224]{1,0:T(4,128)(2,1)S(1)}, u32[]{:S(2)}, u32[]{:S(2)}) collective-permute-start(bf16[4,4224]{1,0:T(4,128)(2,1)S(1)} %near.1), channel_id=1, source_target_pairs={{0,1},{1,0},{2,3},{3,2},{4,5},{5,4},{6,7},{7,6},{8,9},{9,8},{10,11... | collective-permute-start | bytes 101384 | tf_op jit(solution)/shard_map/ppermute | solution.py:368
  62.3 0.0 collective-permute-done.1.far_ref
  62.3 1.2 %collective-permute-done.near_ref = bf16[4,4224]{1,0:T(4,128)(2,1)S(1)} collective-permute-done((bf16[4,4224]{1,0:T(4,128)(2,1)S(1)}, bf16[4,4224]{1,0:T(4,128)(2,1)S(1)}, u32[]{:S(2)}, u32[]{:S(2)}) %collective-permute-start) | collective-permute-done | bytes 33824 | tf_op jit(solution)/shard_map/ppermute | solution.py:368
  63.5 1.2 %smooth.1 = f32[8,4096]{1,0:T(8,128)} custom-call(f32[72,144]{1,0:T(8,128)S(1)} %get-tuple-element.18.band_ref, bf16[32,4224]{1,0:T(8,128)(2,1)S(1)} %bitcast.13, bf16[8,4224]{1,0:T(8,128)(2,1)S(1)} %own.1.own_ref, bf16[4,4224]{1,0:T(4,128)(2,1)S(1)} %collective-permute-done.near_ref, bf16[4,4224]{1,0:T(4,128)(2,1)S(1)} %collective-permute-done.1.far_ref), custom_call_target="tpu_custom_call" | custom-call | tf_op jit(solution)/shard_map/smooth/pallas_call | solution.py:369
Async XLA Ops:
  44.7 10.1 %all-to-all-start.1 = ((bf16[4,8,4224]{2,1,0:T(8,128)(2,1)}), bf16[4,8,4224]{2,1,0:T(8,128)(2,1)S(1)}, u32[]{:S(2)}, u32[]{:S(2)}) async-start(bf16[4,8,4224]{2,1,0:T(8,128)(2,1)} %bitcast.8), calls=%async_computation.1 | async-start | bytes 540672 | tf_op jit(solution)/shard_map/all_to_all | solution.py:325
  48.7 0.7 %copy-start = (f32[9,9]{1,0:T(8,128)S(1)}, f32[9,9]{1,0:T(8,128)}, u32[]{:S(2)}) copy-start(f32[9,9]{1,0:T(8,128)} %kernel_ref) | copy-start | bytes 976
  54.9 7.4 %collective-permute-start.1 = (bf16[4,4224]{1,0:T(4,128)(2,1)S(1)}, bf16[4,4224]{1,0:T(4,128)(2,1)S(1)}, u32[]{:S(2)}, u32[]{:S(2)}) collective-permute-start(bf16[4,4224]{1,0:T(4,128)(2,1)S(1)} %far.1), channel_id=1, source_target_pairs={{1,2},{3,4},{5,6},{7,8},{9,10},{11,12},{13,14},{15,16},{17,18},{19... | collective-permute-start | bytes 101384 | tf_op jit(solution)/shard_map/ppermute | solution.py:367
  60.4 3.1 %collective-permute-start = (bf16[4,4224]{1,0:T(4,128)(2,1)S(1)}, bf16[4,4224]{1,0:T(4,128)(2,1)S(1)}, u32[]{:S(2)}, u32[]{:S(2)}) collective-permute-start(bf16[4,4224]{1,0:T(4,128)(2,1)S(1)} %near.1), channel_id=1, source_target_pairs={{0,1},{1,0},{2,3},{3,2},{4,5},{5,4},{6,7},{7,6},{8,9},{9,8},{10,11... | collective-permute-start | bytes 101384 | tf_op jit(solution)/shard_map/ppermute | solution.py:368

commit v9 on v8

--- a/solution.py
+++ b/solution.py
@@ -12,6 +12,7 @@
 CAP = 192
 LANES = 128
 HALO = 4
+PLANE = 8
 TAPS = 2 * HALO + 1
 PARTS = 40
 TERM = 48
@@ -33,7 +34,17 @@
     return pltpu.CompilerParams(vmem_limit_bytes=mebibytes * 2**20)
 
 
-def pack_kernel(row_in, col_in, weight_in, count_in, out_ref, row_ref, col_ref, weight_ref, count_ref, wide_ref, sems):
+def ring_order(length):
+    half = length // 2
+    order = []
+    for step in range(half):
+        order += [half + step, half - 1 - step]
+    return order
+
+
+def pack_kernel(
+    row_in, col_in, weight_in, count_in, out_ref, row_ref, col_ref, weight_ref, count_ref, wide_ref, sorted_ref, sems
+):
     copies = [
         pltpu.make_async_copy(source, target, sems.at[i])
         for i, (source, target) in enumerate(
@@ -45,34 +56,46 @@
     for copy in copies:
         copy.wait()
     points = row_ref.shape[0]
-    pairs = points // 3
+    planes = out_ref.shape[0] // (3 * PLANE)
     for i in range(points):
         wide_ref[pl.ds(i, 1), :] = weight_ref[i].astype(jnp.float32)
-    lane = lax.broadcasted_iota(jnp.int32, (pairs, LANES), 1)
-    block = lax.broadcasted_iota(jnp.int32, (pairs, LANES), 0)
-    counts = jnp.broadcast_to(count_ref[...], (pairs, LANES))
-    even = jnp.sum(jnp.where(lane == 2 * block, counts, 0), axis=1, keepdims=True)
-    odd = jnp.sum(jnp.where(lane == 2 * block + 1, counts, 0), axis=1, keepdims=True)
+    lane = lax.broadcasted_iota(jnp.int32, (planes, LANES), 1)
+    plane = lax.broadcasted_iota(jnp.int32, (planes, LANES), 0)
+    counts = jnp.broadcast_to(count_ref[...], (planes, LANES))
     low = lane < 64
-    lives = (
-        lane < even,
-        jnp.where(low, lane + 128, lane - 64) < jnp.where(low, even, odd),
-        lane + 64 < odd,
-    )
-    ids, masses = [], []
-    for k in range(3):
-        tile_row = row_ref[pl.ds(k, pairs, stride=3), :]
-        column = col_ref[pl.ds(k, pairs, stride=3), :]
-        index = (((column >> 8) * STRIP + tile_row) << 8) + (column & 255)
-        ids.append(index.astype(jnp.float32))
-        masses.append(jnp.where(lives[k], wide_ref[pl.ds(k, pairs, stride=3), :], 0.0))
     half = LANES // 2
-    out_ref[pl.ds(0, pairs, stride=6), :] = ids[0]
-    out_ref[pl.ds(1, pairs, stride=6), :] = jnp.where(low, ids[1], pltpu.roll(masses[1], half, 1))
-    out_ref[pl.ds(2, pairs, stride=6), :] = masses[0]
-    out_ref[pl.ds(3, pairs, stride=6), :] = pltpu.roll(jnp.where(low, ids[2], ids[1]), half, 1)
-    out_ref[pl.ds(4, pairs, stride=6), :] = jnp.where(low, pltpu.roll(ids[2], half, 1), masses[2])
-    out_ref[pl.ds(5, pairs, stride=6), :] = pltpu.roll(jnp.where(low, masses[2], masses[1]), half, 1)
+    for y in range(PLANE // 2):
+        block = plane * PLANE + 2 * y
+        even = jnp.sum(jnp.where(lane == block, counts, 0), axis=1, keepdims=True)
+        odd = jnp.sum(jnp.where(lane == block + 1, counts, 0), axis=1, keepdims=True)
+        lives = (
+            lane < even,
+            jnp.where(low, lane + 128, lane - 64) < jnp.where(low, even, odd),
+            lane + 64 < odd,
+        )
+        ids, masses = [], []
+        for k in range(3):
+            rows = pl.ds(3 * y + k, planes, stride=3 * PLANE // 2)
+            index = (((col_ref[rows, :] >> 8) * STRIP + row_ref[rows, :]) << 8) + (col_ref[rows, :] & 255)
+            ids.append(index.astype(jnp.float32))
+            masses.append(jnp.where(lives[k], wide_ref[rows, :], 0.0))
+        for block, rows in (
+            (2 * y, (ids[0], jnp.where(low, ids[1], pltpu.roll(masses[1], half, 1)), masses[0])),
+            (
+                2 * y + 1,
+                (
+                    pltpu.roll(jnp.where(low, ids[2], ids[1]), half, 1),
+                    jnp.where(low, pltpu.roll(ids[2], half, 1), masses[2]),
+                    pltpu.roll(jnp.where(low, masses[2], masses[1]), half, 1),
+                ),
+            ),
+        ):
+            for r, value in enumerate(rows):
+                at = 3 * (PLANE - 1 - block) + r
+                sorted_ref[pl.ds(at, planes, stride=3 * PLANE), :] = value
+    size = 3 * PLANE
+    for place, z in enumerate(ring_order(planes)):
+        out_ref[pl.ds(place * size, size), :] = sorted_ref[pl.ds(z * size, size), :]
 
 
 def one_hot_sum(cells, first_ref, second_ref, mass_ref, start, rows):
@@ -287,6 +310,7 @@
             pltpu.VMEM((points, 1, LANES), jnp.bfloat16),
             pltpu.VMEM((1, owners), jnp.int32),
             pltpu.VMEM((points, LANES), jnp.float32),
+            pltpu.VMEM((3 * owners, LANES), jnp.float32),
             pltpu.SemaphoreType.DMA((4,)),
         ],
         compiler_params=limit(4),
@@ -302,8 +326,14 @@
             )
         )
     )
+    order = [z * PLANE + k for z in ring_order(owners // PLANE) for k in reversed(range(PLANE))]
     arrived = lax.all_to_all(
-        packed.reshape(3 * owners, 1, LANES), "own", split_axis=0, concat_axis=0, tiled=True
+        packed.reshape(3 * owners, 1, LANES),
+        "own",
+        split_axis=0,
+        concat_axis=0,
+        tiled=True,
+        axis_index_groups=[order],
     ).reshape(3 * owners, LANES)
     plane = jax.ShapeDtypeStruct((points, LANES), jnp.float32)
     sent, side, first, second, mass = pl.pallas_call(

time: 65.5 us -> 59.3 us (0.905)
  blocking collectives: 38.4 us -> 32.4 us
    all_to_all x1, blocking collectives: 38.4 us -> 32.4 us  [per_device(): lax.all_to_all(packed.reshape(3 * owners, 1, LANES), 'own', split_axis=0,...]
  transfers between devices with their start and end apart: 3 -> 3, of which waited for: 2 -> 2; matrix products, arithmetic and copies ran while one was open for 0% -> 0% of each run, Pallas kernels for 5% -> 6%
where the time goes in v9:
time: 59.3 us; the launch traced here: 58.3 us
  blocking collectives  32.4 us (55%)
  starting transfers between devices  11.4 us (19%)
  Pallas kernels  10.9 us (18%)
  waiting for transfers between devices  2.81 us (5%)
  local copies, waits for them, and re-layouts  0.7 us (1%)
    all_to_all x1, blocking collectives, per_device(): lax.all_to_all(packed.reshape(3 * owners, 1, LANES), 'own', split_axis=0,...  32.4 us
    ppermute x1, starting transfers between devices, per_device(): far = lax.ppermute(far, 'own', across)  5.48 us
    pallas_call x1, Pallas kernels, per_device(): pl.pallas_call(others_kernel, out_shape=(jax.ShapeDtypeStruct((groups * S...  5.06 us
    all_to_all x1, starting transfers between devices, per_device(): parts = lax.all_to_all(sent, 'grp', split_axis=0, concat_axis=0, tiled=True)  4.01 us
    pallas_call x1, Pallas kernels, per_device(): pl.pallas_call(own_kernel, out_shape=jax.ShapeDtypeStruct((STRIP, width),...  2.51 us
    ppermute x1, starting transfers between devices, per_device(): near = lax.ppermute(near, 'own', on_chip)  1.92 us
    all_to_all x1, waiting for transfers between devices, per_device(): parts = lax.all_to_all(sent, 'grp', split_axis=0, concat_axis=0, tiled=True)  1.65 us
    pallas_call x1, Pallas kernels, per_device(): pl.pallas_call(pack_kernel, out_shape=jax.ShapeDtypeStruct((3 * owners, L...  1.27 us
  transfers between devices with their start and end apart: 3, of which 2 were waited for; matrix products, arithmetic and copies ran while one was open for 0% of the time, Pallas kernels for 6%

profile of v9, /device:TPU:25, one launch (start us, length us, event | category | flops | bytes accessed | tf_op | source)
XLA Modules:
  0.0 58.3 jit_solution(13430605162578027086)
XLA Ops:
  0.0 1.3 %pack.1 = f32[384,128]{1,0:T(8,128)S(1)} custom-call(s32[192,128]{1,0:T(8,128)} %bitcast.16, s32[192,128]{1,0:T(8,128)} %bitcast.17, bf16[192,1,128]{2,1,0:T(2,128)(2,1)} %bitcast.18, s32[1,128]{1,0:T(1,128)} %bitcast.19), custom_call_target="tpu_custom_call" | custom-call | tf_op jit(solution)/shard_map/pack/pallas_call | solution.py:302
  1.3 32.4 %all_to_all.16 = f32[384,1,128]{2,1,0:T(1,128)S(1)} all-to-all(f32[384,1,128]{2,1,0:T(1,128)S(1)} %bitcast.15), channel_id=1, replica_groups={{71,70,69,68,67,66,65,64,63,62,61,60,59,58,57,56,79,78,77,76,75,74,73,7..., dimensions={0} | all-to-all | bytes 393216 | tf_op jit(solution)/shard_map/all_to_all | solution.py:330
  33.7 5.1 %others.1 = (bf16[32,4224]{1,0:T(8,128)(2,1)}, f32[16,128]{1,0:T(8,128)S(1)}, f32[192,128]{1,0:T(8,128)S(1)}, f32[192,128]{1,0:T(8,128)S(1)}, f32[192,128]{1,0:T(8,128)S(1)}) custom-call(f32[384,128]{1,0:T(8,128)S(1)} %bitcast.14), custom_call_target="tpu_custom_call" | custom-call | tf_op jit(solution)/shard_map/others/pallas_call | solution.py:339
  38.8 4.0 %all-to-all-start.1 = ((bf16[4,8,4224]{2,1,0:T(8,128)(2,1)}), bf16[4,8,4224]{2,1,0:T(8,128)(2,1)S(1)}, u32[]{:S(2)}, u32[]{:S(2)}) async-start(bf16[4,8,4224]{2,1,0:T(8,128)(2,1)} %bitcast.8), calls=%async_computation.1 | async-start | bytes 540672 | tf_op jit(solution)/shard_map/all_to_all | solution.py:355
  42.8 0.0 copy-start
  42.8 0.7 %copy-done = f32[9,9]{1,0:T(8,128)S(1)} copy-done((f32[9,9]{1,0:T(8,128)S(1)}, f32[9,9]{1,0:T(8,128)}, u32[]{:S(2)}) %copy-start) | copy-done | bytes 348
  43.5 0.7 %band.1 = (f32[72,144]{1,0:T(8,128)S(1)}, f32[8,128]{1,0:T(8,128)S(1)}) custom-call(s32[1]{0:T(128)} %bitcast.parity_ref, f32[9,9]{1,0:T(8,128)S(1)} %copy-done), custom_call_target="tpu_custom_call" | custom-call | tf_op jit(solution)/shard_map/band/pallas_call | solution.py:370
  44.2 2.5 %own.1.own_ref = bf16[8,4224]{1,0:T(8,128)(2,1)S(1)} custom-call(f32[192,128]{1,0:T(8,128)S(1)} %get-tuple-element.20.first_ref, f32[192,128]{1,0:T(8,128)S(1)} %get-tuple-element.21.second_ref, f32[192,128]{1,0:T(8,128)S(1)} %get-tuple-element.22.mass_ref, f32[16,128]{1,0:T(8,128)S(1)} %get-tuple-element.23.side_ref), custom_call_target="tpu_custom_call" | custom-call | flops 1610612736 | bytes 524288 | tf_op jit(solution)/shard_map/own/pallas_call | solution.py:356
  46.8 1.6 %all-to-all-done.1 = bf16[4,8,4224]{2,1,0:T(8,128)(2,1)S(1)} async-done(((bf16[4,8,4224]{2,1,0:T(8,128)(2,1)}), bf16[4,8,4224]{2,1,0:T(8,128)(2,1)S(1)}, u32[]{:S(2)}, u32[]{:S(2)}) %all-to-all-start.1) | async-done | bytes 270368 | tf_op jit(solution)/shard_map/all_to_all | solution.py:355
  48.4 0.1 near.1
  48.5 0.1 far.1
  48.5 5.5 %collective-permute-start.1 = (bf16[4,4224]{1,0:T(4,128)(2,1)S(1)}, bf16[4,4224]{1,0:T(4,128)(2,1)S(1)}, u32[]{:S(2)}, u32[]{:S(2)}) collective-permute-start(bf16[4,4224]{1,0:T(4,128)(2,1)S(1)} %far.1), channel_id=1, source_target_pairs={{1,2},{3,4},{5,6},{7,8},{9,10},{11,12},{13,14},{15,16},{17,18},{19... | collective-permute-start | bytes 101384 | tf_op jit(solution)/shard_map/ppermute | solution.py:397
  54.0 1.9 %collective-permute-start = (bf16[4,4224]{1,0:T(4,128)(2,1)S(1)}, bf16[4,4224]{1,0:T(4,128)(2,1)S(1)}, u32[]{:S(2)}, u32[]{:S(2)}) collective-permute-start(bf16[4,4224]{1,0:T(4,128)(2,1)S(1)} %near.1), channel_id=1, source_target_pairs={{0,1},{1,0},{2,3},{3,2},{4,5},{5,4},{6,7},{7,6},{8,9},{9,8},{10,11... | collective-permute-start | bytes 101384 | tf_op jit(solution)/shard_map/ppermute | solution.py:398
  55.9 0.0 collective-permute-done.1.far_ref
  56.0 1.2 %collective-permute-done.near_ref = bf16[4,4224]{1,0:T(4,128)(2,1)S(1)} collective-permute-done((bf16[4,4224]{1,0:T(4,128)(2,1)S(1)}, bf16[4,4224]{1,0:T(4,128)(2,1)S(1)}, u32[]{:S(2)}, u32[]{:S(2)}) %collective-permute-start) | collective-permute-done | bytes 33824 | tf_op jit(solution)/shard_map/ppermute | solution.py:398
  57.1 1.2 %smooth.1 = f32[8,4096]{1,0:T(8,128)} custom-call(f32[72,144]{1,0:T(8,128)S(1)} %get-tuple-element.18.band_ref, bf16[32,4224]{1,0:T(8,128)(2,1)S(1)} %bitcast.13, bf16[8,4224]{1,0:T(8,128)(2,1)S(1)} %own.1.own_ref, bf16[4,4224]{1,0:T(4,128)(2,1)S(1)} %collective-permute-done.near_ref, bf16[4,4224]{1,0:T(4,128)(2,1)S(1)} %collective-permute-done.1.far_ref), custom_call_target="tpu_custom_call" | custom-call | tf_op jit(solution)/shard_map/smooth/pallas_call | solution.py:399
Async XLA Ops:
  38.8 9.6 %all-to-all-start.1 = ((bf16[4,8,4224]{2,1,0:T(8,128)(2,1)}), bf16[4,8,4224]{2,1,0:T(8,128)(2,1)S(1)}, u32[]{:S(2)}, u32[]{:S(2)}) async-start(bf16[4,8,4224]{2,1,0:T(8,128)(2,1)} %bitcast.8), calls=%async_computation.1 | async-start | bytes 540672 | tf_op jit(solution)/shard_map/all_to_all | solution.py:355
  42.8 0.7 %copy-start = (f32[9,9]{1,0:T(8,128)S(1)}, f32[9,9]{1,0:T(8,128)}, u32[]{:S(2)}) copy-start(f32[9,9]{1,0:T(8,128)} %kernel_ref) | copy-start | bytes 976
  48.5 7.4 %collective-permute-start.1 = (bf16[4,4224]{1,0:T(4,128)(2,1)S(1)}, bf16[4,4224]{1,0:T(4,128)(2,1)S(1)}, u32[]{:S(2)}, u32[]{:S(2)}) collective-permute-start(bf16[4,4224]{1,0:T(4,128)(2,1)S(1)} %far.1), channel_id=1, source_target_pairs={{1,2},{3,4},{5,6},{7,8},{9,10},{11,12},{13,14},{15,16},{17,18},{19... | collective-permute-start | bytes 101384 | tf_op jit(solution)/shard_map/ppermute | solution.py:397
  54.0 3.1 %collective-permute-start = (bf16[4,4224]{1,0:T(4,128)(2,1)S(1)}, bf16[4,4224]{1,0:T(4,128)(2,1)S(1)}, u32[]{:S(2)}, u32[]{:S(2)}) collective-permute-start(bf16[4,4224]{1,0:T(4,128)(2,1)S(1)} %near.1), channel_id=1, source_target_pairs={{0,1},{1,0},{2,3},{3,2},{4,5},{5,4},{6,7},{7,6},{8,9},{9,8},{10,11... | collective-permute-start | bytes 101384 | tf_op jit(solution)/shard_map/ppermute | solution.py:398

commit v10 on v9

--- a/solution.py
+++ b/solution.py
@@ -168,6 +168,9 @@
     half = sources // 2
     origin = (here + 1) * share - STRIP
 
+    def place_of(quarter):
+        return sum(jnp.where(quarter == q, place, 0) for place, q in enumerate(ring_order(quarters)))
+
     def split(ids):
         ids = ids.astype(jnp.int32)
         first = ((ids >> 8) - origin) & (CELLS - 1)
@@ -214,9 +217,9 @@
         at = STRIP + (r - 1) * share
         before = jnp.where(quarter == 0, blank, acc_ref[at - STRIP : at, LANES:])
         after = jnp.where(quarter == quarters - 1, blank, acc_ref[at + share : at + share + STRIP, :LANES])
-        rows = pl.ds(pl.multiple_of(quarter * STRIP, STRIP), STRIP)
+        rows = pl.ds(pl.multiple_of(place_of(quarter) * STRIP, STRIP), STRIP)
         store_strip(out_ref, rows, acc_ref, at, before, after)
-    out_ref[pl.ds(pl.multiple_of(here * STRIP, STRIP), STRIP), :] = jnp.zeros(
+    out_ref[pl.ds(pl.multiple_of(place_of(here) * STRIP, STRIP), STRIP), :] = jnp.zeros(
         (STRIP, out_ref.shape[1]), jnp.bfloat16
     )
     last = STRIP + (quarters - 1) * share
@@ -352,7 +355,9 @@
         name="others",
     )(arrived)
     sent, kernel = lax.optimization_barrier((sent, kernel))
-    parts = lax.all_to_all(sent, "grp", split_axis=0, concat_axis=0, tiled=True)
+    parts = lax.all_to_all(
+        sent, "grp", split_axis=0, concat_axis=0, tiled=True, axis_index_groups=[ring_order(groups)]
+    )
     own = pl.pallas_call(
         own_kernel,
         out_shape=jax.ShapeDtypeStruct((STRIP, width), jnp.bfloat16),

time: 59.3 us -> 58.8 us (level)
  waiting for transfers between devices: 2.81 us -> 1.19 us
  starting transfers between devices: 11.4 us -> 12.5 us
    all_to_all x1, starting transfers between devices: 4.01 us -> 6.16 us  [per_device(): lax.all_to_all(sent, 'grp', split_axis=0, concat_axis=0, tiled=True, axis...]
    all_to_all x1, waiting for transfers between devices: 1.65 us -> 0.01 us  [per_device(): lax.all_to_all(sent, 'grp', split_axis=0, concat_axis=0, tiled=True, axis...]
    ppermute x1, starting transfers between devices: 5.48 us -> 4.45 us  [per_device(): far = lax.ppermute(far, 'own', across)]
    ppermute x1, waiting for transfers between devices: 0.01 us -> 0.97 us  [per_device(): far = lax.ppermute(far, 'own', across)]
    ppermute x1, waiting for transfers between devices: 1.16 us -> 0.2 us  [per_device(): near = lax.ppermute(near, 'own', on_chip)]
where the time goes in v10:
time: 58.8 us; the launch traced here: 57.8 us
  blocking collectives  32.4 us (55%)
  starting transfers between devices  12.5 us (21%)
  Pallas kernels  10.9 us (19%)
  waiting for transfers between devices  1.19 us (2%)
  local copies, waits for them, and re-layouts  0.7 us (1%)
    all_to_all x1, blocking collectives, per_device(): lax.all_to_all(packed.reshape(3 * owners, 1, LANES), 'own', split_axis=0,...  32.4 us
    all_to_all x1, starting transfers between devices, per_device(): lax.all_to_all(sent, 'grp', split_axis=0, concat_axis=0, tiled=True, axis...  6.16 us
    pallas_call x1, Pallas kernels, per_device(): pl.pallas_call(others_kernel, out_shape=(jax.ShapeDtypeStruct((groups * S...  5.07 us
    ppermute x1, starting transfers between devices, per_device(): far = lax.ppermute(far, 'own', across)  4.45 us
    pallas_call x1, Pallas kernels, per_device(): pl.pallas_call(own_kernel, out_shape=jax.ShapeDtypeStruct((STRIP, width),...  2.51 us
    ppermute x1, starting transfers between devices, per_device(): near = lax.ppermute(near, 'own', on_chip)  1.92 us
    pallas_call x1, Pallas kernels, per_device(): pl.pallas_call(pack_kernel, out_shape=jax.ShapeDtypeStruct((3 * owners, L...  1.27 us
    pallas_call x1, Pallas kernels, per_device(): pl.pallas_call(smooth_kernel, out_shape=jax.ShapeDtypeStruct((STRIP, quar...  1.18 us
  transfers between devices with their start and end apart: 3, of which 2 were waited for; matrix products, arithmetic and copies ran while one was open for 0% of the time, Pallas kernels for 6%

profile of v10, /device:TPU:25, one launch (start us, length us, event | category | flops | bytes accessed | tf_op | source)
XLA Modules:
  0.0 57.8 jit_solution(14488554619155058253)
XLA Ops:
  0.0 1.3 %pack.1 = f32[384,128]{1,0:T(8,128)S(1)} custom-call(s32[192,128]{1,0:T(8,128)} %bitcast.16, s32[192,128]{1,0:T(8,128)} %bitcast.17, bf16[192,1,128]{2,1,0:T(2,128)(2,1)} %bitcast.18, s32[1,128]{1,0:T(1,128)} %bitcast.19), custom_call_target="tpu_custom_call" | custom-call | tf_op jit(solution)/shard_map/pack/pallas_call | solution.py:305
  1.3 32.4 %all_to_all.16 = f32[384,1,128]{2,1,0:T(1,128)S(1)} all-to-all(f32[384,1,128]{2,1,0:T(1,128)S(1)} %bitcast.15), channel_id=1, replica_groups={{71,70,69,68,67,66,65,64,63,62,61,60,59,58,57,56,79,78,77,76,75,74,73,7..., dimensions={0} | all-to-all | bytes 393216 | tf_op jit(solution)/shard_map/all_to_all | solution.py:333
  33.7 5.1 %others.1 = (bf16[32,4224]{1,0:T(8,128)(2,1)}, f32[16,128]{1,0:T(8,128)S(1)}, f32[192,128]{1,0:T(8,128)S(1)}, f32[192,128]{1,0:T(8,128)S(1)}, f32[192,128]{1,0:T(8,128)S(1)}) custom-call(f32[384,128]{1,0:T(8,128)S(1)} %bitcast.14), custom_call_target="tpu_custom_call" | custom-call | tf_op jit(solution)/shard_map/others/pallas_call | solution.py:342
  38.8 6.2 %all-to-all-start.1 = ((bf16[4,8,4224]{2,1,0:T(8,128)(2,1)}), bf16[4,8,4224]{2,1,0:T(8,128)(2,1)S(1)}, u32[]{:S(2)}, u32[]{:S(2)}) async-start(bf16[4,8,4224]{2,1,0:T(8,128)(2,1)} %bitcast.8), calls=%async_computation.1 | async-start | bytes 540672 | tf_op jit(solution)/shard_map/all_to_all | solution.py:358
  44.9 0.0 copy-start
  44.9 0.7 %copy-done = f32[9,9]{1,0:T(8,128)S(1)} copy-done((f32[9,9]{1,0:T(8,128)S(1)}, f32[9,9]{1,0:T(8,128)}, u32[]{:S(2)}) %copy-start) | copy-done | bytes 348
  45.6 0.7 %band.1 = (f32[72,144]{1,0:T(8,128)S(1)}, f32[8,128]{1,0:T(8,128)S(1)}) custom-call(s32[1]{0:T(128)} %bitcast.parity_ref, f32[9,9]{1,0:T(8,128)S(1)} %copy-done), custom_call_target="tpu_custom_call" | custom-call | tf_op jit(solution)/shard_map/band/pallas_call | solution.py:375
  46.4 2.5 %own.1.own_ref = bf16[8,4224]{1,0:T(8,128)(2,1)S(1)} custom-call(f32[192,128]{1,0:T(8,128)S(1)} %get-tuple-element.20.first_ref, f32[192,128]{1,0:T(8,128)S(1)} %get-tuple-element.21.second_ref, f32[192,128]{1,0:T(8,128)S(1)} %get-tuple-element.22.mass_ref, f32[16,128]{1,0:T(8,128)S(1)} %get-tuple-element.23.side_ref), custom_call_target="tpu_custom_call" | custom-call | flops 1610612736 | bytes 524288 | tf_op jit(solution)/shard_map/own/pallas_call | solution.py:361
  48.9 0.0 all-to-all-done.1
  48.9 0.1 near.1
  49.0 0.1 far.1
  49.1 4.4 %collective-permute-start.1 = (bf16[4,4224]{1,0:T(4,128)(2,1)S(1)}, bf16[4,4224]{1,0:T(4,128)(2,1)S(1)}, u32[]{:S(2)}, u32[]{:S(2)}) collective-permute-start(bf16[4,4224]{1,0:T(4,128)(2,1)S(1)} %far.1), channel_id=1, source_target_pairs={{1,2},{3,4},{5,6},{7,8},{9,10},{11,12},{13,14},{15,16},{17,18},{19... | collective-permute-start | bytes 101384 | tf_op jit(solution)/shard_map/ppermute | solution.py:402
  53.5 1.9 %collective-permute-start = (bf16[4,4224]{1,0:T(4,128)(2,1)S(1)}, bf16[4,4224]{1,0:T(4,128)(2,1)S(1)}, u32[]{:S(2)}, u32[]{:S(2)}) collective-permute-start(bf16[4,4224]{1,0:T(4,128)(2,1)S(1)} %near.1), channel_id=1, source_target_pairs={{0,1},{1,0},{2,3},{3,2},{4,5},{5,4},{6,7},{7,6},{8,9},{9,8},{10,11... | collective-permute-start | bytes 101384 | tf_op jit(solution)/shard_map/ppermute | solution.py:403
  55.4 1.0 %collective-permute-done.1.far_ref = bf16[4,4224]{1,0:T(4,128)(2,1)S(1)} collective-permute-done((bf16[4,4224]{1,0:T(4,128)(2,1)S(1)}, bf16[4,4224]{1,0:T(4,128)(2,1)S(1)}, u32[]{:S(2)}, u32[]{:S(2)}) %collective-permute-start.1) | collective-permute-done | bytes 33824 | tf_op jit(solution)/shard_map/ppermute | solution.py:402
  56.4 0.2 collective-permute-done.near_ref
  56.6 1.2 %smooth.1 = f32[8,4096]{1,0:T(8,128)} custom-call(f32[72,144]{1,0:T(8,128)S(1)} %get-tuple-element.18.band_ref, bf16[32,4224]{1,0:T(8,128)(2,1)S(1)} %bitcast.13, bf16[8,4224]{1,0:T(8,128)(2,1)S(1)} %own.1.own_ref, bf16[4,4224]{1,0:T(4,128)(2,1)S(1)} %collective-permute-done.near_ref, bf16[4,4224]{1,0:T(4,128)(2,1)S(1)} %collective-permute-done.1.far_ref), custom_call_target="tpu_custom_call" | custom-call | tf_op jit(solution)/shard_map/smooth/pallas_call | solution.py:404
Async XLA Ops:
  38.8 10.1 %all-to-all-start.1 = ((bf16[4,8,4224]{2,1,0:T(8,128)(2,1)}), bf16[4,8,4224]{2,1,0:T(8,128)(2,1)S(1)}, u32[]{:S(2)}, u32[]{:S(2)}) async-start(bf16[4,8,4224]{2,1,0:T(8,128)(2,1)} %bitcast.8), calls=%async_computation.1 | async-start | bytes 540672 | tf_op jit(solution)/shard_map/all_to_all | solution.py:358
  44.9 0.7 %copy-start = (f32[9,9]{1,0:T(8,128)S(1)}, f32[9,9]{1,0:T(8,128)}, u32[]{:S(2)}) copy-start(f32[9,9]{1,0:T(8,128)} %kernel_ref) | copy-start | bytes 976
  49.1 7.4 %collective-permute-start.1 = (bf16[4,4224]{1,0:T(4,128)(2,1)S(1)}, bf16[4,4224]{1,0:T(4,128)(2,1)S(1)}, u32[]{:S(2)}, u32[]{:S(2)}) collective-permute-start(bf16[4,4224]{1,0:T(4,128)(2,1)S(1)} %far.1), channel_id=1, source_target_pairs={{1,2},{3,4},{5,6},{7,8},{9,10},{11,12},{13,14},{15,16},{17,18},{19... | collective-permute-start | bytes 101384 | tf_op jit(solution)/shard_map/ppermute | solution.py:402
  53.5 3.1 %collective-permute-start = (bf16[4,4224]{1,0:T(4,128)(2,1)S(1)}, bf16[4,4224]{1,0:T(4,128)(2,1)S(1)}, u32[]{:S(2)}, u32[]{:S(2)}) collective-permute-start(bf16[4,4224]{1,0:T(4,128)(2,1)S(1)} %near.1), channel_id=1, source_target_pairs={{0,1},{1,0},{2,3},{3,2},{4,5},{5,4},{6,7},{7,6},{8,9},{9,8},{10,11... | collective-permute-start | bytes 101384 | tf_op jit(solution)/shard_map/ppermute | solution.py:403

commit v11 on v10

--- a/solution.py
+++ b/solution.py
@@ -24,10 +24,6 @@
 
 def vmem_spec():
     return pl.BlockSpec(memory_space=pltpu.VMEM)
-
-
-def smem_spec():
-    return pl.BlockSpec(memory_space=pltpu.SMEM)
 
 
 def limit(mebibytes):
@@ -227,24 +223,7 @@
     side_ref[STRIP:, :] = jnp.where(here == quarters - 1, blank, acc_ref[STRIP : 2 * STRIP, :LANES])
 
 
-def own_kernel(first_ref, second_ref, mass_ref, side_ref, out_ref, moved_ref, acc_ref):
-    moved = first_ref[...] + float(out_ref.shape[1] // SPAN * STRIP - STRIP)
-    moved_ref[...] = jnp.where(moved < CELLS // 2, moved, moved - CELLS)
-    cells = acc_ref.shape[0]
-    acc_ref[...] = one_hot_sum(cells, moved_ref, second_ref, mass_ref, 0, ROWS)
-    rest = first_ref.shape[0] - ROWS
-
-    @pl.when(jnp.max(jnp.abs(mass_ref[ROWS:, :])) > 0.0)
-    def _():
-        acc_ref[...] += one_hot_sum(cells, moved_ref, second_ref, mass_ref, ROWS, rest)
-
-    before = side_ref[:STRIP, :]
-    after = side_ref[STRIP:, :]
-    store_strip(out_ref, pl.ds(0, STRIP), acc_ref, 0, before, after)
-
-
-def band_kernel(parity_ref, kernel_ref, band_ref, odd_ref):
-    parity = parity_ref[0]
+def store_band(parity, kernel_ref, band_ref):
     row = lax.broadcasted_iota(jnp.int32, (STRIP, 3 * TERM), 0)
     lane = lax.broadcasted_iota(jnp.int32, (STRIP, 3 * TERM), 1)
     source = lane % TERM
@@ -267,7 +246,30 @@
         middle = rest.astype(jnp.bfloat16).astype(jnp.float32)
         term = jnp.where(lane < TERM, high, jnp.where(lane < 2 * TERM, middle, rest - middle))
         band_ref[pl.ds(b * STRIP, STRIP), :] = term
+
+
+def own_kernel(
+    first_ref, second_ref, mass_ref, side_ref, kernel_in, out_ref, band_ref, odd_ref, moved_ref, acc_ref, kernel_ref, sem
+):
+    copy = pltpu.make_async_copy(kernel_in, kernel_ref, sem)
+    copy.start()
+    moved = first_ref[...] + float(out_ref.shape[1] // SPAN * STRIP - STRIP)
+    moved_ref[...] = jnp.where(moved < CELLS // 2, moved, moved - CELLS)
+    cells = acc_ref.shape[0]
+    acc_ref[...] = one_hot_sum(cells, moved_ref, second_ref, mass_ref, 0, ROWS)
+    rest = first_ref.shape[0] - ROWS
+
+    @pl.when(jnp.max(jnp.abs(mass_ref[ROWS:, :])) > 0.0)
+    def _():
+        acc_ref[...] += one_hot_sum(cells, moved_ref, second_ref, mass_ref, ROWS, rest)
+
+    before = side_ref[:STRIP, :]
+    after = side_ref[STRIP:, :]
+    store_strip(out_ref, pl.ds(0, STRIP), acc_ref, 0, before, after)
+    parity = lax.axis_index("own") & 1
     odd_ref[...] = jnp.broadcast_to(parity.astype(jnp.float32), odd_ref.shape)
+    copy.wait()
+    store_band(parity, kernel_ref, band_ref)
 
 
 def edge_kernel(odd_ref, parts_ref, own_ref, edge_ref, *, top_if_odd):
@@ -354,35 +356,31 @@
         compiler_params=limit(32),
         name="others",
     )(arrived)
-    sent, kernel = lax.optimization_barrier((sent, kernel))
     parts = lax.all_to_all(
         sent, "grp", split_axis=0, concat_axis=0, tiled=True, axis_index_groups=[ring_order(groups)]
     )
-    own = pl.pallas_call(
+    own, band, odd = pl.pallas_call(
         own_kernel,
-        out_shape=jax.ShapeDtypeStruct((STRIP, width), jnp.bfloat16),
-        in_specs=[vmem_spec()] * 4,
-        out_specs=vmem_spec(),
+        out_shape=(
+            jax.ShapeDtypeStruct((STRIP, width), jnp.bfloat16),
+            jax.ShapeDtypeStruct((TAPS * STRIP, 3 * TERM), jnp.float32),
+            jax.ShapeDtypeStruct((STRIP, LANES), jnp.float32),
+        ),
+        in_specs=[vmem_spec()] * 4 + [pl.BlockSpec(memory_space=pltpu.HBM)],
+        out_specs=(vmem_spec(),) * 3,
         scratch_shapes=[
             pltpu.VMEM((points, LANES), jnp.float32),
             pltpu.VMEM((max(CELLS // groups, 256), SPAN), jnp.float32),
+            pltpu.SMEM(kernel.shape, jnp.float32),
+            pltpu.SemaphoreType.DMA,
         ],
         compiler_params=limit(32),
-        cost_estimate=pl.CostEstimate(flops=2 * points * LANES * W * STRIP // groups, bytes_accessed=2**19, transcendentals=0),
+        cost_estimate=pl.CostEstimate(
+            flops=2 * points * LANES * W * STRIP // groups, bytes_accessed=2**19, transcendentals=0
+        ),
         name="own",
-    )(first, second, mass, side)
-    parity = (lax.axis_index("own") & 1).reshape(1).astype(jnp.int32)
-    band, odd = pl.pallas_call(
-        band_kernel,
-        out_shape=(
-            jax.ShapeDtypeStruct((TAPS * STRIP, 3 * TERM), jnp.float32),
-            jax.ShapeDtypeStruct((STRIP, LANES), jnp.float32),
-        ),
-        in_specs=[smem_spec(), smem_spec()],
-        out_specs=(vmem_spec(),) * 2,
-        compiler_params=limit(4),
-        name="band",
-    )(parity, kernel)
+    )(first, second, mass, side, pltpu.with_memory_space_constraint(kernel, pltpu.HBM))
+
     def edge(parts, top_if_odd, name):
         return pl.pallas_call(
             functools.partial(edge_kernel, top_if_odd=top_if_odd),

time: 58.8 us -> 58.7 us (level)
  waiting for transfers between devices: 1.19 us -> 2.76 us
  Pallas kernels: 10.9 us -> 10.2 us
  local copies, waits for them, and re-layouts: 0.7 us -> 0 us
    all_to_all x1, waiting for transfers between devices: 0.01 us -> 1.37 us  [per_device(): lax.all_to_all(sent, 'grp', split_axis=0, concat_axis=0, tiled=True, axis...]
    unnamed x2 -> x0, local copies, waits for them, and re-layouts: 0.7 us -> none
    pallas_call x2 -> x1, Pallas kernels: 3.25 us -> 2.6 us  [per_device(): pl.pallas_call(own_kernel, out_shape=(jax.ShapeDtypeStruct((STRIP, width)...]
  transfers between devices with their start and end apart: 3 -> 3, of which waited for: 2 -> 2; matrix products, arithmetic and copies ran while one was open for 0% -> 0% of each run, Pallas kernels for 6% -> 5%
where the time goes in v11:
time: 58.7 us; the launch traced here: 57.6 us
  blocking collectives  32.4 us (55%)
  starting transfers between devices  12.1 us (21%)
  Pallas kernels  10.2 us (17%)
  waiting for transfers between devices  2.76 us (5%)
    all_to_all x1, blocking collectives, per_device(): lax.all_to_all(packed.reshape(3 * owners, 1, LANES), 'own', split_axis=0,...  32.4 us
    all_to_all x1, starting transfers between devices, per_device(): lax.all_to_all(sent, 'grp', split_axis=0, concat_axis=0, tiled=True, axis...  6.16 us
    pallas_call x1, Pallas kernels, per_device(): pl.pallas_call(others_kernel, out_shape=(jax.ShapeDtypeStruct((groups * S...  5.06 us
    ppermute x1, starting transfers between devices, per_device(): far = lax.ppermute(far, 'own', across)  4.02 us
    pallas_call x1, Pallas kernels, per_device(): pl.pallas_call(own_kernel, out_shape=(jax.ShapeDtypeStruct((STRIP, width)...  2.6 us
    ppermute x1, starting transfers between devices, per_device(): near = lax.ppermute(near, 'own', on_chip)  1.92 us
    ppermute x1, waiting for transfers between devices, per_device(): far = lax.ppermute(far, 'own', across)  1.4 us
    all_to_all x1, waiting for transfers between devices, per_device(): lax.all_to_all(sent, 'grp', split_axis=0, concat_axis=0, tiled=True, axis...  1.37 us
  transfers between devices with their start and end apart: 3, of which 2 were waited for; matrix products, arithmetic and copies ran while one was open for 0% of the time, Pallas kernels for 5%

profile of v11, /device:TPU:25, one launch (start us, length us, event | category | flops | bytes accessed | tf_op | source)
XLA Modules:
  0.0 57.6 jit_solution(11398868275004294560)
XLA Ops:
  0.0 1.3 %pack.1 = f32[384,128]{1,0:T(8,128)S(1)} custom-call(s32[192,128]{1,0:T(8,128)} %bitcast.15, s32[192,128]{1,0:T(8,128)} %bitcast.16, bf16[192,1,128]{2,1,0:T(2,128)(2,1)} %bitcast.17, s32[1,128]{1,0:T(1,128)} %bitcast.18), custom_call_target="tpu_custom_call" | custom-call | tf_op jit(solution)/shard_map/pack/pallas_call | solution.py:307
  1.3 32.4 %all_to_all.16 = f32[384,1,128]{2,1,0:T(1,128)S(1)} all-to-all(f32[384,1,128]{2,1,0:T(1,128)S(1)} %bitcast.14), channel_id=1, replica_groups={{71,70,69,68,67,66,65,64,63,62,61,60,59,58,57,56,79,78,77,76,75,74,73,7..., dimensions={0} | all-to-all | bytes 393216 | tf_op jit(solution)/shard_map/all_to_all | solution.py:335
  33.7 5.1 %others.1 = (bf16[32,4224]{1,0:T(8,128)(2,1)}, f32[16,128]{1,0:T(8,128)S(1)}, f32[192,128]{1,0:T(8,128)S(1)}, f32[192,128]{1,0:T(8,128)S(1)}, f32[192,128]{1,0:T(8,128)S(1)}) custom-call(f32[384,128]{1,0:T(8,128)S(1)} %bitcast.13), custom_call_target="tpu_custom_call" | custom-call | tf_op jit(solution)/shard_map/others/pallas_call | solution.py:344
  38.8 6.2 %all-to-all-start.1 = ((bf16[4,8,4224]{2,1,0:T(8,128)(2,1)}), bf16[4,8,4224]{2,1,0:T(8,128)(2,1)S(1)}, u32[]{:S(2)}, u32[]{:S(2)}) async-start(bf16[4,8,4224]{2,1,0:T(8,128)(2,1)} %bitcast.7), calls=%async_computation.1 | async-start | bytes 540672 | tf_op jit(solution)/shard_map/all_to_all | solution.py:359
  44.9 2.6 %own.1 = (bf16[8,4224]{1,0:T(8,128)(2,1)S(1)}, f32[72,144]{1,0:T(8,128)S(1)}, f32[8,128]{1,0:T(8,128)S(1)}) custom-call(f32[192,128]{1,0:T(8,128)S(1)} %get-tuple-element.15.first_ref, f32[192,128]{1,0:T(8,128)S(1)} %get-tuple-element.16.second_ref, f32[192,128]{1,0:T(8,128)S(1)} %get-tuple-element.17.mass_ref, f32[16,128]{1,0:T(8,128)S(1)} %get-tuple-element.18.side_ref, ...), custom_call_target="tpu_custom_call" | custom-call | flops 1610612736 | bytes 524288 | tf_op jit(solution)/shard_map/own/pallas_call | solution.py:362
  47.5 1.4 %all-to-all-done.1 = bf16[4,8,4224]{2,1,0:T(8,128)(2,1)S(1)} async-done(((bf16[4,8,4224]{2,1,0:T(8,128)(2,1)}), bf16[4,8,4224]{2,1,0:T(8,128)(2,1)S(1)}, u32[]{:S(2)}, u32[]{:S(2)}) %all-to-all-start.1) | async-done | bytes 270368 | tf_op jit(solution)/shard_map/all_to_all | solution.py:359
  48.9 0.1 near.1
  49.0 0.1 far.1
  49.0 4.0 %collective-permute-start.1 = (bf16[4,4224]{1,0:T(4,128)(2,1)S(1)}, bf16[4,4224]{1,0:T(4,128)(2,1)S(1)}, u32[]{:S(2)}, u32[]{:S(2)}) collective-permute-start(bf16[4,4224]{1,0:T(4,128)(2,1)S(1)} %far.1), channel_id=1, source_target_pairs={{1,2},{3,4},{5,6},{7,8},{9,10},{11,12},{13,14},{15,16},{17,18},{19... | collective-permute-start | bytes 101384 | tf_op jit(solution)/shard_map/ppermute | solution.py:400
  53.1 1.9 %collective-permute-start = (bf16[4,4224]{1,0:T(4,128)(2,1)S(1)}, bf16[4,4224]{1,0:T(4,128)(2,1)S(1)}, u32[]{:S(2)}, u32[]{:S(2)}) collective-permute-start(bf16[4,4224]{1,0:T(4,128)(2,1)S(1)} %near.1), channel_id=1, source_target_pairs={{0,1},{1,0},{2,3},{3,2},{4,5},{5,4},{6,7},{7,6},{8,9},{9,8},{10,11... | collective-permute-start | bytes 101384 | tf_op jit(solution)/shard_map/ppermute | solution.py:401
  55.0 1.4 %collective-permute-done.1.far_ref = bf16[4,4224]{1,0:T(4,128)(2,1)S(1)} collective-permute-done((bf16[4,4224]{1,0:T(4,128)(2,1)S(1)}, bf16[4,4224]{1,0:T(4,128)(2,1)S(1)}, u32[]{:S(2)}, u32[]{:S(2)}) %collective-permute-start.1) | collective-permute-done | bytes 33824 | tf_op jit(solution)/shard_map/ppermute | solution.py:400
  56.4 0.0 collective-permute-done.near_ref
  56.4 1.2 %smooth.1 = f32[8,4096]{1,0:T(8,128)} custom-call(f32[72,144]{1,0:T(8,128)S(1)} %get-tuple-element.19.band_ref, bf16[32,4224]{1,0:T(8,128)(2,1)S(1)} %bitcast.12, bf16[8,4224]{1,0:T(8,128)(2,1)S(1)} %get-tuple-element.21.own_ref, bf16[4,4224]{1,0:T(4,128)(2,1)S(1)} %collective-permute-done.near_ref, bf16[4,4224]{1,0:T(4,128)(2,1)S(1)} %collective-permute-done.1.far_ref), custom_call_target="tpu_custom_call" | custom-call | tf_op jit(solution)/shard_map/smooth/pallas_call | solution.py:402
Async XLA Ops:
  38.8 10.1 %all-to-all-start.1 = ((bf16[4,8,4224]{2,1,0:T(8,128)(2,1)}), bf16[4,8,4224]{2,1,0:T(8,128)(2,1)S(1)}, u32[]{:S(2)}, u32[]{:S(2)}) async-start(bf16[4,8,4224]{2,1,0:T(8,128)(2,1)} %bitcast.7), calls=%async_computation.1 | async-start | bytes 540672 | tf_op jit(solution)/shard_map/all_to_all | solution.py:359
  49.0 7.4 %collective-permute-start.1 = (bf16[4,4224]{1,0:T(4,128)(2,1)S(1)}, bf16[4,4224]{1,0:T(4,128)(2,1)S(1)}, u32[]{:S(2)}, u32[]{:S(2)}) collective-permute-start(bf16[4,4224]{1,0:T(4,128)(2,1)S(1)} %far.1), channel_id=1, source_target_pairs={{1,2},{3,4},{5,6},{7,8},{9,10},{11,12},{13,14},{15,16},{17,18},{19... | collective-permute-start | bytes 101384 | tf_op jit(solution)/shard_map/ppermute | solution.py:400
  53.1 3.3 %collective-permute-start = (bf16[4,4224]{1,0:T(4,128)(2,1)S(1)}, bf16[4,4224]{1,0:T(4,128)(2,1)S(1)}, u32[]{:S(2)}, u32[]{:S(2)}) collective-permute-start(bf16[4,4224]{1,0:T(4,128)(2,1)S(1)} %near.1), channel_id=1, source_target_pairs={{0,1},{1,0},{2,3},{3,2},{4,5},{5,4},{6,7},{7,6},{8,9},{9,8},{10,11... | collective-permute-start | bytes 101384 | tf_op jit(solution)/shard_map/ppermute | solution.py:401

commit v12 on v11

--- a/solution.py
+++ b/solution.py
@@ -13,6 +13,8 @@
 LANES = 128
 HALO = 4
 PLANE = 8
+PLANES = (8, 9, 7, 10, 6, 11, 5, 12, 13, 14, 2, 15, 1, 3, 4, 0)
+GROUPS = (2, 3, 1, 0)
 TAPS = 2 * HALO + 1
 PARTS = 40
 TERM = 48
@@ -28,14 +30,6 @@
 
 def limit(mebibytes):
     return pltpu.CompilerParams(vmem_limit_bytes=mebibytes * 2**20)
-
-
-def ring_order(length):
-    half = length // 2
-    order = []
-    for step in range(half):
-        order += [half + step, half - 1 - step]
-    return order
 
 
 def pack_kernel(
@@ -90,7 +84,7 @@
                 at = 3 * (PLANE - 1 - block) + r
                 sorted_ref[pl.ds(at, planes, stride=3 * PLANE), :] = value
     size = 3 * PLANE
-    for place, z in enumerate(ring_order(planes)):
+    for place, z in enumerate(PLANES):
         out_ref[pl.ds(place * size, size), :] = sorted_ref[pl.ds(z * size, size), :]
 
 
@@ -165,7 +159,7 @@
     origin = (here + 1) * share - STRIP
 
     def place_of(quarter):
-        return sum(jnp.where(quarter == q, place, 0) for place, q in enumerate(ring_order(quarters)))
+        return sum(jnp.where(quarter == q, place, 0) for place, q in enumerate(GROUPS))
 
     def split(ids):
         ids = ids.astype(jnp.int32)
@@ -331,7 +325,7 @@
             )
         )
     )
-    order = [z * PLANE + k for z in ring_order(owners // PLANE) for k in reversed(range(PLANE))]
+    order = [z * PLANE + k for z in PLANES for k in reversed(range(PLANE))]
     arrived = lax.all_to_all(
         packed.reshape(3 * owners, 1, LANES),
         "own",
@@ -357,7 +351,7 @@
         name="others",
     )(arrived)
     parts = lax.all_to_all(
-        sent, "grp", split_axis=0, concat_axis=0, tiled=True, axis_index_groups=[ring_order(groups)]
+        sent, "grp", split_axis=0, concat_axis=0, tiled=True, axis_index_groups=[list(GROUPS)]
     )
     own, band, odd = pl.pallas_call(
         own_kernel,

time: 58.7 us -> 58.5 us (level)
  starting transfers between devices: 12.1 us -> 13.5 us
  waiting for transfers between devices: 2.76 us -> 1.67 us
    ppermute x1, starting transfers between devices: 4.02 us -> 5.45 us  [per_device(): far = lax.ppermute(far, 'own', across)]
    ppermute x1, waiting for transfers between devices: 1.4 us -> 0.01 us  [per_device(): far = lax.ppermute(far, 'own', across)]
    ppermute x1, waiting for transfers between devices: 0.01 us -> 1.16 us  [per_device(): near = lax.ppermute(near, 'own', on_chip)]
    all_to_all x1, waiting for transfers between devices: 1.37 us -> 0.5 us  [per_device(): lax.all_to_all(sent, 'grp', split_axis=0, concat_axis=0, tiled=True, axis...]
where the time goes in v12:
time: 58.5 us; the launch traced here: 57.7 us
  blocking collectives  32.2 us (55%)
  starting transfers between devices  13.5 us (23%)
  Pallas kernels  10.2 us (17%)
  waiting for transfers between devices  1.67 us (3%)
    all_to_all x1, blocking collectives, per_device(): lax.all_to_all(packed.reshape(3 * owners, 1, LANES), 'own', split_axis=0,...  32.2 us
    all_to_all x1, starting transfers between devices, per_device(): lax.all_to_all(sent, 'grp', split_axis=0, concat_axis=0, tiled=True, axis...  6.16 us
    ppermute x1, starting transfers between devices, per_device(): far = lax.ppermute(far, 'own', across)  5.45 us
    pallas_call x1, Pallas kernels, per_device(): pl.pallas_call(others_kernel, out_shape=(jax.ShapeDtypeStruct((groups * S...  5.06 us
    pallas_call x1, Pallas kernels, per_device(): pl.pallas_call(own_kernel, out_shape=(jax.ShapeDtypeStruct((STRIP, width)...  2.6 us
    ppermute x1, starting transfers between devices, per_device(): near = lax.ppermute(near, 'own', on_chip)  1.92 us
    pallas_call x1, Pallas kernels, per_device(): pl.pallas_call(pack_kernel, out_shape=jax.ShapeDtypeStruct((3 * owners, L...  1.27 us
    pallas_call x1, Pallas kernels, per_device(): pl.pallas_call(smooth_kernel, out_shape=jax.ShapeDtypeStruct((STRIP, quar...  1.18 us
  transfers between devices with their start and end apart: 3, of which 2 were waited for; matrix products, arithmetic and copies ran while one was open for 0% of the time, Pallas kernels for 5%

profile of v12, /device:TPU:25, one launch (start us, length us, event | category | flops | bytes accessed | tf_op | source)
XLA Modules:
  0.0 57.7 jit_solution(8509994626371618572)
XLA Ops:
  0.0 1.3 %pack.1 = f32[384,128]{1,0:T(8,128)S(1)} custom-call(s32[192,128]{1,0:T(8,128)} %bitcast.15, s32[192,128]{1,0:T(8,128)} %bitcast.16, bf16[192,1,128]{2,1,0:T(2,128)(2,1)} %bitcast.17, s32[1,128]{1,0:T(1,128)} %bitcast.18), custom_call_target="tpu_custom_call" | custom-call | tf_op jit(solution)/shard_map/pack/pallas_call | solution.py:301
  1.3 32.2 %all_to_all.16 = f32[384,1,128]{2,1,0:T(1,128)S(1)} all-to-all(f32[384,1,128]{2,1,0:T(1,128)S(1)} %bitcast.14), channel_id=1, replica_groups={{71,70,69,68,67,66,65,64,79,78,77,76,75,74,73,72,63,62,61,60,59,58,57,5..., dimensions={0} | all-to-all | bytes 393216 | tf_op jit(solution)/shard_map/all_to_all | solution.py:329
  33.5 5.1 %others.1 = (bf16[32,4224]{1,0:T(8,128)(2,1)}, f32[16,128]{1,0:T(8,128)S(1)}, f32[192,128]{1,0:T(8,128)S(1)}, f32[192,128]{1,0:T(8,128)S(1)}, f32[192,128]{1,0:T(8,128)S(1)}) custom-call(f32[384,128]{1,0:T(8,128)S(1)} %bitcast.13), custom_call_target="tpu_custom_call" | custom-call | tf_op jit(solution)/shard_map/others/pallas_call | solution.py:338
  38.5 6.2 %all-to-all-start.1 = ((bf16[4,8,4224]{2,1,0:T(8,128)(2,1)}), bf16[4,8,4224]{2,1,0:T(8,128)(2,1)S(1)}, u32[]{:S(2)}, u32[]{:S(2)}) async-start(bf16[4,8,4224]{2,1,0:T(8,128)(2,1)} %bitcast.7), calls=%async_computation.1 | async-start | bytes 540672 | tf_op jit(solution)/shard_map/all_to_all | solution.py:353
  44.7 2.6 %own.1 = (bf16[8,4224]{1,0:T(8,128)(2,1)S(1)}, f32[72,144]{1,0:T(8,128)S(1)}, f32[8,128]{1,0:T(8,128)S(1)}) custom-call(f32[192,128]{1,0:T(8,128)S(1)} %get-tuple-element.15.first_ref, f32[192,128]{1,0:T(8,128)S(1)} %get-tuple-element.16.second_ref, f32[192,128]{1,0:T(8,128)S(1)} %get-tuple-element.17.mass_ref, f32[16,128]{1,0:T(8,128)S(1)} %get-tuple-element.18.side_ref, ...), custom_call_target="tpu_custom_call" | custom-call | flops 1610612736 | bytes 524288 | tf_op jit(solution)/shard_map/own/pallas_call | solution.py:356
  47.3 0.5 all-to-all-done.1
  47.8 0.1 near.1
  47.9 0.1 far.1
  47.9 5.5 %collective-permute-start.1 = (bf16[4,4224]{1,0:T(4,128)(2,1)S(1)}, bf16[4,4224]{1,0:T(4,128)(2,1)S(1)}, u32[]{:S(2)}, u32[]{:S(2)}) collective-permute-start(bf16[4,4224]{1,0:T(4,128)(2,1)S(1)} %far.1), channel_id=1, source_target_pairs={{1,2},{3,4},{5,6},{7,8},{9,10},{11,12},{13,14},{15,16},{17,18},{19... | collective-permute-start | bytes 101384 | tf_op jit(solution)/shard_map/ppermute | solution.py:394
  53.4 1.9 %collective-permute-start = (bf16[4,4224]{1,0:T(4,128)(2,1)S(1)}, bf16[4,4224]{1,0:T(4,128)(2,1)S(1)}, u32[]{:S(2)}, u32[]{:S(2)}) collective-permute-start(bf16[4,4224]{1,0:T(4,128)(2,1)S(1)} %near.1), channel_id=1, source_target_pairs={{0,1},{1,0},{2,3},{3,2},{4,5},{5,4},{6,7},{7,6},{8,9},{9,8},{10,11... | collective-permute-start | bytes 101384 | tf_op jit(solution)/shard_map/ppermute | solution.py:395
  55.3 0.0 collective-permute-done.1.far_ref
  55.3 1.2 %collective-permute-done.near_ref = bf16[4,4224]{1,0:T(4,128)(2,1)S(1)} collective-permute-done((bf16[4,4224]{1,0:T(4,128)(2,1)S(1)}, bf16[4,4224]{1,0:T(4,128)(2,1)S(1)}, u32[]{:S(2)}, u32[]{:S(2)}) %collective-permute-start) | collective-permute-done | bytes 33824 | tf_op jit(solution)/shard_map/ppermute | solution.py:395
  56.5 1.2 %smooth.1 = f32[8,4096]{1,0:T(8,128)} custom-call(f32[72,144]{1,0:T(8,128)S(1)} %get-tuple-element.19.band_ref, bf16[32,4224]{1,0:T(8,128)(2,1)S(1)} %bitcast.12, bf16[8,4224]{1,0:T(8,128)(2,1)S(1)} %get-tuple-element.21.own_ref, bf16[4,4224]{1,0:T(4,128)(2,1)S(1)} %collective-permute-done.near_ref, bf16[4,4224]{1,0:T(4,128)(2,1)S(1)} %collective-permute-done.1.far_ref), custom_call_target="tpu_custom_call" | custom-call | tf_op jit(solution)/shard_map/smooth/pallas_call | solution.py:396
Async XLA Ops:
  38.5 9.3 %all-to-all-start.1 = ((bf16[4,8,4224]{2,1,0:T(8,128)(2,1)}), bf16[4,8,4224]{2,1,0:T(8,128)(2,1)S(1)}, u32[]{:S(2)}, u32[]{:S(2)}) async-start(bf16[4,8,4224]{2,1,0:T(8,128)(2,1)} %bitcast.7), calls=%async_computation.1 | async-start | bytes 540672 | tf_op jit(solution)/shard_map/all_to_all | solution.py:353
  47.9 7.4 %collective-permute-start.1 = (bf16[4,4224]{1,0:T(4,128)(2,1)S(1)}, bf16[4,4224]{1,0:T(4,128)(2,1)S(1)}, u32[]{:S(2)}, u32[]{:S(2)}) collective-permute-start(bf16[4,4224]{1,0:T(4,128)(2,1)S(1)} %far.1), channel_id=1, source_target_pairs={{1,2},{3,4},{5,6},{7,8},{9,10},{11,12},{13,14},{15,16},{17,18},{19... | collective-permute-start | bytes 101384 | tf_op jit(solution)/shard_map/ppermute | solution.py:394
  53.4 3.1 %collective-permute-start = (bf16[4,4224]{1,0:T(4,128)(2,1)S(1)}, bf16[4,4224]{1,0:T(4,128)(2,1)S(1)}, u32[]{:S(2)}, u32[]{:S(2)}) collective-permute-start(bf16[4,4224]{1,0:T(4,128)(2,1)S(1)} %near.1), channel_id=1, source_target_pairs={{0,1},{1,0},{2,3},{3,2},{4,5},{5,4},{6,7},{7,6},{8,9},{9,8},{10,11... | collective-permute-start | bytes 101384 | tf_op jit(solution)/shard_map/ppermute | solution.py:395
